TPU v7x, 512 devices: a whole 4x4x16 slice. The times are simulated.
512 devices in a mesh: index: 64 (over z, y), query: 8 (over x, core).
Axes of the slice: x: 4, y: 4, z: 16, core: 2. Of those that a mesh axis runs over, the one named last changes fastest.
Arguments:
- queries: bfloat16 [256, 32, 128], P('query'), may hold values from -6 to 6
- passages: bfloat16 [32768, 128, 128], P(('index', 'query')), may hold values from -0.5 to 0.5
- lengths: int32 [32768], P(('index', 'query')), may hold values from 1 to 128
- candidates: int32 [256, 1024], P('query', 'index'), may hold values from 0 to 32767, as said below
Outputs:
- scores: float32 [256, 1024], P('query', 'index')
Inputs may be any that keep to these rules, and one draw needn't show every extreme that they name: Block b is stored on the device of flat position b // 64 along index+query. The 32 x 16 candidates held by one device name blocks of any one storing device at most 2 times, and exactly 2 times for some storing device.
All inputs are finite; a program needn't handle non-finite values.
Results may differ from a plain program's by a relative error of at most 0.0003.
Values may be sent and summed in bfloat16 or wider, within the bound.
No kernel may reach another device: no remote copies, remote signals or barrier semaphores. Data moves between devices by JAX's collectives and lax.ppermute only.
A program may use at most 64 MiB of HBM per device.

v0:
```python
import math

import jax
import jax.numpy as jnp
from jax import lax
from jax.sharding import PartitionSpec as P


def score_slots(slot_rows, slot_blocks, passages, lengths):
    slot_total = slot_blocks.shape[0]
    group = math.gcd(slot_total, 128)
    token_count = passages.shape[1]

    def score_group(packed):
        query_rows, block_ids = packed
        safe_ids = jnp.maximum(block_ids, 0)
        block_rows = passages[safe_ids]
        similar = jnp.einsum(
            "gtd,gpd->gtp", query_rows, block_rows, preferred_element_type=jnp.float32
        )
        token_pos = lax.broadcasted_iota(jnp.int32, (1, 1, token_count), 2)
        live = token_pos < lengths[safe_ids][:, None, None]
        best = jnp.max(jnp.where(live, similar, -jnp.inf), axis=2)
        return jnp.where(block_ids >= 0, jnp.mean(best, axis=1), jnp.float32(0.0))

    grouped_rows = slot_rows.reshape((slot_total // group, group) + slot_rows.shape[1:])
    grouped_ids = slot_blocks.reshape(slot_total // group, group)
    results = lax.map(score_group, (grouped_rows, grouped_ids))
    return results.reshape(slot_total)


def shards(queries, passages, lengths, candidates):
    n_index = lax.axis_size("index")
    n_query = lax.axis_size("query")
    devices = n_index * n_query
    q_local, cand_local = candidates.shape
    blk_local = passages.shape[0]
    request_count = q_local * cand_local
    capacity = max(2, 2 * request_count // devices)
    slot_total = devices * capacity
    flat_ids = candidates.reshape(request_count)
    owner = flat_ids // blk_local
    position = jnp.arange(request_count, dtype=jnp.int32)
    earlier = (owner[None, :] == owner[:, None]) & (position[None, :] < position[:, None])
    owner_rank = jnp.sum(earlier, axis=1)
    target = owner * capacity + owner_rank
    slot_request = jnp.full((slot_total,), -1, jnp.int32).at[target].set(position)
    slot_used = slot_request >= 0
    safe_request = jnp.maximum(slot_request, 0)
    slot_block = jnp.where(slot_used, flat_ids[safe_request] % blk_local, -1)
    slot_query = jnp.where(slot_used, safe_request // cand_local, 0)
    grid_shape = (n_index, n_query, capacity)
    sent_rows = queries[slot_query].reshape(grid_shape + queries.shape[1:])
    got_rows, got_blocks = (
        lax.all_to_all(
            lax.all_to_all(sent_rows, "index", split_axis=0, concat_axis=0, tiled=True),
            "query",
            split_axis=1,
            concat_axis=1,
            tiled=True,
        ),
        lax.all_to_all(
            lax.all_to_all(
                slot_block.reshape(grid_shape), "index", split_axis=0, concat_axis=0, tiled=True
            ),
            "query",
            split_axis=1,
            concat_axis=1,
            tiled=True,
        ),
    )
    got_rows = got_rows.reshape((slot_total,) + queries.shape[1:])
    results = score_slots(got_rows, got_blocks.reshape(slot_total), passages, lengths)
    returned = lax.all_to_all(
        lax.all_to_all(
            results.reshape(grid_shape), "index", split_axis=0, concat_axis=0, tiled=True
        ),
        "query",
        split_axis=1,
        concat_axis=1,
        tiled=True,
    )
    return returned.reshape(slot_total)[target].reshape(q_local, cand_local)


def solution(mesh):
    in_specs = (
        P("query", None, None),
        P(("index", "query"), None, None),
        P(("index", "query")),
        P("query", "index"),
    )
    out_specs = P("query", "index")
    return jax.shard_map(shards, mesh=mesh, in_specs=in_specs, out_specs=out_specs, check_vma=False)
```

profile of v0, /device:TPU:1, one launch (start us, length us, event | category | flops | bytes accessed | tf_op | source)
XLA Modules:
  0.0 660.3 jit_solution(18072776988277648268)
XLA Ops:
  1.3 2.4 scatter_custom_fusion
  3.8 6.9 %gather_fusion.2 = s32[1024]{0:T(1024)S(1)} fusion(s32[512]{0:T(512)S(1)} %reshape.186, s32[1024]{0:T(1024)S(1)} %get-tuple-element.51), kind=kCustom, calls=%fused_computation.2 | custom fusion | bytes 12288 | tf_op jit(solution)/shard_map/gather | solution.py:50
  11.9 19.3 %all-to-all-start = ((s32[64,8,2]{1,2,0:T(2,128)}), s32[64,8,2]{1,2,0:T(2,128)S(1)}, u32[]{:S(2)}, u32[]{:S(2)}) async-start(s32[64,8,2]{1,2,0:T(2,128)} %copy.42), calls=%async_computation | async-start | bytes 131072 | tf_op jit(solution)/shard_map/all_to_all | solution.py:63
  31.2 9.9 %gather_fusion.3 = bf16[1024,32,128]{2,1,0:T(8,128)(2,1)} fusion(bf16[32,32,128]{2,1,0:T(8,128)(2,1)S(1)} %copy-done, s32[1024]{0:T(1024)S(1)} %get-tuple-element.50), kind=kCustom, calls=%fused_computation.3 | custom fusion | bytes 16781312 | tf_op jit(solution)/shard_map/gather | solution.py:53
  41.1 4.1 all-to-all-done
  45.2 10.7 %all-to-all-start.2 = ((bf16[64,8,2,32,128]{4,3,2,1,0:T(8,128)(2,1)}), bf16[64,8,2,32,128]{4,3,2,1,0:T(8,128)(2,1)}, u32[]{:S(2)}, u32[]{:S(2)}) async-start(bf16[64,8,2,32,128]{4,3,2,1,0:T(8,128)(2,1)} %bitcast.24), calls=%async_computation.2 | async-start | bytes 16777216 | tf_op jit(solution)/shard_map/all_to_all | solution.py:56
  56.7 360.2 %all-to-all-done.2 = bf16[64,8,2,32,128]{4,3,2,1,0:T(8,128)(2,1)} async-done(((bf16[64,8,2,32,128]{4,3,2,1,0:T(8,128)(2,1)}), bf16[64,8,2,32,128]{4,3,2,1,0:T(8,128)(2,1)}, u32[]{:S(2)}, u32[]{:S(2)}) %all-to-all-start.2) | async-done | bytes 8388640 | tf_op jit(solution)/shard_map/all_to_all | solution.py:56
  416.9 14.0 %all-to-all-start.1 = ((s32[8,1,128]{2,1,0:T(1,128)}), s32[8,1,128]{2,1,0:T(1,128)S(1)}, u32[]{:S(2)}, u32[]{:S(2)}) async-start(s32[8,1,128]{2,1,0:T(1,128)} %reshape.245), calls=%async_computation.1 | async-start | bytes 8192 | tf_op jit(solution)/shard_map/all_to_all | solution.py:62
  430.9 9.5 %copy.45 = bf16[64,8,2,32,128]{4,3,2,0,1:T(8,128)(2,1)} copy(bf16[64,8,2,32,128]{4,3,2,1,0:T(8,128)(2,1)} %all-to-all-done.2) | data formatting | bytes 16777216 | tf_op jit(solution)/shard_map/all_to_all | solution.py:56
  440.4 5.1 all-to-all-start.3
  447.1 92.1 %all-to-all-done.3 = bf16[64,8,2,32,128]{4,3,2,0,1:T(8,128)(2,1)} async-done(((bf16[64,8,2,32,128]{4,3,2,0,1:T(8,128)(2,1)}), bf16[64,8,2,32,128]{4,3,2,0,1:T(8,128)(2,1)}, u32[]{:S(2)}, u32[]{:S(2)}) %all-to-all-start.3) | async-done | bytes 8388640 | tf_op jit(solution)/shard_map/all_to_all | solution.py:55
  539.2 9.6 %copy.46 = bf16[64,8,2,32,128]{4,3,2,1,0:T(8,128)(2,1)} copy(bf16[64,8,2,32,128]{4,3,2,0,1:T(8,128)(2,1)} %all-to-all-done.3) | data formatting | bytes 16777216 | tf_op jit(solution)/shard_map/all_to_all | solution.py:55
  548.8 75.9 %while.10 = (s32[]{:T(128)}, f32[8,128]{1,0:T(8,128)S(1)}, s32[8,128]{1,0:T(8,128)S(1)}, s32[64]{0:T(128)S(1)}, bf16[8,128,32,128]{3,2,1,0:T(8,128)(2,1)}, /*ind...) while((s32[]{:T(128)}, f32[8,128]{1,0:T(8,128)S(1)}, s32[8,128]{1,0:T(8,128)S(1)}, ...), condition=%wide.region_5.6_spmd, body=%wide.region_2.5_spmd.sunk | while | flops 135284096 | bytes 13708909 | solution.py:28
  548.9 3.1 gather_fusion
  553.2 4.9 select_reduce_fusion.2
  558.3 3.1 gather_fusion
  562.7 4.9 select_reduce_fusion.2
  567.8 3.1 gather_fusion
  572.2 4.9 select_reduce_fusion.2
  577.3 3.1 gather_fusion
  581.7 4.9 select_reduce_fusion.2
  586.8 3.1 gather_fusion
  591.2 4.9 select_reduce_fusion.2
  596.3 3.1 gather_fusion
  600.7 4.9 select_reduce_fusion.2
  605.8 3.1 gather_fusion
  610.2 4.9 select_reduce_fusion.2
  615.3 3.1 gather_fusion
  619.7 4.9 select_reduce_fusion.2
  625.4 19.3 %all_to_all.30 = f32[64,8,2]{1,2,0:T(2,128)S(1)} all-to-all(f32[64,8,2]{1,2,0:T(2,128)S(1)} %copy.47), channel_id=1, replica_groups=mesh['index'=64,'query'=8] {'index'}, dimensions={0} | all-to-all | bytes 8192 | tf_op jit(solution)/shard_map/all_to_all | solution.py:75
  645.5 5.7 all-to-all-start.5
  651.2 4.5 all-to-all-done.5
  (95 shorter events, 22.7 us)
Async XLA Ops:
  0.0 31.2 %copy-start = (bf16[32,32,128]{2,1,0:T(8,128)(2,1)S(1)}, bf16[32,32,128]{2,1,0:T(8,128)(2,1)}, u32[]{:S(2)}) copy-start(bf16[32,32,128]{2,1,0:T(8,128)(2,1)} %param.6) | copy-start | bytes 786436
  11.9 33.3 %all-to-all-start = ((s32[64,8,2]{1,2,0:T(2,128)}), s32[64,8,2]{1,2,0:T(2,128)S(1)}, u32[]{:S(2)}, u32[]{:S(2)}) async-start(s32[64,8,2]{1,2,0:T(2,128)} %copy.42), calls=%async_computation | async-start | bytes 131072 | tf_op jit(solution)/shard_map/all_to_all | solution.py:63
  45.2 371.7 %all-to-all-start.2 = ((bf16[64,8,2,32,128]{4,3,2,1,0:T(8,128)(2,1)}), bf16[64,8,2,32,128]{4,3,2,1,0:T(8,128)(2,1)}, u32[]{:S(2)}, u32[]{:S(2)}) async-start(bf16[64,8,2,32,128]{4,3,2,1,0:T(8,128)(2,1)} %bitcast.24), calls=%async_computation.2 | async-start | bytes 16777216 | tf_op jit(solution)/shard_map/all_to_all | solution.py:56
  416.9 23.5 %all-to-all-start.1 = ((s32[8,1,128]{2,1,0:T(1,128)}), s32[8,1,128]{2,1,0:T(1,128)S(1)}, u32[]{:S(2)}, u32[]{:S(2)}) async-start(s32[8,1,128]{2,1,0:T(1,128)} %reshape.245), calls=%async_computation.1 | async-start | bytes 8192 | tf_op jit(solution)/shard_map/all_to_all | solution.py:62
  440.4 98.8 %all-to-all-start.3 = ((bf16[64,8,2,32,128]{4,3,2,0,1:T(8,128)(2,1)}), bf16[64,8,2,32,128]{4,3,2,0,1:T(8,128)(2,1)}, u32[]{:S(2)}, u32[]{:S(2)}) async-start(bf16[64,8,2,32,128]{4,3,2,0,1:T(8,128)(2,1)} %copy.45), calls=%async_computation.3 | async-start | bytes 16777216 | tf_op jit(solution)/shard_map/all_to_all | solution.py:55
  447.1 101.8 %copy-start.1 = (s32[64]{0:T(128)S(1)}, s32[64]{0:T(128)}, u32[]{:S(2)}) copy-start(s32[64]{0:T(128)} %param.8) | copy-start | bytes 772
  447.1 101.8 %copy-start.2 = (bf16[64,128,128]{2,1,0:T(8,128)(2,1)S(1)}, bf16[64,128,128]{2,1,0:T(8,128)(2,1)}, u32[]{:S(2)}) copy-start(bf16[64,128,128]{2,1,0:T(8,128)(2,1)} %param.7) | copy-start | bytes 6291460
  645.5 10.2 %all-to-all-start.5 = ((f32[8,1,128]{2,1,0:T(1,128)}), f32[8,1,128]{2,1,0:T(1,128)S(1)}, u32[]{:S(2)}, u32[]{:S(2)}) async-start(f32[8,1,128]{2,1,0:T(1,128)} %reshape.247), calls=%async_computation.5 | async-start | bytes 8192 | tf_op jit(solution)/shard_map/all_to_all | solution.py:74
where the time goes:
time: 661 us; the launch traced here: 660 us
  waiting for transfers between devices  461 us (70%)
  local copies, waits for them, and re-layouts  82.2 us (12%)
  starting transfers between devices  54.7 us (8%)
  matrix products  39.1 us (6%)
  blocking collectives  19.3 us (3%)
    all_to_all x1, waiting for transfers between devices, shards(): lax.all_to_all(sent_rows, 'index', split_axis=0, concat_axis=0, tiled=True)  360 us
    all_to_all x1, waiting for transfers between devices, shards(): lax.all_to_all(lax.all_to_all(sent_rows, 'index', split_axis=0, concat_ax...  92.1 us
    dot_general x8, matrix products, score_group(): jnp.einsum('gtd,gpd->gtp', query_rows, block_rows, preferred_element_type...  39.1 us
    gather x8, local copies, waits for them, and re-layouts, score_group(): block_rows = passages[safe_ids]  24.5 us
    all_to_all x1, blocking collectives, shards(): lax.all_to_all(results.reshape(grid_shape), 'index', split_axis=0, concat...  19.3 us
    all_to_all x1, starting transfers between devices, shards(): lax.all_to_all(slot_block.reshape(grid_shape), 'index', split_axis=0, con...  19.3 us
    all_to_all x1, starting transfers between devices, shards(): lax.all_to_all(lax.all_to_all(slot_block.reshape(grid_shape), 'index', sp...  14 us
  transfers between devices with their start and end apart: 5, of which 4 were waited for; matrix products, arithmetic and copies ran while one was open for 3% of the time, Pallas kernels for 0%

commit v1 on v0

v1 whole, which is shorter than its diff:
```python
import jax
import jax.numpy as jnp
from jax import lax
from jax.experimental import pallas as pl
from jax.experimental.pallas import tpu as pltpu
from jax.sharding import PartitionSpec as P

Z, Y, Q = 16, 4, 8
YQ = Y * Q
OWNERS = Z * YQ
BLK = 64
QL, CL = 32, 16
NQ = Q * QL
T, D, PT = 32, 128, 128
GROUP = 8
GMAX = 192
UNROLL = 8
BIG = 1 << 30

Z_GROUPS = [[r + YQ * z for z in range(Z)] for r in range(YQ)]
YQ_GROUPS = [[YQ * z + r for r in range(YQ)] for z in range(Z)]


def iota(shape, axis):
    return lax.broadcasted_iota(jnp.int32, shape, axis)


def exchange(x, groups):
    return lax.all_to_all(
        x, ("index", "query"), split_axis=0, concat_axis=0, tiled=True,
        axis_index_groups=groups,
    )


def request_kernel(cand_ref, table_ref, first_ref):
    cand = cand_ref[...]
    lane_owner = iota((CL, OWNERS), 1)
    sub = iota((CL, 1), 0)
    low = jnp.full((CL, OWNERS), BIG, jnp.int32)
    high = jnp.full((CL, OWNERS), -1, jnp.int32)
    for q in range(QL):
        col = cand[:, q : q + 1]
        key = (q << 10) + (sub << 6) + (col & 63)
        match = (col >> 6) == lane_owner
        low = jnp.minimum(low, jnp.where(match, key, BIG))
        high = jnp.maximum(high, jnp.where(match, key, -1))
    first = jnp.min(low, axis=0, keepdims=True)
    last = jnp.max(high, axis=0, keepdims=True)
    first_ref[...] = first

    def code(key):
        return ((key >> 10) << 6) + (key & 63)

    slot0 = jnp.where(last >= 0, code(first), -1)
    slot1 = jnp.where((last >= 0) & (last != first), code(last), -1)
    row = iota((Z, 128), 0)
    lane = iota((Z, 128), 1)
    out = jnp.full((Z, 128), -1, jnp.int32)
    for k, slot in enumerate((slot0, slot1)):
        for j in range(4):
            shift = (32 * k - 32 * j) % 128
            for t in range(4):
                seg = jnp.broadcast_to(slot[:, 128 * t : 128 * (t + 1)], (Z, 128))
                seg = pltpu.roll(seg, shift, 1) if shift else seg
                out = jnp.where((row == 4 * t + j) & (lane >> 5 == k), seg, out)
    table_ref[...] = out


def turn_kernel(x_ref, o_ref):
    x = jnp.concatenate([x_ref[...], jnp.zeros((112, 128), jnp.int32)], axis=0)
    xt = jnp.transpose(x)
    lane = iota((YQ, 128), 1)
    o_ref[...] = jnp.where(lane < Z, xt[:YQ], pltpu.roll(xt[YQ : 2 * YQ], Z, 1))


def back_kernel(x_ref, o_ref):
    x = jnp.concatenate([x_ref[...], jnp.zeros((96, 128), jnp.float32)], axis=0)
    xt = jnp.transpose(x)
    lane = iota((Z, 128), 1)
    o_ref[...] = jnp.where(lane < YQ, xt[:Z], pltpu.roll(xt[Z : 2 * Z], YQ, 1))


def split3(x):
    hi = x.astype(jnp.bfloat16)
    rest = x - hi.astype(jnp.float32)
    mid = rest.astype(jnp.bfloat16)
    low = (rest - mid.astype(jnp.float32)).astype(jnp.bfloat16)
    return hi, mid, low


def dot(a, b, dims):
    return lax.dot_general(a, b, (dims, ((), ())), preferred_element_type=jnp.float32)


def score_kernel(len_ref, code_ref, q_ref, p_ref, o_ref, plan, plan_s, onehot, best, sem):
    code = jnp.full((Q, 128), -1, jnp.int32)
    lane8 = iota((Q, 128), 1)
    for y in range(Y):
        part = code_ref[Q * y : Q * (y + 1), :]
        part = pltpu.roll(part, 32 * y, 1) if y else part
        code = jnp.where(lane8 >> 5 == y, part, code)
    valid = code >= 0
    block = jnp.where(valid, code & 63, BLK)
    query = jnp.where(valid, (code >> 6) + QL * iota((Q, 128), 0), 0)

    b_iota = iota((BLK, 128), 0)
    hits = [block[q : q + 1, :] == b_iota for q in range(Q)]
    hit = jnp.concatenate([h.astype(jnp.float32) for h in hits], axis=0).astype(jnp.bfloat16)
    r_i, c_i = iota((128, 128), 0), iota((128, 128), 1)
    earlier = jnp.concatenate(
        [(r_i < c_i).astype(jnp.float32), jnp.ones((128, 128), jnp.float32)], axis=1
    ).astype(jnp.bfloat16)
    sums = dot(hit, earlier, ((1,), (0,)))
    base = jnp.zeros((BLK, 128), jnp.float32)
    bases = []
    for q in range(Q):
        bases.append(base + sums[BLK * q : BLK * (q + 1), :128])
        base = base + sums[BLK * q : BLK * (q + 1), 128:]
    groups = ((base.astype(jnp.int32) + (GROUP - 1)) >> 3).astype(jnp.float32)
    l_i, m_i = iota((BLK, BLK), 0), iota((BLK, BLK), 1)
    before = dot(
        (m_i < l_i).astype(jnp.float32).astype(jnp.bfloat16),
        groups.astype(jnp.bfloat16),
        ((1,), (0,)),
    )
    ends = (before + groups).astype(jnp.int32)
    dest = jnp.concatenate(
        [
            jnp.sum(jnp.where(hits[q], GROUP * before + bases[q], 0.0), axis=0, keepdims=True)
            for q in range(Q)
        ],
        axis=0,
    ).astype(jnp.int32)

    g_iota = iota((GMAX, 128), 0)
    c_iota = iota((GROUP, 128), 0)
    named = []
    for q in range(Q):
        d = dest[q : q + 1, :]
        onehot[:, 128 * q : 128 * (q + 1)] = (
            ((d >> 3) == g_iota).astype(jnp.float32).astype(jnp.bfloat16)
        )
        here = ((d & 7) == c_iota) & valid[q : q + 1, :]
        named.append(jnp.where(here, query[q : q + 1, :], 0).astype(jnp.float32))
    lists = dot(
        jnp.concatenate(named, axis=1).astype(jnp.bfloat16), onehot[...], ((1,), (1,))
    )
    plan[0:GROUP, 0:GMAX] = lists.astype(jnp.int32)
    g_lane = iota((BLK, 256), 1)
    ends2 = jnp.concatenate([ends, ends], axis=1)
    owner_block = jnp.minimum(
        jnp.sum((ends2 <= g_lane).astype(jnp.int32), axis=0, keepdims=True), BLK - 1
    )
    total = jnp.broadcast_to(ends2[BLK - 1 : BLK, :], (1, 256))
    plan[GROUP : 2 * GROUP, :] = jnp.where(
        iota((GROUP, 256), 0) == 0,
        jnp.broadcast_to(owner_block, (GROUP, 256)),
        jnp.broadcast_to(total, (GROUP, 256)),
    )
    copy = pltpu.make_async_copy(plan, plan_s, sem)
    copy.start()
    best[...] = jnp.zeros((GMAX, GROUP * T), jnp.float32)
    copy.wait()

    token = iota((PT, GROUP * T), 0)

    def step(it, carry):
        rows = []
        for u in range(UNROLL):
            g = it * UNROLL + u
            b = plan_s[GROUP, g]
            rows_q = jnp.concatenate([q_ref[plan_s[c, g]] for c in range(GROUP)], axis=0)
            similar = dot(p_ref[b], rows_q, ((1,), (1,)))
            similar = jnp.where(token < len_ref[b], similar, -jnp.inf)
            rows.append(jnp.max(similar, axis=0, keepdims=True))
        best[pl.ds(pl.multiple_of(it * UNROLL, UNROLL), UNROLL), :] = jnp.concatenate(rows, axis=0)
        return carry

    lax.fori_loop(0, (plan_s[GROUP + 1, 0] + (UNROLL - 1)) // UNROLL, step, 0)

    w = (iota((GROUP, GROUP * T), 0) == (iota((GROUP, GROUP * T), 1) >> 5)).astype(jnp.float32)
    w = w.astype(jnp.bfloat16)
    means = sum(dot(w, part, ((1,), (1,))) for part in split3(best[...])) * (1.0 / T)
    picked = dot(jnp.concatenate(split3(means), axis=0), onehot[...], ((1,), (0,)))
    picked = picked[0:GROUP] + picked[GROUP : 2 * GROUP] + picked[2 * GROUP : 3 * GROUP]
    out = []
    for q in range(Q):
        here = (dest[q : q + 1, :] & 7) == c_iota
        out.append(
            jnp.sum(jnp.where(here, picked[:, 128 * q : 128 * (q + 1)], 0.0), axis=0, keepdims=True)
        )
    out = jnp.concatenate(out, axis=0)
    for y in range(Y):
        shift = (128 - 32 * y) % 128
        o_ref[Q * y : Q * (y + 1), :] = pltpu.roll(out, shift, 1) if shift else out


def place_kernel(cand_ref, first_ref, x_ref, o_ref):
    cand = cand_ref[...]
    x = x_ref[...]
    lane = iota((1, 128), 1)
    values = []
    for k in range(2):
        segs = []
        for t in range(4):
            seg = jnp.zeros((1, 128), jnp.float32)
            for j in range(4):
                row = x[4 * t + j : 4 * t + j + 1, :]
                shift = (32 * j - 32 * k) % 128
                row = pltpu.roll(row, shift, 1) if shift else row
                seg = jnp.where(lane >> 5 == j, row, seg)
            segs.append(seg)
        values.append(jnp.concatenate(segs, axis=1))
    lane_owner = iota((CL, OWNERS), 1)
    sub = iota((CL, 1), 0)
    first = jnp.broadcast_to(first_ref[...], (CL, OWNERS))
    value0 = jnp.broadcast_to(values[0], (CL, OWNERS))
    value1 = jnp.broadcast_to(values[1], (CL, OWNERS))
    out_lane = iota((CL, QL), 1)
    out = jnp.zeros((CL, QL), jnp.float32)
    for q in range(QL):
        col = cand[:, q : q + 1]
        key = (q << 10) + (sub << 6) + (col & 63)
        value = jnp.where(first == key, value0, value1)
        hit = jnp.where((col >> 6) == lane_owner, value, 0.0)
        out = jnp.where(out_lane == q, jnp.sum(hit, axis=1, keepdims=True), out)
    o_ref[...] = out


def small_call(kernel, out_shape, *args):
    return pl.pallas_call(kernel, out_shape=out_shape)(*args)


def shards(queries, passages, lengths, candidates):
    every = lax.all_to_all(
        jnp.broadcast_to(queries[None], (Q,) + queries.shape),
        "query", split_axis=0, concat_axis=0, tiled=True,
    ).reshape(NQ, T, D)
    cand = candidates.T
    table, first = small_call(
        request_kernel,
        (
            jax.ShapeDtypeStruct((Z, 128), jnp.int32),
            jax.ShapeDtypeStruct((1, OWNERS), jnp.int32),
        ),
        cand,
    )
    got = exchange(table, Z_GROUPS)
    got = small_call(turn_kernel, jax.ShapeDtypeStruct((YQ, 128), jnp.int32), got)
    codes = exchange(got, YQ_GROUPS)
    vmem = pl.BlockSpec(memory_space=pltpu.VMEM)
    scores = pl.pallas_call(
        score_kernel,
        out_shape=jax.ShapeDtypeStruct((YQ, 128), jnp.float32),
        in_specs=[pl.BlockSpec(memory_space=pltpu.SMEM), vmem, vmem, vmem],
        out_specs=vmem,
        scratch_shapes=[
            pltpu.VMEM((2 * GROUP, 256), jnp.int32),
            pltpu.SMEM((2 * GROUP, 256), jnp.int32),
            pltpu.VMEM((GMAX, Q * 128), jnp.bfloat16),
            pltpu.VMEM((GMAX, GROUP * T), jnp.float32),
            pltpu.SemaphoreType.DMA,
        ],
        compiler_params=pltpu.CompilerParams(vmem_limit_bytes=32 << 20),
    )(lengths, codes, every, passages)
    back = exchange(scores, YQ_GROUPS)
    back = small_call(back_kernel, jax.ShapeDtypeStruct((Z, 128), jnp.float32), back)
    back = exchange(back, Z_GROUPS)
    out = small_call(
        place_kernel, jax.ShapeDtypeStruct((CL, QL), jnp.float32), cand, first, back
    )
    return out.T


def solution(mesh):
    in_specs = (
        P("query", None, None),
        P(("index", "query"), None, None),
        P(("index", "query")),
        P("query", "index"),
    )
    return jax.shard_map(
        shards, mesh=mesh, in_specs=in_specs, out_specs=P("query", "index"), check_vma=False
    )
```

time: 661 us -> 116 us (0.18)
  waiting for transfers between devices: 461 us -> 0 us
  local copies, waits for them, and re-layouts: 82.2 us -> 1.32 us
  blocking collectives: 19.3 us -> 99.4 us
  starting transfers between devices: 54.7 us -> 0 us
  matrix products: 39.1 us -> 0 us
  Pallas kernels: 0 us -> 15.1 us
    all_to_all x5 -> x0, waiting for transfers between devices: 461 us -> none  [the longest x1 360 us: shards(): lax.all_to_all(sent_rows, 'index', split_axis=0, concat_axis=0, tiled=True)]
    all_to_all x1 -> x5, blocking collectives: 19.3 us -> 99.4 us  [the longest x4 69.7 us: exchange(): lax.all_to_all(x, ('index', 'query'), split_axis=0, concat_axis=0, tiled=...]
    all_to_all x5 -> x0, starting transfers between devices: 54.7 us -> none  [the longest x1 19.3 us: shards(): lax.all_to_all(slot_block.reshape(grid_shape), 'index', split_axis=0, con...]
    gather x19 -> x0, local copies, waits for them, and re-layouts: 53.3 us -> none  [the longest x8 24.5 us: score_group(): block_rows = passages[safe_ids]]
    dot_general x8 -> x0, matrix products: 39.1 us -> none  [score_group(): jnp.einsum('gtd,gpd->gtp', query_rows, block_rows, preferred_element_type...]
    all_to_all x8 -> x0, local copies, waits for them, and re-layouts: 20.6 us -> none  [the longest x1 9.61 us: shards(): lax.all_to_all(lax.all_to_all(sent_rows, 'index', split_axis=0, concat_ax...]
    pallas_call x0 -> x5, Pallas kernels: none -> 15.1 us  [the longest x4 8.53 us: small_call(): return pl.pallas_call(kernel, out_shape=out_shape)(*args)]
  transfers between devices with their start and end apart: 5 -> 0, of which waited for: 4 -> 0; matrix products, arithmetic and copies ran while one was open for 3% -> 0% of each run, Pallas kernels for 0% -> 0%
where the time goes in v1:
time: 116 us
  blocking collectives  99.4 us (86%)
  Pallas kernels  15.1 us (13%)
  local copies, waits for them, and re-layouts  1.32 us (1%)
    all_to_all x4, blocking collectives, exchange(): lax.all_to_all(x, ('index', 'query'), split_axis=0, concat_axis=0, tiled=...  69.7 us
    all_to_all x1, blocking collectives, shards(): lax.all_to_all(jnp.broadcast_to(queries[None], (Q,) + queries.shape), 'qu...  29.7 us
    pallas_call x4, Pallas kernels, small_call(): return pl.pallas_call(kernel, out_shape=out_shape)(*args)  8.53 us
    pallas_call x1, Pallas kernels, shards(): pl.pallas_call(score_kernel, out_shape=jax.ShapeDtypeStruct((YQ, 128), jn...  6.53 us

profile of v1, /device:TPU:1, one launch (start us, length us, event | category | flops | bytes accessed | tf_op | source)
XLA Modules:
  0.0 115.8 jit_solution(17587942689651019163)
XLA Ops:
  0.0 1.7 %shard_map.46 = (s32[16,128]{1,0:T(8,128)}, s32[1,512]{1,0:T(1,128)}) custom-call(s32[16,32]{1,0:T(8,128)} %bitcast.26), custom_call_target="tpu_custom_call" | custom-call | tf_op jit(solution)/shard_map/pallas_call | solution.py:231
  1.8 26.9 %all_to_all.49 = s32[16,1,128]{2,1,0:T(1,128)} all-to-all(s32[16,1,128]{2,1,0:T(1,128)} %bitcast.29), channel_id=1, replica_groups={{0,32,64,96,128,160,192,224,256,288,320,352,384,416,448,480},{1,33,65,9..., dimensions={0} | all-to-all | bytes 16384 | tf_op jit(solution)/shard_map/all_to_all | solution.py:29
  28.7 1.4 %shard_map.47 = s32[32,128]{1,0:T(8,128)} custom-call(s32[16,128]{1,0:T(8,128)} %bitcast.24), custom_call_target="tpu_custom_call" | custom-call | tf_op jit(solution)/shard_map/pallas_call | solution.py:231
  30.1 16.3 %all_to_all.50 = s32[32,1,128]{2,1,0:T(1,128)S(1)} all-to-all(s32[32,1,128]{2,1,0:T(1,128)} %bitcast.22), channel_id=1, replica_groups={{0,1,2,3,4,5,6,7,8,9,10,11,12,13,14,15,16,17,18,19,20,21,22,23,24,25,26..., dimensions={0} | all-to-all | bytes 32768 | tf_op jit(solution)/shard_map/all_to_all | solution.py:29
  46.4 1.3 %broadcast_in_dim.2 = bf16[8,32,32,128]{3,2,1,0:T(8,128)(2,1)S(1)} broadcast(bf16[32,32,128]{2,1,0:T(8,128)(2,1)} %param.4), dimensions={1,2,3} | broadcast | bytes 2359296 | tf_op jit(solution)/shard_map/broadcast_in_dim | solution.py:236
  47.7 0.0 copy-start
  47.7 0.0 copy-start.1
  47.7 29.7 %all_to_all.51 = bf16[8,32,32,128]{3,2,1,0:T(8,128)(2,1)S(1)} all-to-all(bf16[8,32,32,128]{3,2,1,0:T(8,128)(2,1)S(1)} %broadcast_in_dim.2), channel_id=1, replica_groups=mesh['index'=64,'query'=8] {'query'}, dimensions={0} | all-to-all | bytes 4194304 | tf_op jit(solution)/shard_map/all_to_all | solution.py:235
  77.4 0.0 copy-done
  77.4 0.0 copy-done.1
  77.4 6.5 %shard_map.48 = f32[32,128]{1,0:T(8,128)S(1)} custom-call(s32[64]{0:T(128)S(1)} %copy-done.1, s32[32,128]{1,0:T(8,128)S(1)} %bitcast.20, bf16[256,32,128]{2,1,0:T(8,128)(2,1)S(1)} %bitcast.19, bf16[64,128,128]{2,1,0:T(8,128)(2,1)S(1)} %copy-done), custom_call_target="tpu_custom_call" | custom-call | tf_op jit(solution)/shard_map/pallas_call | solution.py:252
  84.0 11.4 %all_to_all.52 = f32[32,1,128]{2,1,0:T(1,128)} all-to-all(f32[32,1,128]{2,1,0:T(1,128)S(1)} %bitcast.21), channel_id=1, replica_groups={{0,1,2,3,4,5,6,7,8,9,10,11,12,13,14,15,16,17,18,19,20,21,22,23,24,25,26..., dimensions={0} | all-to-all | bytes 32768 | tf_op jit(solution)/shard_map/all_to_all | solution.py:29
  95.4 1.5 %shard_map.49 = f32[16,128]{1,0:T(8,128)} custom-call(f32[32,128]{1,0:T(8,128)} %bitcast.23), custom_call_target="tpu_custom_call" | custom-call | tf_op jit(solution)/shard_map/pallas_call | solution.py:231
  96.8 15.1 %all_to_all.53 = f32[16,1,128]{2,1,0:T(1,128)} all-to-all(f32[16,1,128]{2,1,0:T(1,128)} %bitcast.25), channel_id=1, replica_groups={{0,32,64,96,128,160,192,224,256,288,320,352,384,416,448,480},{1,33,65,9..., dimensions={0} | all-to-all | bytes 16384 | tf_op jit(solution)/shard_map/all_to_all | solution.py:29
  111.9 3.9 %shard_map.50 = f32[16,32]{1,0:T(8,128)} custom-call(s32[16,32]{1,0:T(8,128)} %bitcast.27, s32[1,512]{1,0:T(1,128)} %get-tuple-element.7.first_ref, f32[16,128]{1,0:T(8,128)} %bitcast.28), custom_call_target="tpu_custom_call" | custom-call | tf_op jit(solution)/shard_map/pallas_call | solution.py:231
Async XLA Ops:
  47.7 29.7 %copy-start = (bf16[64,128,128]{2,1,0:T(8,128)(2,1)S(1)}, bf16[64,128,128]{2,1,0:T(8,128)(2,1)}, u32[]{:S(2)}) copy-start(bf16[64,128,128]{2,1,0:T(8,128)(2,1)} %p_ref.1) | copy-start | bytes 6291460
  47.7 29.7 %copy-start.1 = (s32[64]{0:T(128)S(1)}, s32[64]{0:T(128)}, u32[]{:S(2)}) copy-start(s32[64]{0:T(128)} %len_ref.1) | copy-start | bytes 772

commit v2 on v1

--- a/solution.py
+++ b/solution.py
@@ -232,10 +232,7 @@
 
 
 def shards(queries, passages, lengths, candidates):
-    every = lax.all_to_all(
-        jnp.broadcast_to(queries[None], (Q,) + queries.shape),
-        "query", split_axis=0, concat_axis=0, tiled=True,
-    ).reshape(NQ, T, D)
+    every = lax.all_gather(queries, "query", axis=0, tiled=True)
     cand = candidates.T
     table, first = small_call(
         request_kernel,

time: 116 us -> 107 us (0.922)
  blocking collectives: 99.4 us -> 73.9 us
  between operations: 0.04 us -> 13.4 us
  local copies, waits for them, and re-layouts: 1.32 us -> 3.84 us
    all_to_all x1 -> x0, blocking collectives: 29.7 us -> none  [shards(): lax.all_to_all(jnp.broadcast_to(queries[None], (Q,) + queries.shape), 'qu...]
    all_to_all x4, blocking collectives: 69.7 us -> 73.9 us  [exchange(): lax.all_to_all(x, ('index', 'query'), split_axis=0, concat_axis=0, tiled=...]
    unnamed x4 -> x6, local copies, waits for them, and re-layouts: 0.01 us -> 3.84 us
    broadcast_in_dim x1 -> x0, local copies, waits for them, and re-layouts: 1.31 us -> none  [shards(): jnp.broadcast_to(queries[None], (Q,) + queries.shape)]
  transfers between devices with their start and end apart: 0 -> 1, of which waited for: 0 -> 0; matrix products, arithmetic and copies ran while one was open for 0% -> 0% of each run, Pallas kernels for 0% -> 3%
where the time goes in v2:
time: 107 us
  blocking collectives  73.9 us (69%)
  Pallas kernels  15.1 us (14%)
  between operations  13.4 us (13%)
  local copies, waits for them, and re-layouts  3.84 us (4%)
    all_to_all x4, blocking collectives, exchange(): lax.all_to_all(x, ('index', 'query'), split_axis=0, concat_axis=0, tiled=...  73.9 us
    pallas_call x4, Pallas kernels, small_call(): return pl.pallas_call(kernel, out_shape=out_shape)(*args)  8.53 us
    pallas_call x1, Pallas kernels, shards(): pl.pallas_call(score_kernel, out_shape=jax.ShapeDtypeStruct((YQ, 128), jn...  6.53 us
    unnamed x6, local copies, waits for them, and re-layouts  3.84 us
  transfers between devices with their start and end apart: 1, of which 0 were waited for; matrix products, arithmetic and copies ran while one was open for 0% of the time, Pallas kernels for 3%

profile of v2, /device:TPU:1, one launch (start us, length us, event | category | flops | bytes accessed | tf_op | source)
XLA Modules:
  0.0 106.9 jit_solution(11743828517602362390)
XLA Ops:
  6.5 0.0 all-gather.2.cloned.1.call-start
  6.5 0.7 all-gather.2.cloned.1.call-update
  7.3 1.8 %shard_map.46 = (s32[16,128]{1,0:T(8,128)}, s32[1,512]{1,0:T(1,128)}) custom-call(s32[16,32]{1,0:T(8,128)} %bitcast.24), custom_call_target="tpu_custom_call" | custom-call | tf_op jit(solution)/shard_map/pallas_call | solution.py:231
  9.0 27.1 %all_to_all.44 = s32[16,1,128]{2,1,0:T(1,128)} all-to-all(s32[16,1,128]{2,1,0:T(1,128)} %bitcast.27), channel_id=1, replica_groups={{0,32,64,96,128,160,192,224,256,288,320,352,384,416,448,480},{1,33,65,9..., dimensions={0} | all-to-all | bytes 16384 | tf_op jit(solution)/shard_map/all_to_all | solution.py:29
  36.1 1.4 %shard_map.47 = s32[32,128]{1,0:T(8,128)} custom-call(s32[16,128]{1,0:T(8,128)} %bitcast.22), custom_call_target="tpu_custom_call" | custom-call | tf_op jit(solution)/shard_map/pallas_call | solution.py:231
  37.5 16.0 %all_to_all.45 = s32[32,1,128]{2,1,0:T(1,128)S(1)} all-to-all(s32[32,1,128]{2,1,0:T(1,128)} %bitcast.20), channel_id=1, replica_groups={{0,1,2,3,4,5,6,7,8,9,10,11,12,13,14,15,16,17,18,19,20,21,22,23,24,25,26..., dimensions={0} | all-to-all | bytes 32768 | tf_op jit(solution)/shard_map/all_to_all | solution.py:29
  53.5 0.0 all-gather.2.cloned.1.call-done.q_ref
  53.5 0.0 copy-start
  53.5 1.6 %copy-done = bf16[64,128,128]{2,1,0:T(8,128)(2,1)S(1)} copy-done((bf16[64,128,128]{2,1,0:T(8,128)(2,1)S(1)}, bf16[64,128,128]{2,1,0:T(8,128)(2,1)}, u32[]{:S(2)}) %copy-start) | copy-done | bytes 2097176
  55.1 0.0 copy-start.1
  55.1 1.6 %copy-done.1 = bf16[256,32,128]{2,1,0:T(8,128)(2,1)S(1)} copy-done((bf16[256,32,128]{2,1,0:T(8,128)(2,1)S(1)}, bf16[256,32,128]{2,1,0:T(8,128)(2,1)}, u32[]{:S(2)}) %copy-start.1) | copy-done | bytes 2097176
  56.7 0.0 copy-start.2
  56.7 0.7 copy-done.2
  57.3 6.5 %shard_map.48 = f32[32,128]{1,0:T(8,128)S(1)} custom-call(s32[64]{0:T(128)S(1)} %copy-done.2, s32[32,128]{1,0:T(8,128)S(1)} %bitcast.18, bf16[256,32,128]{2,1,0:T(8,128)(2,1)S(1)} %copy-done.1, bf16[64,128,128]{2,1,0:T(8,128)(2,1)S(1)} %copy-done), custom_call_target="tpu_custom_call" | custom-call | tf_op jit(solution)/shard_map/pallas_call | solution.py:249
  63.9 11.0 %all_to_all.46 = f32[32,1,128]{2,1,0:T(1,128)} all-to-all(f32[32,1,128]{2,1,0:T(1,128)S(1)} %bitcast.19), channel_id=1, replica_groups={{0,1,2,3,4,5,6,7,8,9,10,11,12,13,14,15,16,17,18,19,20,21,22,23,24,25,26..., dimensions={0} | all-to-all | bytes 32768 | tf_op jit(solution)/shard_map/all_to_all | solution.py:29
  74.9 1.5 %shard_map.49 = f32[16,128]{1,0:T(8,128)} custom-call(f32[32,128]{1,0:T(8,128)} %bitcast.21), custom_call_target="tpu_custom_call" | custom-call | tf_op jit(solution)/shard_map/pallas_call | solution.py:231
  76.4 19.8 %all_to_all.47 = f32[16,1,128]{2,1,0:T(1,128)} all-to-all(f32[16,1,128]{2,1,0:T(1,128)} %bitcast.23), channel_id=1, replica_groups={{0,32,64,96,128,160,192,224,256,288,320,352,384,416,448,480},{1,33,65,9..., dimensions={0} | all-to-all | bytes 16384 | tf_op jit(solution)/shard_map/all_to_all | solution.py:29
  96.2 3.9 %shard_map.50 = f32[16,32]{1,0:T(8,128)} custom-call(s32[16,32]{1,0:T(8,128)} %bitcast.25, s32[1,512]{1,0:T(1,128)} %get-tuple-element.7.first_ref, f32[16,128]{1,0:T(8,128)} %bitcast.26), custom_call_target="tpu_custom_call" | custom-call | tf_op jit(solution)/shard_map/pallas_call | solution.py:231
Async XLA Ops:
  6.5 47.0 %all-gather.2.cloned.1.call-start = ((), (), s32[]{:S(2)}) async-start(), calls=%async_computation.4 | async-start | bytes 2359296 | tf_op jit(solution)/shard_map/all_gather | solution.py:235
  53.5 1.6 %copy-start = (bf16[64,128,128]{2,1,0:T(8,128)(2,1)S(1)}, bf16[64,128,128]{2,1,0:T(8,128)(2,1)}, u32[]{:S(2)}) copy-start(bf16[64,128,128]{2,1,0:T(8,128)(2,1)} %p_ref.1) | copy-start | bytes 6291460
  55.1 1.6 %copy-start.1 = (bf16[256,32,128]{2,1,0:T(8,128)(2,1)S(1)}, bf16[256,32,128]{2,1,0:T(8,128)(2,1)}, u32[]{:S(2)}) copy-start(bf16[256,32,128]{2,1,0:T(8,128)(2,1)} %all-gather.2.cloned.1.call-done.q_ref) | copy-start | bytes 6291460
  56.7 0.7 copy-start.2
Sparse Core Ops, SparseCore 0:
  9.5 38.5 all-gather.1

commit v3 on v2

--- a/solution.py
+++ b/solution.py
@@ -32,7 +32,19 @@
     )
 
 
-def request_kernel(cand_ref, table_ref, first_ref):
+def spread(rows, row, lane):
+    out = jnp.zeros((Z, 128), jnp.int32)
+    for k, slot in enumerate(rows):
+        for j in range(4):
+            shift = (32 * k - 32 * j) % 128
+            for t in range(4):
+                seg = jnp.broadcast_to(slot[:, 128 * t : 128 * (t + 1)], (Z, 128))
+                seg = pltpu.roll(seg, shift, 1) if shift else seg
+                out = jnp.where((row == 4 * t + j) & (lane >> 5 == k), seg, out)
+    return out
+
+
+def request_kernel(cand_ref, code_ref, key_ref):
     cand = cand_ref[...]
     lane_owner = iota((CL, OWNERS), 1)
     sub = iota((CL, 1), 0)
@@ -44,26 +56,16 @@
         match = (col >> 6) == lane_owner
         low = jnp.minimum(low, jnp.where(match, key, BIG))
         high = jnp.maximum(high, jnp.where(match, key, -1))
-    first = jnp.min(low, axis=0, keepdims=True)
     last = jnp.max(high, axis=0, keepdims=True)
-    first_ref[...] = first
-
-    def code(key):
-        return ((key >> 10) << 6) + (key & 63)
-
-    slot0 = jnp.where(last >= 0, code(first), -1)
-    slot1 = jnp.where((last >= 0) & (last != first), code(last), -1)
+    first = jnp.where(last >= 0, jnp.min(low, axis=0, keepdims=True), -1)
+    last = jnp.where(last != first, last, -1)
     row = iota((Z, 128), 0)
     lane = iota((Z, 128), 1)
-    out = jnp.full((Z, 128), -1, jnp.int32)
-    for k, slot in enumerate((slot0, slot1)):
-        for j in range(4):
-            shift = (32 * k - 32 * j) % 128
-            for t in range(4):
-                seg = jnp.broadcast_to(slot[:, 128 * t : 128 * (t + 1)], (Z, 128))
-                seg = pltpu.roll(seg, shift, 1) if shift else seg
-                out = jnp.where((row == 4 * t + j) & (lane >> 5 == k), seg, out)
-    table_ref[...] = out
+    key = spread((first, last), row, lane)
+    key_ref[...] = key
+    code_ref[...] = jnp.where(
+        (key >= 0) & (lane < 2 * YQ), ((key >> 10) << 6) + (key & 63), -1
+    )
 
 
 def turn_kernel(x_ref, o_ref):
@@ -92,7 +94,16 @@
     return lax.dot_general(a, b, (dims, ((), ())), preferred_element_type=jnp.float32)
 
 
-def score_kernel(len_ref, code_ref, q_ref, p_ref, o_ref, plan, plan_s, onehot, best, sem):
+def score_kernel(
+    len_hbm, code_ref, q_hbm, p_hbm, o_ref,
+    len_ref, q_ref, p_ref, plan, plan_s, onehot, best, sem, len_sem, q_sem, p_sem,
+):
+    len_copy = pltpu.make_async_copy(len_hbm, len_ref, len_sem)
+    len_copy.start()
+    p_copy = pltpu.make_async_copy(p_hbm, p_ref, p_sem)
+    p_copy.start()
+    q_copy = pltpu.make_async_copy(q_hbm, q_ref, q_sem)
+    q_copy.start()
     code = jnp.full((Q, 128), -1, jnp.int32)
     lane8 = iota((Q, 128), 1)
     for y in range(Y):
@@ -161,6 +172,9 @@
     copy.start()
     best[...] = jnp.zeros((GMAX, GROUP * T), jnp.float32)
     copy.wait()
+    len_copy.wait()
+    p_copy.wait()
+    q_copy.wait()
 
     token = iota((PT, GROUP * T), 0)
 
@@ -195,76 +209,111 @@
         o_ref[Q * y : Q * (y + 1), :] = pltpu.roll(out, shift, 1) if shift else out
 
 
-def place_kernel(cand_ref, first_ref, x_ref, o_ref):
-    cand = cand_ref[...]
-    x = x_ref[...]
+def place_kernel(cand_ref, key_ref, x_ref, o_ref):
+    cand = jnp.concatenate([cand_ref[...], jnp.zeros((CL, 128 - QL), jnp.int32)], axis=1)
     lane = iota((1, 128), 1)
-    values = []
-    for k in range(2):
-        segs = []
+    turned = [cand] + [pltpu.roll(cand, 32 * i, 1) for i in range(1, 4)]
+    segs = []
+    for t in range(4):
+        seg = turned[0][4 * t : 4 * t + 1, :]
+        for i in range(1, 4):
+            seg = jnp.where(lane >> 5 == i, turned[i][4 * t + i : 4 * t + i + 1, :], seg)
+        segs.append(seg)
+    asked = jnp.concatenate(segs, axis=1)
+    place = iota((1, QL * CL), 1)
+    own_key = ((place & 31) << 10) + ((place >> 5) << 6) + (asked & 63)
+    owner = asked >> 6
+    lane_z = iota((Z, 128), 1)
+    x = jnp.where(lane_z < 2 * YQ, x_ref[...], 0.0)
+    key = jnp.where(lane_z < YQ, key_ref[...], 0)
+    key_high = pltpu.roll(key >> 8, 2 * YQ, 1).astype(jnp.float32)
+    key_low = pltpu.roll(key & 255, 3 * YQ, 1).astype(jnp.float32)
+    high, mid, low = split3(x)
+    high = jnp.where(
+        lane_z < 2 * YQ,
+        high.astype(jnp.float32),
+        jnp.where(lane_z < 3 * YQ, key_high, key_low),
+    ).astype(jnp.bfloat16)
+    tables = jnp.concatenate([high, mid, low], axis=1)
+    on_z = ((owner >> 5) == iota((Z, QL * CL), 0)).astype(jnp.float32).astype(jnp.bfloat16)
+    found = dot(tables, on_z, ((0,), (0,)))
+    on_yq = (owner & 31) == iota((YQ, QL * CL), 0)
+
+    def pick(rows):
+        return jnp.sum(jnp.where(on_yq, rows, 0.0), axis=0, keepdims=True)
+
+    score = found[0 : 2 * YQ] + found[128 : 128 + 2 * YQ] + found[256 : 256 + 2 * YQ]
+    first = pick(found[2 * YQ : 3 * YQ] * 256.0 + found[3 * YQ : 4 * YQ])
+    out = jnp.where(
+        first.astype(jnp.int32) == own_key, pick(score[0:YQ]), pick(score[YQ : 2 * YQ])
+    )
+    row = iota((CL, 128), 0)
+    res = jnp.zeros((CL, 128), jnp.float32)
+    for i in range(4):
         for t in range(4):
-            seg = jnp.zeros((1, 128), jnp.float32)
-            for j in range(4):
-                row = x[4 * t + j : 4 * t + j + 1, :]
-                shift = (32 * j - 32 * k) % 128
-                row = pltpu.roll(row, shift, 1) if shift else row
-                seg = jnp.where(lane >> 5 == j, row, seg)
-            segs.append(seg)
-        values.append(jnp.concatenate(segs, axis=1))
-    lane_owner = iota((CL, OWNERS), 1)
-    sub = iota((CL, 1), 0)
-    first = jnp.broadcast_to(first_ref[...], (CL, OWNERS))
-    value0 = jnp.broadcast_to(values[0], (CL, OWNERS))
-    value1 = jnp.broadcast_to(values[1], (CL, OWNERS))
-    out_lane = iota((CL, QL), 1)
-    out = jnp.zeros((CL, QL), jnp.float32)
-    for q in range(QL):
-        col = cand[:, q : q + 1]
-        key = (q << 10) + (sub << 6) + (col & 63)
-        value = jnp.where(first == key, value0, value1)
-        hit = jnp.where((col >> 6) == lane_owner, value, 0.0)
-        out = jnp.where(out_lane == q, jnp.sum(hit, axis=1, keepdims=True), out)
-    o_ref[...] = out
+            seg = jnp.broadcast_to(out[:, 128 * t : 128 * (t + 1)], (CL, 128))
+            seg = pltpu.roll(seg, 128 - 32 * i, 1) if i else seg
+            res = jnp.where(row == 4 * t + i, seg, res)
+    o_ref[...] = res[:, :QL]
+
+
+VMEM = pl.BlockSpec(memory_space=pltpu.VMEM)
 
 
 def small_call(kernel, out_shape, *args):
-    return pl.pallas_call(kernel, out_shape=out_shape)(*args)
+    return pl.pallas_call(
+        kernel,
+        out_shape=out_shape,
+        in_specs=[VMEM] * len(args),
+        out_specs=jax.tree.map(lambda _: VMEM, out_shape),
+    )(*[pltpu.with_memory_space_constraint(a, pltpu.VMEM) for a in args])
 
 
 def shards(queries, passages, lengths, candidates):
     every = lax.all_gather(queries, "query", axis=0, tiled=True)
     cand = candidates.T
-    table, first = small_call(
+    table, keys = small_call(
         request_kernel,
         (
-            jax.ShapeDtypeStruct((Z, 128), jnp.int32),
-            jax.ShapeDtypeStruct((1, OWNERS), jnp.int32),
+            pltpu.VMEM((Z, 128), jnp.int32),
+            pltpu.VMEM((Z, 128), jnp.int32),
         ),
         cand,
     )
     got = exchange(table, Z_GROUPS)
-    got = small_call(turn_kernel, jax.ShapeDtypeStruct((YQ, 128), jnp.int32), got)
+    got = small_call(turn_kernel, pltpu.VMEM((YQ, 128), jnp.int32), got)
     codes = exchange(got, YQ_GROUPS)
-    vmem = pl.BlockSpec(memory_space=pltpu.VMEM)
+    hbm = pl.BlockSpec(memory_space=pltpu.HBM)
     scores = pl.pallas_call(
         score_kernel,
         out_shape=jax.ShapeDtypeStruct((YQ, 128), jnp.float32),
-        in_specs=[pl.BlockSpec(memory_space=pltpu.SMEM), vmem, vmem, vmem],
-        out_specs=vmem,
+        in_specs=[hbm, VMEM, hbm, hbm],
+        out_specs=VMEM,
         scratch_shapes=[
+            pltpu.SMEM((BLK,), jnp.int32),
+            pltpu.VMEM((NQ, T, D), jnp.bfloat16),
+            pltpu.VMEM((BLK, PT, D), jnp.bfloat16),
             pltpu.VMEM((2 * GROUP, 256), jnp.int32),
             pltpu.SMEM((2 * GROUP, 256), jnp.int32),
             pltpu.VMEM((GMAX, Q * 128), jnp.bfloat16),
             pltpu.VMEM((GMAX, GROUP * T), jnp.float32),
             pltpu.SemaphoreType.DMA,
+            pltpu.SemaphoreType.DMA,
+            pltpu.SemaphoreType.DMA,
+            pltpu.SemaphoreType.DMA,
         ],
         compiler_params=pltpu.CompilerParams(vmem_limit_bytes=32 << 20),
-    )(lengths, codes, every, passages)
+    )(
+        pltpu.with_memory_space_constraint(lengths, pltpu.HBM),
+        pltpu.with_memory_space_constraint(codes, pltpu.VMEM),
+        pltpu.with_memory_space_constraint(every, pltpu.HBM),
+        pltpu.with_memory_space_constraint(passages, pltpu.HBM),
+    )
     back = exchange(scores, YQ_GROUPS)
-    back = small_call(back_kernel, jax.ShapeDtypeStruct((Z, 128), jnp.float32), back)
+    back = small_call(back_kernel, pltpu.VMEM((Z, 128), jnp.float32), back)
     back = exchange(back, Z_GROUPS)
     out = small_call(
-        place_kernel, jax.ShapeDtypeStruct((CL, QL), jnp.float32), cand, first, back
+        place_kernel, jax.ShapeDtypeStruct((CL, QL), jnp.float32), cand, keys, back
     )
     return out.T
 

time: 107 us -> 99.5 us (0.930)
  Pallas kernels: 15.1 us -> 8.07 us
  local copies, waits for them, and re-layouts: 3.84 us -> 0.7 us
  blocking collectives: 73.9 us -> 76.3 us
    pallas_call x4, Pallas kernels: 8.53 us -> 1.72 us  [small_call(): pl.pallas_call(kernel, out_shape=out_shape, in_specs=[VMEM] * len(args),...]
    unnamed x6 -> x4, local copies, waits for them, and re-layouts: 3.84 us -> 0.7 us
    all_to_all x4, blocking collectives: 73.9 us -> 76.3 us  [exchange(): lax.all_to_all(x, ('index', 'query'), split_axis=0, concat_axis=0, tiled=...]
  transfers between devices with their start and end apart: 1 -> 1, of which waited for: 0 -> 0; matrix products, arithmetic and copies ran while one was open for 0% -> 0% of each run, Pallas kernels for 3% -> 1%
where the time goes in v3:
time: 99.5 us; the launch traced here: 99.2 us
  blocking collectives  76.3 us (77%)
  between operations  13.4 us (13%)
  Pallas kernels  8.07 us (8%)
    all_to_all x4, blocking collectives, exchange(): lax.all_to_all(x, ('index', 'query'), split_axis=0, concat_axis=0, tiled=...  76.3 us
    pallas_call x1, Pallas kernels, shards(): pl.pallas_call(score_kernel, out_shape=jax.ShapeDtypeStruct((YQ, 128), jn...  6.35 us
  transfers between devices with their start and end apart: 1, of which 0 were waited for; matrix products, arithmetic and copies ran while one was open for 0% of the time, Pallas kernels for 1%

profile of v3, /device:TPU:1, one launch (start us, length us, event | category | flops | bytes accessed | tf_op | source)
XLA Modules:
  0.0 99.2 jit_solution(13039101514218679771)
XLA Ops:
  6.5 0.0 all-gather.2.cloned.1.call-start
  6.5 0.7 all-gather.2.cloned.1.call-update
  7.3 0.0 copy-start
  7.3 0.7 copy-done
  8.0 0.5 shard_map.46
  8.4 26.8 %all_to_all.44 = s32[16,1,128]{2,1,0:T(1,128)S(1)} all-to-all(s32[16,1,128]{2,1,0:T(1,128)S(1)} %bitcast.27), channel_id=1, replica_groups={{0,32,64,96,128,160,192,224,256,288,320,352,384,416,448,480},{1,33,65,9..., dimensions={0} | all-to-all | bytes 16384 | tf_op jit(solution)/shard_map/all_to_all | solution.py:29
  35.3 0.2 shard_map.47
  35.4 15.9 %all_to_all.45 = s32[32,1,128]{2,1,0:T(1,128)S(1)} all-to-all(s32[32,1,128]{2,1,0:T(1,128)S(1)} %bitcast.20), channel_id=1, replica_groups={{0,1,2,3,4,5,6,7,8,9,10,11,12,13,14,15,16,17,18,19,20,21,22,23,24,25,26..., dimensions={0} | all-to-all | bytes 32768 | tf_op jit(solution)/shard_map/all_to_all | solution.py:29
  51.3 0.0 all-gather.2.cloned.1.call-done.q_hbm
  51.3 0.0 copy-start.1
  51.3 6.4 %shard_map.48 = f32[32,128]{1,0:T(8,128)S(1)} custom-call(s32[64]{0:T(128)} %len_hbm.1, s32[32,128]{1,0:T(8,128)S(1)} %bitcast.18, bf16[256,32,128]{2,1,0:T(8,128)(2,1)} %all-gather.2.cloned.1.call-done.q_hbm, bf16[64,128,128]{2,1,0:T(8,128)(2,1)} %p_hbm.1), custom_call_target="tpu_custom_call" | custom-call | tf_op jit(solution)/shard_map/pallas_call | solution.py:287
  57.7 11.0 %all_to_all.46 = f32[32,1,128]{2,1,0:T(1,128)S(1)} all-to-all(f32[32,1,128]{2,1,0:T(1,128)S(1)} %bitcast.19), channel_id=1, replica_groups={{0,1,2,3,4,5,6,7,8,9,10,11,12,13,14,15,16,17,18,19,20,21,22,23,24,25,26..., dimensions={0} | all-to-all | bytes 32768 | tf_op jit(solution)/shard_map/all_to_all | solution.py:29
  68.6 0.1 shard_map.49
  68.7 22.6 %all_to_all.47 = f32[16,1,128]{2,1,0:T(1,128)S(1)} all-to-all(f32[16,1,128]{2,1,0:T(1,128)S(1)} %bitcast.23), channel_id=1, replica_groups={{0,32,64,96,128,160,192,224,256,288,320,352,384,416,448,480},{1,33,65,9..., dimensions={0} | all-to-all | bytes 16384 | tf_op jit(solution)/shard_map/all_to_all | solution.py:29
  91.3 0.0 copy-done.1
  91.3 1.0 %shard_map.50 = f32[16,32]{1,0:T(8,128)} custom-call(s32[16,32]{1,0:T(8,128)S(1)} %bitcast.25, s32[16,128]{1,0:T(8,128)S(1)} %get-tuple-element.7.key_ref, f32[16,128]{1,0:T(8,128)S(1)} %bitcast.26), custom_call_target="tpu_custom_call" | custom-call | tf_op jit(solution)/shard_map/pallas_call | solution.py:264
Async XLA Ops:
  6.5 44.8 %all-gather.2.cloned.1.call-start = ((), (), s32[]{:S(2)}) async-start(), calls=%async_computation.4 | async-start | bytes 2359296 | tf_op jit(solution)/shard_map/all_gather | solution.py:273
  7.3 0.7 copy-start
  51.3 40.0 %copy-start.1 = (s32[32,16]{0,1:T(8,128)S(1)}, s32[32,16]{0,1:T(8,128)}, u32[]{:S(2)}) copy-start(s32[32,16]{0,1:T(8,128)} %param.7) | copy-start | bytes 6148
Sparse Core Ops, SparseCore 0:
  9.5 38.5 all-gather.1

commit v4 on v3

--- a/solution.py
+++ b/solution.py
@@ -95,15 +95,18 @@
 
 
 def score_kernel(
-    len_hbm, code_ref, q_hbm, p_hbm, o_ref,
-    len_ref, q_ref, p_ref, plan, plan_s, onehot, best, sem, len_sem, q_sem, p_sem,
+    len_hbm, code_ref, same_ref, other_ref, p_hbm, o_ref,
+    len_ref, q_ref, p_ref, plan, plan_s, onehot, best, sem, len_sem, same_sem, other_sem, p_sem,
 ):
     len_copy = pltpu.make_async_copy(len_hbm, len_ref, len_sem)
     len_copy.start()
     p_copy = pltpu.make_async_copy(p_hbm, p_ref, p_sem)
     p_copy.start()
-    q_copy = pltpu.make_async_copy(q_hbm, q_ref, q_sem)
-    q_copy.start()
+    half = NQ // 2
+    same_copy = pltpu.make_async_copy(same_ref, q_ref.at[pl.ds(0, half)], same_sem)
+    same_copy.start()
+    other_copy = pltpu.make_async_copy(other_ref, q_ref.at[pl.ds(half, half)], other_sem)
+    other_copy.start()
     code = jnp.full((Q, 128), -1, jnp.int32)
     lane8 = iota((Q, 128), 1)
     for y in range(Y):
@@ -112,7 +115,10 @@
         code = jnp.where(lane8 >> 5 == y, part, code)
     valid = code >= 0
     block = jnp.where(valid, code & 63, BLK)
-    query = jnp.where(valid, (code >> 6) + QL * iota((Q, 128), 0), 0)
+    me = lax.axis_index("query")
+    source = iota((Q, 128), 0)
+    piece = (((source ^ me) & 1) << 2) + (((me >> 1) - (source >> 1)) & 3)
+    query = jnp.where(valid, (code >> 6) + QL * piece, 0)
 
     b_iota = iota((BLK, 128), 0)
     hits = [block[q : q + 1, :] == b_iota for q in range(Q)]
@@ -174,7 +180,8 @@
     copy.wait()
     len_copy.wait()
     p_copy.wait()
-    q_copy.wait()
+    same_copy.wait()
+    other_copy.wait()
 
     token = iota((PT, GROUP * T), 0)
 
@@ -270,7 +277,10 @@
 
 
 def shards(queries, passages, lengths, candidates):
-    every = lax.all_gather(queries, "query", axis=0, tiled=True)
+    same = [queries] + [
+        lax.ppermute(queries, "query", [(k, (k + 2 * d) % Q) for k in range(Q)])
+        for d in range(1, Q // 2)
+    ]
     cand = candidates.T
     table, keys = small_call(
         request_kernel,
@@ -281,13 +291,16 @@
         cand,
     )
     got = exchange(table, Z_GROUPS)
+    same = jnp.concatenate(same, axis=0)
+    got, same = lax.optimization_barrier((got, same))
+    other = lax.ppermute(same, "query", [(k, k ^ 1) for k in range(Q)])
     got = small_call(turn_kernel, pltpu.VMEM((YQ, 128), jnp.int32), got)
     codes = exchange(got, YQ_GROUPS)
     hbm = pl.BlockSpec(memory_space=pltpu.HBM)
     scores = pl.pallas_call(
         score_kernel,
         out_shape=jax.ShapeDtypeStruct((YQ, 128), jnp.float32),
-        in_specs=[hbm, VMEM, hbm, hbm],
+        in_specs=[hbm, VMEM, VMEM, VMEM, hbm],
         out_specs=VMEM,
         scratch_shapes=[
             pltpu.SMEM((BLK,), jnp.int32),
@@ -301,12 +314,14 @@
             pltpu.SemaphoreType.DMA,
             pltpu.SemaphoreType.DMA,
             pltpu.SemaphoreType.DMA,
+            pltpu.SemaphoreType.DMA,
         ],
         compiler_params=pltpu.CompilerParams(vmem_limit_bytes=32 << 20),
     )(
         pltpu.with_memory_space_constraint(lengths, pltpu.HBM),
         pltpu.with_memory_space_constraint(codes, pltpu.VMEM),
-        pltpu.with_memory_space_constraint(every, pltpu.HBM),
+        pltpu.with_memory_space_constraint(same, pltpu.VMEM),
+        pltpu.with_memory_space_constraint(other, pltpu.VMEM),
         pltpu.with_memory_space_constraint(passages, pltpu.HBM),
     )
     back = exchange(scores, YQ_GROUPS)

time: 99.5 us -> 88.4 us (0.89)
  blocking collectives: 76.3 us -> 36.1 us
  starting transfers between devices: 0.01 us -> 31.7 us
  between operations: 13.4 us -> 0.1 us
  waiting for transfers between devices: 0.71 us -> 10.1 us
  other arithmetic: 0 us -> 1.09 us
    all_to_all x4 -> x3, blocking collectives: 76.3 us -> 36.1 us  [exchange(): lax.all_to_all(x, ('index', 'query'), split_axis=0, concat_axis=0, tiled=...]
    ppermute x0 -> x4, starting transfers between devices: none -> 16.8 us  [the longest x3 12 us: shards(): lax.ppermute(queries, 'query', [(k, (k + 2 * d) % Q) for k in range(Q)])]
    all_to_all x0 -> x1, starting transfers between devices: none -> 14.9 us  [exchange(): lax.all_to_all(x, ('index', 'query'), split_axis=0, concat_axis=0, tiled=...]
    all_to_all x0 -> x1, waiting for transfers between devices: none -> 10.1 us  [exchange(): lax.all_to_all(x, ('index', 'query'), split_axis=0, concat_axis=0, tiled=...]
    concatenate x0 -> x1, other arithmetic: none -> 1.09 us  [shards(): same = jnp.concatenate(same, axis=0)]
  transfers between devices with their start and end apart: 1 -> 5, of which waited for: 0 -> 1; matrix products, arithmetic and copies ran while one was open for 0% -> 1% of each run, Pallas kernels for 1% -> 1%
where the time goes in v4:
time: 88.4 us; the launch traced here: 87.9 us
  blocking collectives  36.1 us (41%)
  starting transfers between devices  31.7 us (36%)
  waiting for transfers between devices  10.1 us (11%)
  Pallas kernels  8.15 us (9%)
  other arithmetic  1.09 us (1%)
    all_to_all x3, blocking collectives, exchange(): lax.all_to_all(x, ('index', 'query'), split_axis=0, concat_axis=0, tiled=...  36.1 us
    all_to_all x1, starting transfers between devices, exchange(): lax.all_to_all(x, ('index', 'query'), split_axis=0, concat_axis=0, tiled=...  14.9 us
    ppermute x3, starting transfers between devices, shards(): lax.ppermute(queries, 'query', [(k, (k + 2 * d) % Q) for k in range(Q)])  12 us
    all_to_all x1, waiting for transfers between devices, exchange(): lax.all_to_all(x, ('index', 'query'), split_axis=0, concat_axis=0, tiled=...  10.1 us
    pallas_call x1, Pallas kernels, shards(): pl.pallas_call(score_kernel, out_shape=jax.ShapeDtypeStruct((YQ, 128), jn...  5.9 us
    ppermute x1, starting transfers between devices, shards(): other = lax.ppermute(same, 'query', [(k, k ^ 1) for k in range(Q)])  4.84 us
    pallas_call x4, Pallas kernels, small_call(): pl.pallas_call(kernel, out_shape=out_shape, in_specs=[VMEM] * len(args),...  2.25 us
  transfers between devices with their start and end apart: 5, of which 1 were waited for; matrix products, arithmetic and copies ran while one was open for 1% of the time, Pallas kernels for 1%

profile of v4, /device:TPU:1, one launch (start us, length us, event | category | flops | bytes accessed | tf_op | source)
XLA Modules:
  0.0 87.9 jit_solution(3589580567096323409)
XLA Ops:
  0.0 5.5 %collective-permute-start.1 = (bf16[32,32,128]{2,1,0:T(8,128)(2,1)}, bf16[32,32,128]{2,1,0:T(8,128)(2,1)S(1)}, u32[]{:S(2)}, u32[]{:S(2)}) collective-permute-start(bf16[32,32,128]{2,1,0:T(8,128)(2,1)} %param.4), channel_id=1, source_target_pairs={{0,4},{1,5},{2,6},{3,7},{4,0},{5,1},{6,2},{7,3},{8,12},{9,13},{10,... | collective-permute-start | bytes 786440 | tf_op jit(solution)/shard_map/ppermute | solution.py:281
  5.5 2.2 %collective-permute-start = (bf16[32,32,128]{2,1,0:T(8,128)(2,1)}, bf16[32,32,128]{2,1,0:T(8,128)(2,1)S(1)}, u32[]{:S(2)}, u32[]{:S(2)}) collective-permute-start(bf16[32,32,128]{2,1,0:T(8,128)(2,1)} %param.4), channel_id=1, source_target_pairs={{0,2},{1,3},{2,4},{3,5},{4,6},{5,7},{6,0},{7,1},{8,10},{9,11},{10,... | collective-permute-start | bytes 786440 | tf_op jit(solution)/shard_map/ppermute | solution.py:281
  7.7 4.3 %collective-permute-start.2 = (bf16[32,32,128]{2,1,0:T(8,128)(2,1)}, bf16[32,32,128]{2,1,0:T(8,128)(2,1)S(1)}, u32[]{:S(2)}, u32[]{:S(2)}) collective-permute-start(bf16[32,32,128]{2,1,0:T(8,128)(2,1)} %param.4), channel_id=1, source_target_pairs={{0,6},{1,7},{2,0},{3,1},{4,2},{5,3},{6,4},{7,5},{8,14},{9,15},{10,... | collective-permute-start | bytes 786440 | tf_op jit(solution)/shard_map/ppermute | solution.py:281
  12.0 0.0 copy-start
  12.0 0.7 copy-done
  12.7 1.1 %shard_map.46 = (s32[16,128]{1,0:T(8,128)}, s32[16,128]{1,0:T(8,128)S(1)}) custom-call(s32[16,32]{1,0:T(8,128)S(1)} %bitcast.24), custom_call_target="tpu_custom_call" | custom-call | tf_op jit(solution)/shard_map/pallas_call | solution.py:271
  13.7 14.9 %all-to-all-start = ((s32[16,1,128]{2,1,0:T(1,128)}), s32[16,1,128]{2,1,0:T(1,128)S(1)}, u32[]{:S(2)}, u32[]{:S(2)}) async-start(s32[16,1,128]{2,1,0:T(1,128)} %bitcast.2), calls=%async_computation | async-start | bytes 16384 | tf_op jit(solution)/shard_map/all_to_all | solution.py:29
  28.7 0.0 collective-permute-done.1
  28.7 0.0 collective-permute-done
  28.7 0.0 collective-permute-done.2
  28.7 1.1 %pad_maximum_fusion.same_ref = bf16[128,32,128]{2,1,0:T(8,128)(2,1)S(1)} fusion(bf16[32,32,128]{2,1,0:T(8,128)(2,1)S(1)} %collective-permute-done.2, bf16[32,32,128]{2,1,0:T(8,128)(2,1)S(1)} %collective-permute-done.1, bf16[32,32,128]{2,1,0:T(8,128)(2,1)S(1)} %collective-permute-done, bf16[32,32,128]{2,1,0:T(8,128)(2,1)} %param.4), kind=kLoop, calls=%fused_computation | loop fusion | flops 1572864 | bytes 2097152 | tf_op jit(solution)/shard_map/concatenate | solution.py:294
  29.8 10.1 %all-to-all-done = s32[16,1,128]{2,1,0:T(1,128)S(1)} async-done(((s32[16,1,128]{2,1,0:T(1,128)}), s32[16,1,128]{2,1,0:T(1,128)S(1)}, u32[]{:S(2)}, u32[]{:S(2)}) %all-to-all-start) | async-done | bytes 8224 | tf_op jit(solution)/shard_map/all_to_all | solution.py:29
  39.9 4.8 %collective-permute-start.3 = (bf16[128,32,128]{2,1,0:T(8,128)(2,1)S(1)}, bf16[128,32,128]{2,1,0:T(8,128)(2,1)S(1)}, u32[]{:S(2)}, u32[]{:S(2)}) collective-permute-start(bf16[128,32,128]{2,1,0:T(8,128)(2,1)S(1)} %pad_maximum_fusion.same_ref), channel_id=1, source_target_pairs={{0,1},{1,0},{2,3},{3,2},{4,5},{5,4},{6,7},{7,6},{8,9},{9,8},{10,11... | collective-permute-start | bytes 3145736 | tf_op jit(solution)/shard_map/ppermute | solution.py:296
  44.7 0.1 shard_map.47
  44.8 11.5 %all_to_all.45 = s32[32,1,128]{2,1,0:T(1,128)S(1)} all-to-all(s32[32,1,128]{2,1,0:T(1,128)S(1)} %bitcast.20), channel_id=1, replica_groups={{0,1,2,3,4,5,6,7,8,9,10,11,12,13,14,15,16,17,18,19,20,21,22,23,24,25,26..., dimensions={0} | all-to-all | bytes 32768 | tf_op jit(solution)/shard_map/all_to_all | solution.py:29
  56.4 0.0 collective-permute-done.3.other_ref
  56.4 0.0 copy-start.1
  56.4 5.9 %shard_map.48 = f32[32,128]{1,0:T(8,128)S(1)} custom-call(s32[64]{0:T(128)} %len_hbm.1, s32[32,128]{1,0:T(8,128)S(1)} %bitcast.18, bf16[128,32,128]{2,1,0:T(8,128)(2,1)S(1)} %pad_maximum_fusion.same_ref, bf16[128,32,128]{2,1,0:T(8,128)(2,1)S(1)} %collective-permute-done.3.other_ref, bf16[64,128,128]{2,1,0:T(8,128)(2,1)} %p_hbm.1), custom_call_target="tpu_custom_call" | custom-call | tf_op jit(solution)/shard_map/pallas_call | solution.py:300
  62.3 10.7 %all_to_all.46 = f32[32,1,128]{2,1,0:T(1,128)S(1)} all-to-all(f32[32,1,128]{2,1,0:T(1,128)S(1)} %bitcast.19), channel_id=1, replica_groups={{0,1,2,3,4,5,6,7,8,9,10,11,12,13,14,15,16,17,18,19,20,21,22,23,24,25,26..., dimensions={0} | all-to-all | bytes 32768 | tf_op jit(solution)/shard_map/all_to_all | solution.py:29
  73.0 0.1 shard_map.49
  73.0 13.9 %all_to_all.47 = f32[16,1,128]{2,1,0:T(1,128)S(1)} all-to-all(f32[16,1,128]{2,1,0:T(1,128)S(1)} %bitcast.23), channel_id=1, replica_groups={{0,32,64,96,128,160,192,224,256,288,320,352,384,416,448,480},{1,33,65,9..., dimensions={0} | all-to-all | bytes 16384 | tf_op jit(solution)/shard_map/all_to_all | solution.py:29
  86.9 0.0 copy-done.1
  86.9 1.0 %shard_map.50 = f32[16,32]{1,0:T(8,128)} custom-call(s32[16,32]{1,0:T(8,128)S(1)} %bitcast.25, s32[16,128]{1,0:T(8,128)S(1)} %get-tuple-element.9.key_ref, f32[16,128]{1,0:T(8,128)S(1)} %bitcast.26), custom_call_target="tpu_custom_call" | custom-call | tf_op jit(solution)/shard_map/pallas_call | solution.py:271
Async XLA Ops:
  0.0 28.7 %collective-permute-start.1 = (bf16[32,32,128]{2,1,0:T(8,128)(2,1)}, bf16[32,32,128]{2,1,0:T(8,128)(2,1)S(1)}, u32[]{:S(2)}, u32[]{:S(2)}) collective-permute-start(bf16[32,32,128]{2,1,0:T(8,128)(2,1)} %param.4), channel_id=1, source_target_pairs={{0,4},{1,5},{2,6},{3,7},{4,0},{5,1},{6,2},{7,3},{8,12},{9,13},{10,... | collective-permute-start | bytes 786440 | tf_op jit(solution)/shard_map/ppermute | solution.py:281
  5.5 23.2 %collective-permute-start = (bf16[32,32,128]{2,1,0:T(8,128)(2,1)}, bf16[32,32,128]{2,1,0:T(8,128)(2,1)S(1)}, u32[]{:S(2)}, u32[]{:S(2)}) collective-permute-start(bf16[32,32,128]{2,1,0:T(8,128)(2,1)} %param.4), channel_id=1, source_target_pairs={{0,2},{1,3},{2,4},{3,5},{4,6},{5,7},{6,0},{7,1},{8,10},{9,11},{10,... | collective-permute-start | bytes 786440 | tf_op jit(solution)/shard_map/ppermute | solution.py:281
  7.7 21.0 %collective-permute-start.2 = (bf16[32,32,128]{2,1,0:T(8,128)(2,1)}, bf16[32,32,128]{2,1,0:T(8,128)(2,1)S(1)}, u32[]{:S(2)}, u32[]{:S(2)}) collective-permute-start(bf16[32,32,128]{2,1,0:T(8,128)(2,1)} %param.4), channel_id=1, source_target_pairs={{0,6},{1,7},{2,0},{3,1},{4,2},{5,3},{6,4},{7,5},{8,14},{9,15},{10,... | collective-permute-start | bytes 786440 | tf_op jit(solution)/shard_map/ppermute | solution.py:281
  12.0 0.7 copy-start
  13.7 26.1 %all-to-all-start = ((s32[16,1,128]{2,1,0:T(1,128)}), s32[16,1,128]{2,1,0:T(1,128)S(1)}, u32[]{:S(2)}, u32[]{:S(2)}) async-start(s32[16,1,128]{2,1,0:T(1,128)} %bitcast.2), calls=%async_computation | async-start | bytes 16384 | tf_op jit(solution)/shard_map/all_to_all | solution.py:29
  39.9 16.5 %collective-permute-start.3 = (bf16[128,32,128]{2,1,0:T(8,128)(2,1)S(1)}, bf16[128,32,128]{2,1,0:T(8,128)(2,1)S(1)}, u32[]{:S(2)}, u32[]{:S(2)}) collective-permute-start(bf16[128,32,128]{2,1,0:T(8,128)(2,1)S(1)} %pad_maximum_fusion.same_ref), channel_id=1, source_target_pairs={{0,1},{1,0},{2,3},{3,2},{4,5},{5,4},{6,7},{7,6},{8,9},{9,8},{10,11... | collective-permute-start | bytes 3145736 | tf_op jit(solution)/shard_map/ppermute | solution.py:296
  56.4 30.5 %copy-start.1 = (s32[32,16]{0,1:T(8,128)S(1)}, s32[32,16]{0,1:T(8,128)}, u32[]{:S(2)}) copy-start(s32[32,16]{0,1:T(8,128)} %param.7) | copy-start | bytes 6148

commit v5 on v3

v5 whole, which is shorter than its diff:
```python
import jax
import jax.numpy as jnp
from jax import lax
from jax.experimental import pallas as pl
from jax.experimental.pallas import tpu as pltpu
from jax.sharding import PartitionSpec as P

Z, Y, X, C = 16, 4, 4, 2
YX = Y * X
PLANE = YX * C
OWNERS = Z * PLANE
BLK = 64
BLOCKS = C * BLK
QL, CL = 32, 16
T, D, PT = 32, 128, 128
GROUP = 8
GMAX = 240
UNROLL = 8
BIG = 1 << 30

Z_GROUPS = [[r + PLANE * z for z in range(Z)] for r in range(PLANE)]
YX_GROUPS = [[PLANE * z + C * r + c for r in range(YX)] for z in range(Z) for c in range(C)]


def iota(shape, axis):
    return lax.broadcasted_iota(jnp.int32, shape, axis)


def exchange(x, groups):
    return lax.all_to_all(
        x, ("index", "query"), split_axis=0, concat_axis=0, tiled=True,
        axis_index_groups=groups,
    )


def place_of(cand):
    owner = cand >> 6
    return (owner & ~(PLANE - 1)) + ((owner & 1) << 4) + ((owner >> 1) & (YX - 1))


def spread(rows, row, lane):
    out = jnp.zeros((Z, 128), jnp.int32)
    for k, slot in enumerate(rows):
        for j in range(4):
            shift = (32 * k - 32 * j) % 128
            for t in range(4):
                seg = jnp.broadcast_to(slot[:, 128 * t : 128 * (t + 1)], (Z, 128))
                seg = pltpu.roll(seg, shift, 1) if shift else seg
                out = jnp.where((row == 4 * t + j) & (lane >> 5 == k), seg, out)
    return out


def request_kernel(cand_ref, code_ref, key_ref):
    cand = cand_ref[...]
    owners = place_of(cand)
    keys = (iota((CL, QL), 1) << 10) + (iota((CL, QL), 0) << 6) + (cand & 63)
    lane_owner = iota((CL, OWNERS), 1)
    low = jnp.full((CL, OWNERS), BIG, jnp.int32)
    high = jnp.full((CL, OWNERS), -1, jnp.int32)
    for q in range(QL):
        key = keys[:, q : q + 1]
        match = owners[:, q : q + 1] == lane_owner
        low = jnp.minimum(low, jnp.where(match, key, BIG))
        high = jnp.maximum(high, jnp.where(match, key, -1))
    last = jnp.max(high, axis=0, keepdims=True)
    first = jnp.where(last >= 0, jnp.min(low, axis=0, keepdims=True), -1)
    last = jnp.where(last != first, last, -1)
    row = iota((Z, 128), 0)
    lane = iota((Z, 128), 1)
    key = spread((first, last), row, lane)
    key_ref[...] = key
    code_ref[...] = jnp.where(
        (key >= 0) & (lane < 2 * PLANE), ((key >> 10) << 6) + (key & 63), -1
    )


def turn_kernel(x_ref, o_ref):
    x = x_ref[...]
    xt = jnp.transpose(jnp.concatenate([x, jnp.zeros((112, 128), x.dtype)], axis=0))
    lane = iota((16, 128), 1)
    out = xt[0:16]
    for m in range(1, 4):
        out = jnp.where(lane >> 4 == m, pltpu.roll(xt[16 * m : 16 * (m + 1)], 16 * m, 1), out)
    o_ref[...] = out


def split3(x):
    hi = x.astype(jnp.bfloat16)
    rest = x - hi.astype(jnp.float32)
    mid = rest.astype(jnp.bfloat16)
    low = (rest - mid.astype(jnp.float32)).astype(jnp.bfloat16)
    return hi, mid, low


def dot(a, b, dims):
    return lax.dot_general(a, b, (dims, ((), ())), preferred_element_type=jnp.float32)


def score_kernel(
    len_hbm, mate_len_hbm, code_ref, q0_hbm, q1_ref, q2_ref, q3_ref, p_hbm, mate_ref, o_ref,
    len_ref, q_ref, p_ref, plan, plan_s, onehot, best, sem, sems,
):
    moves = [(p_hbm, p_ref.at[pl.ds(0, BLK)]), (mate_ref, p_ref.at[pl.ds(BLK, BLK)])]
    for d, ref in enumerate((q0_hbm, q1_ref, q2_ref, q3_ref)):
        moves.append((ref, q_ref.at[pl.ds(QL * d, QL)]))
    moves += [(len_hbm, len_ref.at[0]), (mate_len_hbm, len_ref.at[1])]
    moves = [pltpu.make_async_copy(a, b, sems.at[i]) for i, (a, b) in enumerate(moves)]
    for move in moves:
        move.start()
    lane8 = iota((8, 128), 1)
    code = jnp.where(lane8 < 64, code_ref[0:8, :], pltpu.roll(code_ref[8:16, :], 64, 1))
    valid = code >= 0
    me = lax.axis_index("query")
    other = ((lane8 >> 4) ^ me) & 1
    block = jnp.where(valid, (other << 6) + (code & 63), BLOCKS)
    piece = ((me >> 1) - iota((8, 128), 0)) & (X - 1)
    query = jnp.where(valid, (code >> 6) + QL * piece, 0)

    b_iota = iota((BLOCKS, 128), 0)
    hits = [block[q : q + 1, :] == b_iota for q in range(8)]
    hit = jnp.concatenate([h.astype(jnp.float32) for h in hits], axis=0).astype(jnp.bfloat16)
    r_i, c_i = iota((128, 128), 0), iota((128, 128), 1)
    earlier = jnp.concatenate(
        [(r_i < c_i).astype(jnp.float32), jnp.ones((128, 128), jnp.float32)], axis=1
    ).astype(jnp.bfloat16)
    sums = dot(hit, earlier, ((1,), (0,)))
    base = jnp.zeros((BLOCKS, 128), jnp.float32)
    bases = []
    for q in range(8):
        bases.append(base + sums[BLOCKS * q : BLOCKS * (q + 1), :128])
        base = base + sums[BLOCKS * q : BLOCKS * (q + 1), 128:]
    groups = ((base.astype(jnp.int32) + (GROUP - 1)) >> 3).astype(jnp.float32)
    l_i, m_i = iota((BLOCKS, BLOCKS), 0), iota((BLOCKS, BLOCKS), 1)
    before = dot(
        (m_i < l_i).astype(jnp.float32).astype(jnp.bfloat16),
        groups.astype(jnp.bfloat16),
        ((1,), (0,)),
    )
    ends = (before + groups).astype(jnp.int32)
    dest = jnp.concatenate(
        [
            jnp.sum(jnp.where(hits[q], GROUP * before + bases[q], 0.0), axis=0, keepdims=True)
            for q in range(8)
        ],
        axis=0,
    ).astype(jnp.int32)

    g_iota = iota((GMAX, 128), 0)
    c_iota = iota((GROUP, 128), 0)
    named = []
    for q in range(8):
        d = dest[q : q + 1, :]
        onehot[:, 128 * q : 128 * (q + 1)] = (
            ((d >> 3) == g_iota).astype(jnp.float32).astype(jnp.bfloat16)
        )
        here = ((d & 7) == c_iota) & valid[q : q + 1, :]
        named.append(jnp.where(here, query[q : q + 1, :], 0).astype(jnp.float32))
    lists = dot(
        jnp.concatenate(named, axis=1).astype(jnp.bfloat16), onehot[...], ((1,), (1,))
    )
    plan[0:GROUP, 0:GMAX] = lists.astype(jnp.int32)
    g_lane = iota((BLOCKS, 256), 1)
    ends2 = jnp.concatenate([ends, ends], axis=1)
    owner_block = jnp.minimum(
        jnp.sum((ends2 <= g_lane).astype(jnp.int32), axis=0, keepdims=True), BLOCKS - 1
    )
    total = jnp.broadcast_to(ends2[BLOCKS - 1 : BLOCKS, :], (1, 256))
    plan[GROUP : 2 * GROUP, :] = jnp.where(
        iota((GROUP, 256), 0) == 0,
        jnp.broadcast_to(owner_block, (GROUP, 256)),
        jnp.broadcast_to(total, (GROUP, 256)),
    )
    copy = pltpu.make_async_copy(plan, plan_s, sem)
    copy.start()
    best[...] = jnp.zeros((GMAX, GROUP * T), jnp.float32)
    copy.wait()
    for move in moves:
        move.wait()

    token = iota((PT, GROUP * T), 0)

    def step(it, carry):
        rows = []
        for u in range(UNROLL):
            g = it * UNROLL + u
            b = plan_s[GROUP, g]
            rows_q = jnp.concatenate([q_ref[plan_s[c, g]] for c in range(GROUP)], axis=0)
            similar = dot(p_ref[b], rows_q, ((1,), (1,)))
            similar = jnp.where(token < len_ref[b >> 6, b & 63], similar, -jnp.inf)
            rows.append(jnp.max(similar, axis=0, keepdims=True))
        best[pl.ds(pl.multiple_of(it * UNROLL, UNROLL), UNROLL), :] = jnp.concatenate(rows, axis=0)
        return carry

    lax.fori_loop(0, (plan_s[GROUP + 1, 0] + (UNROLL - 1)) // UNROLL, step, 0)

    w = (iota((GROUP, GROUP * T), 0) == (iota((GROUP, GROUP * T), 1) >> 5)).astype(jnp.float32)
    w = w.astype(jnp.bfloat16)
    means = sum(dot(w, part, ((1,), (1,))) for part in split3(best[...])) * (1.0 / T)
    picked = dot(jnp.concatenate(split3(means), axis=0), onehot[...], ((1,), (0,)))
    picked = picked[0:GROUP] + picked[GROUP : 2 * GROUP] + picked[2 * GROUP : 3 * GROUP]
    out = []
    for q in range(8):
        here = (dest[q : q + 1, :] & 7) == c_iota
        out.append(
            jnp.sum(jnp.where(here, picked[:, 128 * q : 128 * (q + 1)], 0.0), axis=0, keepdims=True)
        )
    out = jnp.concatenate(out, axis=0)
    o_ref[0:8, :] = out
    o_ref[8:16, :] = pltpu.roll(out, 64, 1)


def place_kernel(cand_ref, key_ref, x_ref, o_ref):
    cand = jnp.concatenate([cand_ref[...], jnp.zeros((CL, 128 - QL), jnp.int32)], axis=1)
    lane = iota((1, 128), 1)
    turned = [cand] + [pltpu.roll(cand, 32 * i, 1) for i in range(1, 4)]
    segs = []
    for t in range(4):
        seg = turned[0][4 * t : 4 * t + 1, :]
        for i in range(1, 4):
            seg = jnp.where(lane >> 5 == i, turned[i][4 * t + i : 4 * t + i + 1, :], seg)
        segs.append(seg)
    asked = jnp.concatenate(segs, axis=1)
    place = iota((1, QL * CL), 1)
    own_key = ((place & 31) << 10) + ((place >> 5) << 6) + (asked & 63)
    owner = place_of(asked)
    lane_z = iota((Z, 128), 1)
    x = jnp.where(lane_z < 2 * PLANE, x_ref[...], 0.0)
    key = jnp.where(lane_z < PLANE, key_ref[...], 0)
    key_high = pltpu.roll(key >> 8, 2 * PLANE, 1).astype(jnp.float32)
    key_low = pltpu.roll(key & 255, 3 * PLANE, 1).astype(jnp.float32)
    high, mid, low = split3(x)
    high = jnp.where(
        lane_z < 2 * PLANE,
        high.astype(jnp.float32),
        jnp.where(lane_z < 3 * PLANE, key_high, key_low),
    ).astype(jnp.bfloat16)
    tables = jnp.concatenate([high, mid, low], axis=1)
    on_z = ((owner >> 5) == iota((Z, QL * CL), 0)).astype(jnp.float32).astype(jnp.bfloat16)
    found = dot(tables, on_z, ((0,), (0,)))
    on_plane = (owner & 31) == iota((PLANE, QL * CL), 0)

    def pick(rows):
        return jnp.sum(jnp.where(on_plane, rows, 0.0), axis=0, keepdims=True)

    score = found[0 : 2 * PLANE] + found[128 : 128 + 2 * PLANE] + found[256 : 256 + 2 * PLANE]
    first = pick(found[2 * PLANE : 3 * PLANE] * 256.0 + found[3 * PLANE : 4 * PLANE])
    out = jnp.where(
        first.astype(jnp.int32) == own_key, pick(score[0:PLANE]), pick(score[PLANE : 2 * PLANE])
    )
    row = iota((CL, 128), 0)
    res = jnp.zeros((CL, 128), jnp.float32)
    for i in range(4):
        for t in range(4):
            seg = jnp.broadcast_to(out[:, 128 * t : 128 * (t + 1)], (CL, 128))
            seg = pltpu.roll(seg, 128 - 32 * i, 1) if i else seg
            res = jnp.where(row == 4 * t + i, seg, res)
    o_ref[...] = res[:, :QL]


VMEM = pl.BlockSpec(memory_space=pltpu.VMEM)


def small_call(kernel, out_shape, *args):
    return pl.pallas_call(
        kernel,
        out_shape=out_shape,
        in_specs=[VMEM] * len(args),
        out_specs=jax.tree.map(lambda _: VMEM, out_shape),
    )(*[pltpu.with_memory_space_constraint(a, pltpu.VMEM) for a in args])


def shards(queries, passages, lengths, candidates):
    same = [queries] + [
        lax.ppermute(queries, "query", [(k, (k + C * d) % (X * C)) for k in range(X * C)])
        for d in range(1, X)
    ]
    cand = candidates.T
    table, keys = small_call(
        request_kernel,
        (pltpu.VMEM((Z, 128), jnp.int32), pltpu.VMEM((Z, 128), jnp.int32)),
        cand,
    )
    mates = [(k, k ^ 1) for k in range(X * C)]
    mate = lax.ppermute(passages, "query", mates)
    mate_len = lax.ppermute(lengths, "query", mates)
    got = exchange(table, Z_GROUPS)
    got, mate, mate_len, *same = lax.optimization_barrier((got, mate, mate_len, *same))
    got = small_call(turn_kernel, pltpu.VMEM((YX, 128), jnp.int32), got)
    codes = exchange(got, YX_GROUPS)
    hbm = pl.BlockSpec(memory_space=pltpu.HBM)

    def at(x, space):
        return pltpu.with_memory_space_constraint(x, space)

    scores = pl.pallas_call(
        score_kernel,
        out_shape=pltpu.VMEM((YX, 128), jnp.float32),
        in_specs=[hbm, hbm, VMEM, hbm, VMEM, VMEM, VMEM, hbm, VMEM],
        out_specs=VMEM,
        scratch_shapes=[
            pltpu.SMEM((C, BLK), jnp.int32),
            pltpu.VMEM((X * QL, T, D), jnp.bfloat16),
            pltpu.VMEM((BLOCKS, PT, D), jnp.bfloat16),
            pltpu.VMEM((2 * GROUP, 256), jnp.int32),
            pltpu.SMEM((2 * GROUP, 256), jnp.int32),
            pltpu.VMEM((GMAX, 1024), jnp.bfloat16),
            pltpu.VMEM((GMAX, GROUP * T), jnp.float32),
            pltpu.SemaphoreType.DMA,
            pltpu.SemaphoreType.DMA((8,)),
        ],
        compiler_params=pltpu.CompilerParams(vmem_limit_bytes=32 << 20),
    )(
        at(lengths, pltpu.HBM), at(mate_len, pltpu.HBM), at(codes, pltpu.VMEM),
        at(queries, pltpu.HBM), *[at(x, pltpu.VMEM) for x in same[1:]],
        at(passages, pltpu.HBM), at(mate, pltpu.VMEM),
    )
    back = exchange(scores, YX_GROUPS)
    back = small_call(turn_kernel, pltpu.VMEM((Z, 128), jnp.float32), back)
    back = exchange(back, Z_GROUPS)
    out = small_call(
        place_kernel, jax.ShapeDtypeStruct((CL, QL), jnp.float32), cand, keys, back
    )
    return out.T


def solution(mesh):
    in_specs = (
        P("query", None, None),
        P(("index", "query"), None, None),
        P(("index", "query")),
        P("query", "index"),
    )
    return jax.shard_map(
        shards, mesh=mesh, in_specs=in_specs, out_specs=P("query", "index"), check_vma=False
    )
```

time: 99.5 us -> 89.8 us (0.903)
  the two profiles are of different devices: /device:TPU:1 before, /device:TPU:2 now
where the time goes in v5:
time: 89.8 us; the launch traced here: 89.4 us
  blocking collectives  38.5 us (43%)
  starting transfers between devices  29.5 us (33%)
  waiting for transfers between devices  10.4 us (12%)
  Pallas kernels  10.2 us (11%)
    all_to_all x3, blocking collectives, exchange(): lax.all_to_all(x, ('index', 'query'), split_axis=0, concat_axis=0, tiled=...  38.5 us
    ppermute x3, starting transfers between devices, shards(): lax.ppermute(queries, 'query', [(k, (k + C * d) % (X * C)) for k in range...  13.1 us
    all_to_all x1, starting transfers between devices, exchange(): lax.all_to_all(x, ('index', 'query'), split_axis=0, concat_axis=0, tiled=...  12.6 us
    all_to_all x1, waiting for transfers between devices, exchange(): lax.all_to_all(x, ('index', 'query'), split_axis=0, concat_axis=0, tiled=...  9.21 us
    pallas_call x1, Pallas kernels, shards(): pl.pallas_call(score_kernel, out_shape=pltpu.VMEM((YX, 128), jnp.float32)...  7.92 us
    pallas_call x4, Pallas kernels, small_call(): pl.pallas_call(kernel, out_shape=out_shape, in_specs=[VMEM] * len(args),...  2.24 us
    ppermute x1, starting transfers between devices, shards(): mate_len = lax.ppermute(lengths, 'query', mates)  1.92 us
    ppermute x1, starting transfers between devices, shards(): mate = lax.ppermute(passages, 'query', mates)  1.91 us
  transfers between devices with their start and end apart: 6, of which 2 were waited for; matrix products, arithmetic and copies ran while one was open for 0% of the time, Pallas kernels for 1%

profile of v5, /device:TPU:2, one launch (start us, length us, event | category | flops | bytes accessed | tf_op | source)
XLA Modules:
  0.0 89.4 jit_solution(7585673483554037857)
XLA Ops:
  0.0 1.9 %collective-permute-start = (bf16[64,128,128]{2,1,0:T(8,128)(2,1)}, bf16[64,128,128]{2,1,0:T(8,128)(2,1)S(1)}, u32[]{:S(2)}, u32[]{:S(2)}) collective-permute-start(bf16[64,128,128]{2,1,0:T(8,128)(2,1)} %p_hbm.1), channel_id=1, source_target_pairs={{0,1},{1,0},{2,3},{3,2},{4,5},{5,4},{6,7},{7,6},{8,9},{9,8},{10,11... | collective-permute-start | bytes 6291464 | tf_op jit(solution)/shard_map/ppermute | solution.py:284
  1.9 7.8 %collective-permute-start.4 = (bf16[32,32,128]{2,1,0:T(8,128)(2,1)}, bf16[32,32,128]{2,1,0:T(8,128)(2,1)S(1)}, u32[]{:S(2)}, u32[]{:S(2)}) collective-permute-start(bf16[32,32,128]{2,1,0:T(8,128)(2,1)} %q0_hbm.1), channel_id=1, source_target_pairs={{0,6},{1,7},{2,0},{3,1},{4,2},{5,3},{6,4},{7,5},{8,14},{9,15},{10,... | collective-permute-start | bytes 786440 | tf_op jit(solution)/shard_map/ppermute | solution.py:274
  9.7 1.9 %collective-permute-start.3 = (bf16[32,32,128]{2,1,0:T(8,128)(2,1)}, bf16[32,32,128]{2,1,0:T(8,128)(2,1)S(1)}, u32[]{:S(2)}, u32[]{:S(2)}) collective-permute-start(bf16[32,32,128]{2,1,0:T(8,128)(2,1)} %q0_hbm.1), channel_id=1, source_target_pairs={{0,4},{1,5},{2,6},{3,7},{4,0},{5,1},{6,2},{7,3},{8,12},{9,13},{10,... | collective-permute-start | bytes 786440 | tf_op jit(solution)/shard_map/ppermute | solution.py:274
  11.7 3.4 %collective-permute-start.2 = (bf16[32,32,128]{2,1,0:T(8,128)(2,1)}, bf16[32,32,128]{2,1,0:T(8,128)(2,1)S(1)}, u32[]{:S(2)}, u32[]{:S(2)}) collective-permute-start(bf16[32,32,128]{2,1,0:T(8,128)(2,1)} %q0_hbm.1), channel_id=1, source_target_pairs={{0,2},{1,3},{2,4},{3,5},{4,6},{5,7},{6,0},{7,1},{8,10},{9,11},{10,... | collective-permute-start | bytes 786440 | tf_op jit(solution)/shard_map/ppermute | solution.py:274
  15.1 0.0 copy-start
  15.1 0.7 copy-done
  15.8 1.0 %shard_map.46 = (s32[16,128]{1,0:T(8,128)}, s32[16,128]{1,0:T(8,128)S(1)}) custom-call(s32[16,32]{1,0:T(8,128)S(1)} %bitcast.24), custom_call_target="tpu_custom_call" | custom-call | tf_op jit(solution)/shard_map/pallas_call | solution.py:264
  16.8 12.6 %all-to-all-start = ((s32[16,1,128]{2,1,0:T(1,128)}), s32[16,1,128]{2,1,0:T(1,128)S(1)}, u32[]{:S(2)}, u32[]{:S(2)}) async-start(s32[16,1,128]{2,1,0:T(1,128)} %bitcast.2), calls=%async_computation | async-start | bytes 16384 | tf_op jit(solution)/shard_map/all_to_all | solution.py:30
  29.4 1.9 %collective-permute-start.1 = (s32[64]{0:T(128)}, s32[64]{0:T(128)S(1)}, u32[]{:S(2)}, u32[]{:S(2)}) collective-permute-start(s32[64]{0:T(128)} %len_hbm.1), channel_id=1, source_target_pairs={{0,1},{1,0},{2,3},{3,2},{4,5},{5,4},{6,7},{7,6},{8,9},{9,8},{10,11... | collective-permute-start | bytes 776 | tf_op jit(solution)/shard_map/ppermute | solution.py:285
  31.3 1.2 %collective-permute-done.1.mate_len_hbm = s32[64]{0:T(128)S(1)} collective-permute-done((s32[64]{0:T(128)}, s32[64]{0:T(128)S(1)}, u32[]{:S(2)}, u32[]{:S(2)}) %collective-permute-start.1) | collective-permute-done | bytes 288 | tf_op jit(solution)/shard_map/ppermute | solution.py:285
  32.5 0.0 copy-start.2
  32.5 9.2 %all-to-all-done = s32[16,1,128]{2,1,0:T(1,128)S(1)} async-done(((s32[16,1,128]{2,1,0:T(1,128)}), s32[16,1,128]{2,1,0:T(1,128)S(1)}, u32[]{:S(2)}, u32[]{:S(2)}) %all-to-all-start) | async-done | bytes 8224 | tf_op jit(solution)/shard_map/all_to_all | solution.py:30
  41.7 0.0 collective-permute-done.4.q3_ref
  41.7 0.0 collective-permute-done.3.q2_ref
  41.7 0.0 collective-permute-done.2.q1_ref
  41.7 0.0 collective-permute-done.mate_ref
  41.7 0.1 shard_map.47
  41.8 12.5 %all_to_all.45 = s32[16,1,128]{2,1,0:T(1,128)S(1)} all-to-all(s32[16,1,128]{2,1,0:T(1,128)S(1)} %bitcast.21), channel_id=1, replica_groups={{0,2,4,6,8,10,12,14,16,18,20,22,24,26,28,30},{1,3,5,7,9,11,13,15,17,19,..., dimensions={0} | all-to-all | bytes 16384 | tf_op jit(solution)/shard_map/all_to_all | solution.py:30
  54.4 0.0 copy-done.2
  54.4 0.0 copy-start.1
  54.4 7.9 %shard_map.48 = f32[16,128]{1,0:T(8,128)S(1)} custom-call(s32[64]{0:T(128)} %len_hbm.1, s32[64]{0:T(128)} %copy-done.2, s32[16,128]{1,0:T(8,128)S(1)} %bitcast.18, bf16[32,32,128]{2,1,0:T(8,128)(2,1)} %q0_hbm.1, bf16[32,32,128]{2,1,0:T(8,128)(2,1)S(1)} %collective-permute-done.2.q1_ref, bf16[32,32,128]{2,1,0:T(8,128)(2,1)S(1)} %collective-permute-done.3.q2_ref, ...), custom_call_target="tpu_custom_call" | custom-call | tf_op jit(solution)/shard_map/pallas_call | solution.py:295
  62.3 10.8 %all_to_all.46 = f32[16,1,128]{2,1,0:T(1,128)S(1)} all-to-all(f32[16,1,128]{2,1,0:T(1,128)S(1)} %bitcast.19), channel_id=1, replica_groups={{0,2,4,6,8,10,12,14,16,18,20,22,24,26,28,30},{1,3,5,7,9,11,13,15,17,19,..., dimensions={0} | all-to-all | bytes 16384 | tf_op jit(solution)/shard_map/all_to_all | solution.py:30
  73.1 0.1 shard_map.49
  73.2 15.1 %all_to_all.47 = f32[16,1,128]{2,1,0:T(1,128)S(1)} all-to-all(f32[16,1,128]{2,1,0:T(1,128)S(1)} %bitcast.23), channel_id=1, replica_groups={{0,32,64,96,128,160,192,224,256,288,320,352,384,416,448,480},{1,33,65,9..., dimensions={0} | all-to-all | bytes 16384 | tf_op jit(solution)/shard_map/all_to_all | solution.py:30
  88.4 0.0 copy-done.1
  88.4 1.0 %shard_map.50 = f32[16,32]{1,0:T(8,128)} custom-call(s32[16,32]{1,0:T(8,128)S(1)} %bitcast.25, s32[16,128]{1,0:T(8,128)S(1)} %get-tuple-element.13.key_ref, f32[16,128]{1,0:T(8,128)S(1)} %bitcast.26), custom_call_target="tpu_custom_call" | custom-call | tf_op jit(solution)/shard_map/pallas_call | solution.py:264
Async XLA Ops:
  0.0 41.7 %collective-permute-start = (bf16[64,128,128]{2,1,0:T(8,128)(2,1)}, bf16[64,128,128]{2,1,0:T(8,128)(2,1)S(1)}, u32[]{:S(2)}, u32[]{:S(2)}) collective-permute-start(bf16[64,128,128]{2,1,0:T(8,128)(2,1)} %p_hbm.1), channel_id=1, source_target_pairs={{0,1},{1,0},{2,3},{3,2},{4,5},{5,4},{6,7},{7,6},{8,9},{9,8},{10,11... | collective-permute-start | bytes 6291464 | tf_op jit(solution)/shard_map/ppermute | solution.py:284
  1.9 39.8 %collective-permute-start.4 = (bf16[32,32,128]{2,1,0:T(8,128)(2,1)}, bf16[32,32,128]{2,1,0:T(8,128)(2,1)S(1)}, u32[]{:S(2)}, u32[]{:S(2)}) collective-permute-start(bf16[32,32,128]{2,1,0:T(8,128)(2,1)} %q0_hbm.1), channel_id=1, source_target_pairs={{0,6},{1,7},{2,0},{3,1},{4,2},{5,3},{6,4},{7,5},{8,14},{9,15},{10,... | collective-permute-start | bytes 786440 | tf_op jit(solution)/shard_map/ppermute | solution.py:274
  9.7 32.0 %collective-permute-start.3 = (bf16[32,32,128]{2,1,0:T(8,128)(2,1)}, bf16[32,32,128]{2,1,0:T(8,128)(2,1)S(1)}, u32[]{:S(2)}, u32[]{:S(2)}) collective-permute-start(bf16[32,32,128]{2,1,0:T(8,128)(2,1)} %q0_hbm.1), channel_id=1, source_target_pairs={{0,4},{1,5},{2,6},{3,7},{4,0},{5,1},{6,2},{7,3},{8,12},{9,13},{10,... | collective-permute-start | bytes 786440 | tf_op jit(solution)/shard_map/ppermute | solution.py:274
  11.7 30.1 %collective-permute-start.2 = (bf16[32,32,128]{2,1,0:T(8,128)(2,1)}, bf16[32,32,128]{2,1,0:T(8,128)(2,1)S(1)}, u32[]{:S(2)}, u32[]{:S(2)}) collective-permute-start(bf16[32,32,128]{2,1,0:T(8,128)(2,1)} %q0_hbm.1), channel_id=1, source_target_pairs={{0,2},{1,3},{2,4},{3,5},{4,6},{5,7},{6,0},{7,1},{8,10},{9,11},{10,... | collective-permute-start | bytes 786440 | tf_op jit(solution)/shard_map/ppermute | solution.py:274
  15.1 0.7 copy-start
  16.8 24.9 %all-to-all-start = ((s32[16,1,128]{2,1,0:T(1,128)}), s32[16,1,128]{2,1,0:T(1,128)S(1)}, u32[]{:S(2)}, u32[]{:S(2)}) async-start(s32[16,1,128]{2,1,0:T(1,128)} %bitcast.2), calls=%async_computation | async-start | bytes 16384 | tf_op jit(solution)/shard_map/all_to_all | solution.py:30
  29.4 3.2 %collective-permute-start.1 = (s32[64]{0:T(128)}, s32[64]{0:T(128)S(1)}, u32[]{:S(2)}, u32[]{:S(2)}) collective-permute-start(s32[64]{0:T(128)} %len_hbm.1), channel_id=1, source_target_pairs={{0,1},{1,0},{2,3},{3,2},{4,5},{5,4},{6,7},{7,6},{8,9},{9,8},{10,11... | collective-permute-start | bytes 776 | tf_op jit(solution)/shard_map/ppermute | solution.py:285
  32.5 21.9 %copy-start.2 = (s32[64]{0:T(128)}, s32[64]{0:T(128)S(1)}, u32[]{:S(2)}) copy-start(s32[64]{0:T(128)S(1)} %collective-permute-done.1.mate_len_hbm) | copy-start | bytes 772
  54.4 34.0 %copy-start.1 = (s32[32,16]{0,1:T(8,128)S(1)}, s32[32,16]{0,1:T(8,128)}, u32[]{:S(2)}) copy-start(s32[32,16]{0,1:T(8,128)} %param.7) | copy-start | bytes 6148

commit v6 on v4

--- a/solution.py
+++ b/solution.py
@@ -14,7 +14,7 @@
 T, D, PT = 32, 128, 128
 GROUP = 8
 GMAX = 192
-UNROLL = 8
+UNROLL = 32
 BIG = 1 << 30
 
 Z_GROUPS = [[r + YQ * z for z in range(Z)] for r in range(YQ)]
@@ -44,7 +44,10 @@
     return out
 
 
-def request_kernel(cand_ref, code_ref, key_ref):
+def request_kernel(cand_hbm, code_ref, key_ref, cand_ref, sem):
+    copy = pltpu.make_async_copy(cand_hbm, cand_ref, sem)
+    copy.start()
+    copy.wait()
     cand = cand_ref[...]
     lane_owner = iota((CL, OWNERS), 1)
     sub = iota((CL, 1), 0)
@@ -282,14 +285,13 @@
         for d in range(1, Q // 2)
     ]
     cand = candidates.T
-    table, keys = small_call(
+    table, keys = pl.pallas_call(
         request_kernel,
-        (
-            pltpu.VMEM((Z, 128), jnp.int32),
-            pltpu.VMEM((Z, 128), jnp.int32),
-        ),
-        cand,
-    )
+        out_shape=(pltpu.VMEM((Z, 128), jnp.int32), pltpu.VMEM((Z, 128), jnp.int32)),
+        in_specs=[pl.BlockSpec(memory_space=pltpu.HBM)],
+        out_specs=(VMEM, VMEM),
+        scratch_shapes=[pltpu.VMEM((CL, QL), jnp.int32), pltpu.SemaphoreType.DMA],
+    )(pltpu.with_memory_space_constraint(cand, pltpu.HBM))
     got = exchange(table, Z_GROUPS)
     same = jnp.concatenate(same, axis=0)
     got, same = lax.optimization_barrier((got, same))

time: 88.4 us -> 87.1 us (0.985)
    pallas_call x0 -> x1, Pallas kernels: none -> 1.76 us  [shards(): pl.pallas_call(request_kernel, out_shape=(pltpu.VMEM((Z, 128), jnp.int32)...]
    pallas_call x1, Pallas kernels: 5.9 us -> 4.62 us  [shards(): pl.pallas_call(score_kernel, out_shape=jax.ShapeDtypeStruct((YQ, 128), jn...]
    pallas_call x4 -> x3, Pallas kernels: 2.25 us -> 1.2 us  [small_call(): pl.pallas_call(kernel, out_shape=out_shape, in_specs=[VMEM] * len(args),...]
  transfers between devices with their start and end apart: 5 -> 5, of which waited for: 1 -> 1; matrix products, arithmetic and copies ran while one was open for 1% -> 1% of each run, Pallas kernels for 1% -> 2%
where the time goes in v6:
time: 87.1 us; the launch traced here: 86.7 us
  blocking collectives  36.1 us (41%)
  starting transfers between devices  31.7 us (36%)
  waiting for transfers between devices  10.1 us (12%)
  Pallas kernels  7.58 us (9%)
  other arithmetic  1.09 us (1%)
    all_to_all x3, blocking collectives, exchange(): lax.all_to_all(x, ('index', 'query'), split_axis=0, concat_axis=0, tiled=...  36.1 us
    all_to_all x1, starting transfers between devices, exchange(): lax.all_to_all(x, ('index', 'query'), split_axis=0, concat_axis=0, tiled=...  14.9 us
    ppermute x3, starting transfers between devices, shards(): lax.ppermute(queries, 'query', [(k, (k + 2 * d) % Q) for k in range(Q)])  12 us
    all_to_all x1, waiting for transfers between devices, exchange(): lax.all_to_all(x, ('index', 'query'), split_axis=0, concat_axis=0, tiled=...  10.1 us
    ppermute x1, starting transfers between devices, shards(): other = lax.ppermute(same, 'query', [(k, k ^ 1) for k in range(Q)])  4.84 us
    pallas_call x1, Pallas kernels, shards(): pl.pallas_call(score_kernel, out_shape=jax.ShapeDtypeStruct((YQ, 128), jn...  4.62 us
    pallas_call x1, Pallas kernels, shards(): pl.pallas_call(request_kernel, out_shape=(pltpu.VMEM((Z, 128), jnp.int32)...  1.76 us
  transfers between devices with their start and end apart: 5, of which 1 were waited for; matrix products, arithmetic and copies ran while one was open for 1% of the time, Pallas kernels for 2%

profile of v6, /device:TPU:1, one launch (start us, length us, event | category | flops | bytes accessed | tf_op | source)
XLA Modules:
  0.0 86.7 jit_solution(16626245831564961560)
XLA Ops:
  0.0 5.5 %collective-permute-start.1 = (bf16[32,32,128]{2,1,0:T(8,128)(2,1)}, bf16[32,32,128]{2,1,0:T(8,128)(2,1)S(1)}, u32[]{:S(2)}, u32[]{:S(2)}) collective-permute-start(bf16[32,32,128]{2,1,0:T(8,128)(2,1)} %param.4), channel_id=1, source_target_pairs={{0,4},{1,5},{2,6},{3,7},{4,0},{5,1},{6,2},{7,3},{8,12},{9,13},{10,... | collective-permute-start | bytes 786440 | tf_op jit(solution)/shard_map/ppermute | solution.py:284
  5.5 2.2 %collective-permute-start = (bf16[32,32,128]{2,1,0:T(8,128)(2,1)}, bf16[32,32,128]{2,1,0:T(8,128)(2,1)S(1)}, u32[]{:S(2)}, u32[]{:S(2)}) collective-permute-start(bf16[32,32,128]{2,1,0:T(8,128)(2,1)} %param.4), channel_id=1, source_target_pairs={{0,2},{1,3},{2,4},{3,5},{4,6},{5,7},{6,0},{7,1},{8,10},{9,11},{10,... | collective-permute-start | bytes 786440 | tf_op jit(solution)/shard_map/ppermute | solution.py:284
  7.7 4.3 %collective-permute-start.2 = (bf16[32,32,128]{2,1,0:T(8,128)(2,1)}, bf16[32,32,128]{2,1,0:T(8,128)(2,1)S(1)}, u32[]{:S(2)}, u32[]{:S(2)}) collective-permute-start(bf16[32,32,128]{2,1,0:T(8,128)(2,1)} %param.4), channel_id=1, source_target_pairs={{0,6},{1,7},{2,0},{3,1},{4,2},{5,3},{6,4},{7,5},{8,14},{9,15},{10,... | collective-permute-start | bytes 786440 | tf_op jit(solution)/shard_map/ppermute | solution.py:284
  12.0 1.8 %shard_map.46 = (s32[16,128]{1,0:T(8,128)}, s32[16,128]{1,0:T(8,128)S(1)}) custom-call(s32[16,32]{1,0:T(8,128)} %bitcast.24), custom_call_target="tpu_custom_call" | custom-call | tf_op jit(solution)/shard_map/pallas_call | solution.py:288
  13.8 14.9 %all-to-all-start = ((s32[16,1,128]{2,1,0:T(1,128)}), s32[16,1,128]{2,1,0:T(1,128)S(1)}, u32[]{:S(2)}, u32[]{:S(2)}) async-start(s32[16,1,128]{2,1,0:T(1,128)} %bitcast.2), calls=%async_computation | async-start | bytes 16384 | tf_op jit(solution)/shard_map/all_to_all | solution.py:29
  28.7 0.0 collective-permute-done.1
  28.7 0.0 collective-permute-done
  28.7 0.0 collective-permute-done.2
  28.7 1.1 %pad_maximum_fusion.same_ref = bf16[128,32,128]{2,1,0:T(8,128)(2,1)S(1)} fusion(bf16[32,32,128]{2,1,0:T(8,128)(2,1)S(1)} %collective-permute-done.2, bf16[32,32,128]{2,1,0:T(8,128)(2,1)S(1)} %collective-permute-done.1, bf16[32,32,128]{2,1,0:T(8,128)(2,1)S(1)} %collective-permute-done, bf16[32,32,128]{2,1,0:T(8,128)(2,1)} %param.4), kind=kLoop, calls=%fused_computation | loop fusion | flops 1572864 | bytes 2097152 | tf_op jit(solution)/shard_map/concatenate | solution.py:296
  29.8 10.1 %all-to-all-done = s32[16,1,128]{2,1,0:T(1,128)S(1)} async-done(((s32[16,1,128]{2,1,0:T(1,128)}), s32[16,1,128]{2,1,0:T(1,128)S(1)}, u32[]{:S(2)}, u32[]{:S(2)}) %all-to-all-start) | async-done | bytes 8224 | tf_op jit(solution)/shard_map/all_to_all | solution.py:29
  39.9 4.8 %collective-permute-start.3 = (bf16[128,32,128]{2,1,0:T(8,128)(2,1)S(1)}, bf16[128,32,128]{2,1,0:T(8,128)(2,1)S(1)}, u32[]{:S(2)}, u32[]{:S(2)}) collective-permute-start(bf16[128,32,128]{2,1,0:T(8,128)(2,1)S(1)} %pad_maximum_fusion.same_ref), channel_id=1, source_target_pairs={{0,1},{1,0},{2,3},{3,2},{4,5},{5,4},{6,7},{7,6},{8,9},{9,8},{10,11... | collective-permute-start | bytes 3145736 | tf_op jit(solution)/shard_map/ppermute | solution.py:298
  44.8 0.1 shard_map.47
  44.9 11.5 %all_to_all.45 = s32[32,1,128]{2,1,0:T(1,128)S(1)} all-to-all(s32[32,1,128]{2,1,0:T(1,128)S(1)} %bitcast.20), channel_id=1, replica_groups={{0,1,2,3,4,5,6,7,8,9,10,11,12,13,14,15,16,17,18,19,20,21,22,23,24,25,26..., dimensions={0} | all-to-all | bytes 32768 | tf_op jit(solution)/shard_map/all_to_all | solution.py:29
  56.4 0.0 collective-permute-done.3.other_ref
  56.4 0.0 copy-start
  56.4 4.6 %shard_map.48 = f32[32,128]{1,0:T(8,128)S(1)} custom-call(s32[64]{0:T(128)} %len_hbm.1, s32[32,128]{1,0:T(8,128)S(1)} %bitcast.18, bf16[128,32,128]{2,1,0:T(8,128)(2,1)S(1)} %pad_maximum_fusion.same_ref, bf16[128,32,128]{2,1,0:T(8,128)(2,1)S(1)} %collective-permute-done.3.other_ref, bf16[64,128,128]{2,1,0:T(8,128)(2,1)} %p_hbm.1), custom_call_target="tpu_custom_call" | custom-call | tf_op jit(solution)/shard_map/pallas_call | solution.py:302
  61.0 10.7 %all_to_all.46 = f32[32,1,128]{2,1,0:T(1,128)S(1)} all-to-all(f32[32,1,128]{2,1,0:T(1,128)S(1)} %bitcast.19), channel_id=1, replica_groups={{0,1,2,3,4,5,6,7,8,9,10,11,12,13,14,15,16,17,18,19,20,21,22,23,24,25,26..., dimensions={0} | all-to-all | bytes 32768 | tf_op jit(solution)/shard_map/all_to_all | solution.py:29
  71.7 0.1 shard_map.49
  71.8 13.9 %all_to_all.47 = f32[16,1,128]{2,1,0:T(1,128)S(1)} all-to-all(f32[16,1,128]{2,1,0:T(1,128)S(1)} %bitcast.23), channel_id=1, replica_groups={{0,32,64,96,128,160,192,224,256,288,320,352,384,416,448,480},{1,33,65,9..., dimensions={0} | all-to-all | bytes 16384 | tf_op jit(solution)/shard_map/all_to_all | solution.py:29
  85.6 0.0 copy-done
  85.6 1.0 %shard_map.50 = f32[16,32]{1,0:T(8,128)} custom-call(s32[16,32]{1,0:T(8,128)S(1)} %bitcast.25, s32[16,128]{1,0:T(8,128)S(1)} %get-tuple-element.9.key_ref, f32[16,128]{1,0:T(8,128)S(1)} %bitcast.26), custom_call_target="tpu_custom_call" | custom-call | tf_op jit(solution)/shard_map/pallas_call | solution.py:274
Async XLA Ops:
  0.0 28.7 %collective-permute-start.1 = (bf16[32,32,128]{2,1,0:T(8,128)(2,1)}, bf16[32,32,128]{2,1,0:T(8,128)(2,1)S(1)}, u32[]{:S(2)}, u32[]{:S(2)}) collective-permute-start(bf16[32,32,128]{2,1,0:T(8,128)(2,1)} %param.4), channel_id=1, source_target_pairs={{0,4},{1,5},{2,6},{3,7},{4,0},{5,1},{6,2},{7,3},{8,12},{9,13},{10,... | collective-permute-start | bytes 786440 | tf_op jit(solution)/shard_map/ppermute | solution.py:284
  5.5 23.2 %collective-permute-start = (bf16[32,32,128]{2,1,0:T(8,128)(2,1)}, bf16[32,32,128]{2,1,0:T(8,128)(2,1)S(1)}, u32[]{:S(2)}, u32[]{:S(2)}) collective-permute-start(bf16[32,32,128]{2,1,0:T(8,128)(2,1)} %param.4), channel_id=1, source_target_pairs={{0,2},{1,3},{2,4},{3,5},{4,6},{5,7},{6,0},{7,1},{8,10},{9,11},{10,... | collective-permute-start | bytes 786440 | tf_op jit(solution)/shard_map/ppermute | solution.py:284
  7.7 21.0 %collective-permute-start.2 = (bf16[32,32,128]{2,1,0:T(8,128)(2,1)}, bf16[32,32,128]{2,1,0:T(8,128)(2,1)S(1)}, u32[]{:S(2)}, u32[]{:S(2)}) collective-permute-start(bf16[32,32,128]{2,1,0:T(8,128)(2,1)} %param.4), channel_id=1, source_target_pairs={{0,6},{1,7},{2,0},{3,1},{4,2},{5,3},{6,4},{7,5},{8,14},{9,15},{10,... | collective-permute-start | bytes 786440 | tf_op jit(solution)/shard_map/ppermute | solution.py:284
  13.8 26.2 %all-to-all-start = ((s32[16,1,128]{2,1,0:T(1,128)}), s32[16,1,128]{2,1,0:T(1,128)S(1)}, u32[]{:S(2)}, u32[]{:S(2)}) async-start(s32[16,1,128]{2,1,0:T(1,128)} %bitcast.2), calls=%async_computation | async-start | bytes 16384 | tf_op jit(solution)/shard_map/all_to_all | solution.py:29
  39.9 16.5 %collective-permute-start.3 = (bf16[128,32,128]{2,1,0:T(8,128)(2,1)S(1)}, bf16[128,32,128]{2,1,0:T(8,128)(2,1)S(1)}, u32[]{:S(2)}, u32[]{:S(2)}) collective-permute-start(bf16[128,32,128]{2,1,0:T(8,128)(2,1)S(1)} %pad_maximum_fusion.same_ref), channel_id=1, source_target_pairs={{0,1},{1,0},{2,3},{3,2},{4,5},{5,4},{6,7},{7,6},{8,9},{9,8},{10,11... | collective-permute-start | bytes 3145736 | tf_op jit(solution)/shard_map/ppermute | solution.py:298
  56.4 29.3 %copy-start = (s32[32,16]{0,1:T(8,128)S(1)}, s32[32,16]{0,1:T(8,128)}, u32[]{:S(2)}) copy-start(s32[32,16]{0,1:T(8,128)} %param.7) | copy-start | bytes 6148

commit v7 on v4

--- a/solution.py
+++ b/solution.py
@@ -14,7 +14,7 @@
 T, D, PT = 32, 128, 128
 GROUP = 8
 GMAX = 192
-UNROLL = 8
+UNROLL = 32
 BIG = 1 << 30
 
 Z_GROUPS = [[r + YQ * z for z in range(Z)] for r in range(YQ)]
@@ -42,6 +42,26 @@
                 seg = pltpu.roll(seg, shift, 1) if shift else seg
                 out = jnp.where((row == 4 * t + j) & (lane >> 5 == k), seg, out)
     return out
+
+
+def by_plane(x):
+    xt = jnp.transpose(jnp.concatenate([x, jnp.zeros((112, 128), x.dtype)], axis=0))
+    lane = iota((YQ, 128), 1)
+    return jnp.where(lane < Z, xt[:YQ], pltpu.roll(xt[YQ : 2 * YQ], Z, 1))
+
+
+def by_z(x):
+    xt = jnp.transpose(jnp.concatenate([x, jnp.zeros((96, 128), x.dtype)], axis=0))
+    lane = iota((Z, 128), 1)
+    return jnp.where(lane < YQ, xt[:Z], pltpu.roll(xt[Z : 2 * Z], YQ, 1))
+
+
+def by_plane_kernel(x_ref, o_ref):
+    o_ref[...] = by_plane(x_ref[...])
+
+
+def by_z_kernel(x_ref, o_ref):
+    o_ref[...] = by_z(x_ref[...])
 
 
 def request_kernel(cand_ref, code_ref, key_ref):
@@ -63,23 +83,8 @@
     lane = iota((Z, 128), 1)
     key = spread((first, last), row, lane)
     key_ref[...] = key
-    code_ref[...] = jnp.where(
-        (key >= 0) & (lane < 2 * YQ), ((key >> 10) << 6) + (key & 63), -1
-    )
-
-
-def turn_kernel(x_ref, o_ref):
-    x = jnp.concatenate([x_ref[...], jnp.zeros((112, 128), jnp.int32)], axis=0)
-    xt = jnp.transpose(x)
-    lane = iota((YQ, 128), 1)
-    o_ref[...] = jnp.where(lane < Z, xt[:YQ], pltpu.roll(xt[YQ : 2 * YQ], Z, 1))
-
-
-def back_kernel(x_ref, o_ref):
-    x = jnp.concatenate([x_ref[...], jnp.zeros((96, 128), jnp.float32)], axis=0)
-    xt = jnp.transpose(x)
-    lane = iota((Z, 128), 1)
-    o_ref[...] = jnp.where(lane < YQ, xt[:Z], pltpu.roll(xt[Z : 2 * Z], YQ, 1))
+    code = jnp.where((key >= 0) & (lane < 2 * YQ), ((key >> 10) << 6) + (key & 63), -1)
+    code_ref[...] = by_plane(code)
 
 
 def split3(x):
@@ -107,16 +112,12 @@
     same_copy.start()
     other_copy = pltpu.make_async_copy(other_ref, q_ref.at[pl.ds(half, half)], other_sem)
     other_copy.start()
-    code = jnp.full((Q, 128), -1, jnp.int32)
     lane8 = iota((Q, 128), 1)
-    for y in range(Y):
-        part = code_ref[Q * y : Q * (y + 1), :]
-        part = pltpu.roll(part, 32 * y, 1) if y else part
-        code = jnp.where(lane8 >> 5 == y, part, code)
+    code = jnp.where(lane8 < 64, code_ref[0:8, :], pltpu.roll(code_ref[8:16, :], 64, 1))
     valid = code >= 0
     block = jnp.where(valid, code & 63, BLK)
     me = lax.axis_index("query")
-    source = iota((Q, 128), 0)
+    source = lane8 & (Q - 1)
     piece = (((source ^ me) & 1) << 2) + (((me >> 1) - (source >> 1)) & 3)
     query = jnp.where(valid, (code >> 6) + QL * piece, 0)
 
@@ -211,9 +212,8 @@
             jnp.sum(jnp.where(here, picked[:, 128 * q : 128 * (q + 1)], 0.0), axis=0, keepdims=True)
         )
     out = jnp.concatenate(out, axis=0)
-    for y in range(Y):
-        shift = (128 - 32 * y) % 128
-        o_ref[Q * y : Q * (y + 1), :] = pltpu.roll(out, shift, 1) if shift else out
+    o_ref[0:8, :] = out
+    o_ref[8:16, :] = pltpu.roll(out, 64, 1)
 
 
 def place_kernel(cand_ref, key_ref, x_ref, o_ref):
@@ -267,9 +267,10 @@
 VMEM = pl.BlockSpec(memory_space=pltpu.VMEM)
 
 
-def small_call(kernel, out_shape, *args):
+def small_call(kernel, out_shape, *args, hint=None):
     return pl.pallas_call(
         kernel,
+        cost_estimate=hint,
         out_shape=out_shape,
         in_specs=[VMEM] * len(args),
         out_specs=jax.tree.map(lambda _: VMEM, out_shape),
@@ -284,22 +285,20 @@
     cand = candidates.T
     table, keys = small_call(
         request_kernel,
-        (
-            pltpu.VMEM((Z, 128), jnp.int32),
-            pltpu.VMEM((Z, 128), jnp.int32),
-        ),
+        (pltpu.VMEM((YQ, 128), jnp.int32), pltpu.VMEM((Z, 128), jnp.int32)),
         cand,
     )
-    got = exchange(table, Z_GROUPS)
+    got = exchange(table, YQ_GROUPS)
+    hint = pl.CostEstimate(flops=10**11, transcendentals=0, bytes_accessed=2**20)
+    got = small_call(by_z_kernel, pltpu.VMEM((Z, 128), jnp.int32), got, hint=hint)
+    codes = exchange(got, Z_GROUPS)
     same = jnp.concatenate(same, axis=0)
-    got, same = lax.optimization_barrier((got, same))
+    codes, same = lax.optimization_barrier((codes, same))
     other = lax.ppermute(same, "query", [(k, k ^ 1) for k in range(Q)])
-    got = small_call(turn_kernel, pltpu.VMEM((YQ, 128), jnp.int32), got)
-    codes = exchange(got, YQ_GROUPS)
     hbm = pl.BlockSpec(memory_space=pltpu.HBM)
     scores = pl.pallas_call(
         score_kernel,
-        out_shape=jax.ShapeDtypeStruct((YQ, 128), jnp.float32),
+        out_shape=pltpu.VMEM((Z, 128), jnp.float32),
         in_specs=[hbm, VMEM, VMEM, VMEM, hbm],
         out_specs=VMEM,
         scratch_shapes=[
@@ -324,8 +323,9 @@
         pltpu.with_memory_space_constraint(other, pltpu.VMEM),
         pltpu.with_memory_space_constraint(passages, pltpu.HBM),
     )
-    back = exchange(scores, YQ_GROUPS)
-    back = small_call(back_kernel, pltpu.VMEM((Z, 128), jnp.float32), back)
+    back = small_call(by_plane_kernel, pltpu.VMEM((YQ, 128), jnp.float32), scores)
+    back = exchange(back, YQ_GROUPS)
+    back = small_call(by_z_kernel, pltpu.VMEM((Z, 128), jnp.float32), back)
     back = exchange(back, Z_GROUPS)
     out = small_call(
         place_kernel, jax.ShapeDtypeStruct((CL, QL), jnp.float32), cand, keys, back

time: 88.4 us -> 87.4 us (0.989)
  blocking collectives: 36.1 us -> 25.5 us
  starting transfers between devices: 31.7 us -> 39.5 us
  waiting for transfers between devices: 10.1 us -> 13.3 us
  other arithmetic: 1.09 us -> 0.13 us
    all_to_all x3 -> x2, blocking collectives: 36.1 us -> 25.5 us  [exchange(): lax.all_to_all(x, ('index', 'query'), split_axis=0, concat_axis=0, tiled=...]
    all_to_all x1 -> x2, starting transfers between devices: 14.9 us -> 23.5 us  [exchange(): lax.all_to_all(x, ('index', 'query'), split_axis=0, concat_axis=0, tiled=...]
    ppermute x1, waiting for transfers between devices: 0.01 us -> 2.26 us  [shards(): other = lax.ppermute(same, 'query', [(k, k ^ 1) for k in range(Q)])]
    concatenate x1, other arithmetic: 1.09 us -> 0.13 us  [shards(): same = jnp.concatenate(same, axis=0)]
    all_to_all x1 -> x2, waiting for transfers between devices: 10.1 us -> 11 us  [exchange(): lax.all_to_all(x, ('index', 'query'), split_axis=0, concat_axis=0, tiled=...]
    pallas_call x5 -> x6, Pallas kernels: 8.15 us -> 7.77 us  [the longest x1 4.62 us: shards(): pl.pallas_call(score_kernel, out_shape=pltpu.VMEM((Z, 128), jnp.float32),...]
  transfers between devices with their start and end apart: 5 -> 6, of which waited for: 1 -> 2; matrix products, arithmetic and copies ran while one was open for 1% -> 0% of each run, Pallas kernels for 1% -> 1%
where the time goes in v7:
time: 87.4 us; the launch traced here: 87 us
  starting transfers between devices  39.5 us (45%)
  blocking collectives  25.5 us (29%)
  waiting for transfers between devices  13.3 us (15%)
  Pallas kernels  7.77 us (9%)
    all_to_all x2, blocking collectives, exchange(): lax.all_to_all(x, ('index', 'query'), split_axis=0, concat_axis=0, tiled=...  25.5 us
    all_to_all x2, starting transfers between devices, exchange(): lax.all_to_all(x, ('index', 'query'), split_axis=0, concat_axis=0, tiled=...  23.5 us
    ppermute x3, starting transfers between devices, shards(): lax.ppermute(queries, 'query', [(k, (k + 2 * d) % Q) for k in range(Q)])  11.3 us
    all_to_all x2, waiting for transfers between devices, exchange(): lax.all_to_all(x, ('index', 'query'), split_axis=0, concat_axis=0, tiled=...  11 us
    ppermute x1, starting transfers between devices, shards(): other = lax.ppermute(same, 'query', [(k, k ^ 1) for k in range(Q)])  4.66 us
    pallas_call x1, Pallas kernels, shards(): pl.pallas_call(score_kernel, out_shape=pltpu.VMEM((Z, 128), jnp.float32),...  4.62 us
    pallas_call x5, Pallas kernels, small_call(): pl.pallas_call(kernel, cost_estimate=hint, out_shape=out_shape, in_specs=...  3.15 us
    ppermute x1, waiting for transfers between devices, shards(): other = lax.ppermute(same, 'query', [(k, k ^ 1) for k in range(Q)])  2.26 us
  transfers between devices with their start and end apart: 6, of which 2 were waited for; matrix products, arithmetic and copies ran while one was open for 0% of the time, Pallas kernels for 1%

profile of v7, /device:TPU:1, one launch (start us, length us, event | category | flops | bytes accessed | tf_op | source)
XLA Modules:
  0.0 87.0 jit_solution(2407981724220950752)
XLA Ops:
  0.0 0.0 copy-start
  0.0 0.7 copy-done
  0.7 1.2 %shard_map.46 = (s32[32,128]{1,0:T(8,128)}, s32[16,128]{1,0:T(8,128)S(1)}) custom-call(s32[16,32]{1,0:T(8,128)S(1)} %bitcast.22), custom_call_target="tpu_custom_call" | custom-call | tf_op jit(solution)/shard_map/pallas_call | solution.py:271
  1.9 10.4 %all-to-all-start = ((s32[32,1,128]{2,1,0:T(1,128)}), s32[32,1,128]{2,1,0:T(1,128)S(1)}, u32[]{:S(2)}, u32[]{:S(2)}) async-start(s32[32,1,128]{2,1,0:T(1,128)} %bitcast.2), calls=%async_computation | async-start | bytes 32768 | tf_op jit(solution)/shard_map/all_to_all | solution.py:29
  12.3 4.8 %collective-permute-start.1 = (bf16[32,32,128]{2,1,0:T(8,128)(2,1)}, bf16[32,32,128]{2,1,0:T(8,128)(2,1)S(1)}, u32[]{:S(2)}, u32[]{:S(2)}) collective-permute-start(bf16[32,32,128]{2,1,0:T(8,128)(2,1)} %param.4), channel_id=1, source_target_pairs={{0,4},{1,5},{2,6},{3,7},{4,0},{5,1},{6,2},{7,3},{8,12},{9,13},{10,... | collective-permute-start | bytes 786440 | tf_op jit(solution)/shard_map/ppermute | solution.py:282
  17.1 2.2 %collective-permute-start = (bf16[32,32,128]{2,1,0:T(8,128)(2,1)}, bf16[32,32,128]{2,1,0:T(8,128)(2,1)S(1)}, u32[]{:S(2)}, u32[]{:S(2)}) collective-permute-start(bf16[32,32,128]{2,1,0:T(8,128)(2,1)} %param.4), channel_id=1, source_target_pairs={{0,2},{1,3},{2,4},{3,5},{4,6},{5,7},{6,0},{7,1},{8,10},{9,11},{10,... | collective-permute-start | bytes 786440 | tf_op jit(solution)/shard_map/ppermute | solution.py:282
  19.3 4.3 %collective-permute-start.2 = (bf16[32,32,128]{2,1,0:T(8,128)(2,1)}, bf16[32,32,128]{2,1,0:T(8,128)(2,1)S(1)}, u32[]{:S(2)}, u32[]{:S(2)}) collective-permute-start(bf16[32,32,128]{2,1,0:T(8,128)(2,1)} %param.4), channel_id=1, source_target_pairs={{0,6},{1,7},{2,0},{3,1},{4,2},{5,3},{6,4},{7,5},{8,14},{9,15},{10,... | collective-permute-start | bytes 786440 | tf_op jit(solution)/shard_map/ppermute | solution.py:282
  23.6 0.0 all-to-all-done
  23.6 0.0 copy-start.2
  23.6 0.7 shard_map.47
  24.4 13.1 %all-to-all-start.1 = ((s32[16,1,128]{2,1,0:T(1,128)}), s32[16,1,128]{2,1,0:T(1,128)S(1)}, u32[]{:S(2)}, u32[]{:S(2)}) async-start(s32[16,1,128]{2,1,0:T(1,128)} %bitcast.5), calls=%async_computation.1 | async-start | bytes 16384 | tf_op jit(solution)/shard_map/all_to_all | solution.py:29
  37.5 0.0 collective-permute-done.1
  37.5 0.0 collective-permute-done
  37.5 0.0 collective-permute-done.2
  37.5 0.0 copy-done.2
  37.6 0.1 pad_maximum_fusion.same_ref
  37.7 11.0 %all-to-all-done.1 = s32[16,1,128]{2,1,0:T(1,128)S(1)} async-done(((s32[16,1,128]{2,1,0:T(1,128)}), s32[16,1,128]{2,1,0:T(1,128)S(1)}, u32[]{:S(2)}, u32[]{:S(2)}) %all-to-all-start.1) | async-done | bytes 8224 | tf_op jit(solution)/shard_map/all_to_all | solution.py:29
  48.7 0.0 copy-start.1
  48.7 4.7 %collective-permute-start.3 = (bf16[128,32,128]{2,1,0:T(8,128)(2,1)S(1)}, bf16[128,32,128]{2,1,0:T(8,128)(2,1)S(1)}, u32[]{:S(2)}, u32[]{:S(2)}) collective-permute-start(bf16[128,32,128]{2,1,0:T(8,128)(2,1)S(1)} %pad_maximum_fusion.same_ref), channel_id=1, source_target_pairs={{0,1},{1,0},{2,3},{3,2},{4,5},{5,4},{6,7},{7,6},{8,9},{9,8},{10,11... | collective-permute-start | bytes 3145736 | tf_op jit(solution)/shard_map/ppermute | solution.py:297
  53.4 2.3 %collective-permute-done.3.other_ref = bf16[128,32,128]{2,1,0:T(8,128)(2,1)S(1)} collective-permute-done((bf16[128,32,128]{2,1,0:T(8,128)(2,1)S(1)}, bf16[128,32,128]{2,1,0:T(8,128)(2,1)S(1)}, u32[]{:S(2)}, u32[]{:S(2)}) %collective-permute-start.3) | collective-permute-done | bytes 1048608 | tf_op jit(solution)/shard_map/ppermute | solution.py:297
  55.7 4.6 %shard_map.48.x_ref = f32[16,128]{1,0:T(8,128)S(1)} custom-call(s32[64]{0:T(128)} %len_hbm.1, s32[16,128]{1,0:T(8,128)S(1)} %bitcast.20, bf16[128,32,128]{2,1,0:T(8,128)(2,1)S(1)} %pad_maximum_fusion.same_ref, bf16[128,32,128]{2,1,0:T(8,128)(2,1)S(1)} %collective-permute-done.3.other_ref, bf16[64,128,128]{2,1,0:T(8,128)(2,1)} %p_hbm.1), custom_call_target="tpu_custom_call" | custom-call | tf_op jit(solution)/shard_map/pallas_call | solution.py:299
  60.3 0.1 shard_map.49
  60.4 11.6 %all_to_all.45 = f32[32,1,128]{2,1,0:T(1,128)S(1)} all-to-all(f32[32,1,128]{2,1,0:T(1,128)S(1)} %bitcast.18), channel_id=1, replica_groups={{0,1,2,3,4,5,6,7,8,9,10,11,12,13,14,15,16,17,18,19,20,21,22,23,24,25,26..., dimensions={0} | all-to-all | bytes 32768 | tf_op jit(solution)/shard_map/all_to_all | solution.py:29
  72.0 0.1 shard_map.50
  72.1 13.9 %all_to_all.46 = f32[16,1,128]{2,1,0:T(1,128)S(1)} all-to-all(f32[16,1,128]{2,1,0:T(1,128)S(1)} %bitcast.21), channel_id=1, replica_groups={{0,32,64,96,128,160,192,224,256,288,320,352,384,416,448,480},{1,33,65,9..., dimensions={0} | all-to-all | bytes 16384 | tf_op jit(solution)/shard_map/all_to_all | solution.py:29
  85.9 0.0 copy-done.1
  85.9 1.0 %shard_map.51 = f32[16,32]{1,0:T(8,128)} custom-call(s32[16,32]{1,0:T(8,128)S(1)} %bitcast.23, s32[16,128]{1,0:T(8,128)S(1)} %get-tuple-element.9.key_ref, f32[16,128]{1,0:T(8,128)S(1)} %bitcast.24), custom_call_target="tpu_custom_call" | custom-call | tf_op jit(solution)/shard_map/pallas_call | solution.py:271
Async XLA Ops:
  0.0 0.7 copy-start
  1.9 21.7 %all-to-all-start = ((s32[32,1,128]{2,1,0:T(1,128)}), s32[32,1,128]{2,1,0:T(1,128)S(1)}, u32[]{:S(2)}, u32[]{:S(2)}) async-start(s32[32,1,128]{2,1,0:T(1,128)} %bitcast.2), calls=%async_computation | async-start | bytes 32768 | tf_op jit(solution)/shard_map/all_to_all | solution.py:29
  12.3 25.2 %collective-permute-start.1 = (bf16[32,32,128]{2,1,0:T(8,128)(2,1)}, bf16[32,32,128]{2,1,0:T(8,128)(2,1)S(1)}, u32[]{:S(2)}, u32[]{:S(2)}) collective-permute-start(bf16[32,32,128]{2,1,0:T(8,128)(2,1)} %param.4), channel_id=1, source_target_pairs={{0,4},{1,5},{2,6},{3,7},{4,0},{5,1},{6,2},{7,3},{8,12},{9,13},{10,... | collective-permute-start | bytes 786440 | tf_op jit(solution)/shard_map/ppermute | solution.py:282
  17.1 20.4 %collective-permute-start = (bf16[32,32,128]{2,1,0:T(8,128)(2,1)}, bf16[32,32,128]{2,1,0:T(8,128)(2,1)S(1)}, u32[]{:S(2)}, u32[]{:S(2)}) collective-permute-start(bf16[32,32,128]{2,1,0:T(8,128)(2,1)} %param.4), channel_id=1, source_target_pairs={{0,2},{1,3},{2,4},{3,5},{4,6},{5,7},{6,0},{7,1},{8,10},{9,11},{10,... | collective-permute-start | bytes 786440 | tf_op jit(solution)/shard_map/ppermute | solution.py:282
  19.3 18.2 %collective-permute-start.2 = (bf16[32,32,128]{2,1,0:T(8,128)(2,1)}, bf16[32,32,128]{2,1,0:T(8,128)(2,1)S(1)}, u32[]{:S(2)}, u32[]{:S(2)}) collective-permute-start(bf16[32,32,128]{2,1,0:T(8,128)(2,1)} %param.4), channel_id=1, source_target_pairs={{0,6},{1,7},{2,0},{3,1},{4,2},{5,3},{6,4},{7,5},{8,14},{9,15},{10,... | collective-permute-start | bytes 786440 | tf_op jit(solution)/shard_map/ppermute | solution.py:282
  23.6 13.9 %copy-start.2 = (bf16[32,32,128]{2,1,0:T(8,128)(2,1)S(1)}, bf16[32,32,128]{2,1,0:T(8,128)(2,1)}, u32[]{:S(2)}) copy-start(bf16[32,32,128]{2,1,0:T(8,128)(2,1)} %param.4) | copy-start | bytes 786436
  24.4 24.4 %all-to-all-start.1 = ((s32[16,1,128]{2,1,0:T(1,128)}), s32[16,1,128]{2,1,0:T(1,128)S(1)}, u32[]{:S(2)}, u32[]{:S(2)}) async-start(s32[16,1,128]{2,1,0:T(1,128)} %bitcast.5), calls=%async_computation.1 | async-start | bytes 16384 | tf_op jit(solution)/shard_map/all_to_all | solution.py:29
  48.7 37.2 %copy-start.1 = (s32[32,16]{0,1:T(8,128)S(1)}, s32[32,16]{0,1:T(8,128)}, u32[]{:S(2)}) copy-start(s32[32,16]{0,1:T(8,128)} %param.7) | copy-start | bytes 6148
  48.7 6.9 %collective-permute-start.3 = (bf16[128,32,128]{2,1,0:T(8,128)(2,1)S(1)}, bf16[128,32,128]{2,1,0:T(8,128)(2,1)S(1)}, u32[]{:S(2)}, u32[]{:S(2)}) collective-permute-start(bf16[128,32,128]{2,1,0:T(8,128)(2,1)S(1)} %pad_maximum_fusion.same_ref), channel_id=1, source_target_pairs={{0,1},{1,0},{2,3},{3,2},{4,5},{5,4},{6,7},{7,6},{8,9},{9,8},{10,11... | collective-permute-start | bytes 3145736 | tf_op jit(solution)/shard_map/ppermute | solution.py:297

commit v8 on v7

--- a/solution.py
+++ b/solution.py
@@ -99,19 +99,9 @@
     return lax.dot_general(a, b, (dims, ((), ())), preferred_element_type=jnp.float32)
 
 
-def score_kernel(
-    len_hbm, code_ref, same_ref, other_ref, p_hbm, o_ref,
-    len_ref, q_ref, p_ref, plan, plan_s, onehot, best, sem, len_sem, same_sem, other_sem, p_sem,
-):
-    len_copy = pltpu.make_async_copy(len_hbm, len_ref, len_sem)
-    len_copy.start()
+def sort_kernel(code_ref, p_hbm, plan_ref, dest_ref, p_ref, p_sem):
     p_copy = pltpu.make_async_copy(p_hbm, p_ref, p_sem)
     p_copy.start()
-    half = NQ // 2
-    same_copy = pltpu.make_async_copy(same_ref, q_ref.at[pl.ds(0, half)], same_sem)
-    same_copy.start()
-    other_copy = pltpu.make_async_copy(other_ref, q_ref.at[pl.ds(half, half)], other_sem)
-    other_copy.start()
     lane8 = iota((Q, 128), 1)
     code = jnp.where(lane8 < 64, code_ref[0:8, :], pltpu.roll(code_ref[8:16, :], 64, 1))
     valid = code >= 0
@@ -150,39 +140,54 @@
         axis=0,
     ).astype(jnp.int32)
 
-    g_iota = iota((GMAX, 128), 0)
+    dest_ref[...] = dest
     c_iota = iota((GROUP, 128), 0)
     named = []
     for q in range(Q):
-        d = dest[q : q + 1, :]
-        onehot[:, 128 * q : 128 * (q + 1)] = (
-            ((d >> 3) == g_iota).astype(jnp.float32).astype(jnp.bfloat16)
-        )
-        here = ((d & 7) == c_iota) & valid[q : q + 1, :]
+        here = ((dest[q : q + 1, :] & 7) == c_iota) & valid[q : q + 1, :]
         named.append(jnp.where(here, query[q : q + 1, :], 0).astype(jnp.float32))
     lists = dot(
-        jnp.concatenate(named, axis=1).astype(jnp.bfloat16), onehot[...], ((1,), (1,))
-    )
-    plan[0:GROUP, 0:GMAX] = lists.astype(jnp.int32)
+        jnp.concatenate(named, axis=1).astype(jnp.bfloat16), in_group(dest), ((1,), (1,))
+    )
+    plan_ref[0:GROUP, 0:GMAX] = lists.astype(jnp.int32)
+    plan_ref[0:GROUP, GMAX:256] = jnp.zeros((GROUP, 256 - GMAX), jnp.int32)
     g_lane = iota((BLK, 256), 1)
     ends2 = jnp.concatenate([ends, ends], axis=1)
     owner_block = jnp.minimum(
         jnp.sum((ends2 <= g_lane).astype(jnp.int32), axis=0, keepdims=True), BLK - 1
     )
     total = jnp.broadcast_to(ends2[BLK - 1 : BLK, :], (1, 256))
-    plan[GROUP : 2 * GROUP, :] = jnp.where(
+    plan_ref[GROUP : 2 * GROUP, :] = jnp.where(
         iota((GROUP, 256), 0) == 0,
         jnp.broadcast_to(owner_block, (GROUP, 256)),
         jnp.broadcast_to(total, (GROUP, 256)),
     )
+    p_copy.wait()
+
+
+def in_group(dest):
+    g_iota = iota((GMAX, 128), 0)
+    return jnp.concatenate(
+        [((dest[q : q + 1, :] >> 3) == g_iota).astype(jnp.float32) for q in range(Q)], axis=1
+    ).astype(jnp.bfloat16)
+
+
+def score_kernel(
+    len_hbm, plan, dest_ref, same_ref, other_ref, p_ref, o_ref, len_ref, plan_s, best, sem, len_sem
+):
+    len_copy = pltpu.make_async_copy(len_hbm, len_ref, len_sem)
+    len_copy.start()
     copy = pltpu.make_async_copy(plan, plan_s, sem)
     copy.start()
+    dest = dest_ref[...]
+    c_iota = iota((GROUP, 128), 0)
     best[...] = jnp.zeros((GMAX, GROUP * T), jnp.float32)
     copy.wait()
     len_copy.wait()
-    p_copy.wait()
-    same_copy.wait()
-    other_copy.wait()
+    half = NQ // 2
+
+    def rows_of(i):
+        return jnp.where(i < half, same_ref[i & (half - 1)], other_ref[i & (half - 1)])
 
     token = iota((PT, GROUP * T), 0)
 
@@ -191,7 +196,7 @@
         for u in range(UNROLL):
             g = it * UNROLL + u
             b = plan_s[GROUP, g]
-            rows_q = jnp.concatenate([q_ref[plan_s[c, g]] for c in range(GROUP)], axis=0)
+            rows_q = jnp.concatenate([rows_of(plan_s[c, g]) for c in range(GROUP)], axis=0)
             similar = dot(p_ref[b], rows_q, ((1,), (1,)))
             similar = jnp.where(token < len_ref[b], similar, -jnp.inf)
             rows.append(jnp.max(similar, axis=0, keepdims=True))
@@ -203,7 +208,7 @@
     w = (iota((GROUP, GROUP * T), 0) == (iota((GROUP, GROUP * T), 1) >> 5)).astype(jnp.float32)
     w = w.astype(jnp.bfloat16)
     means = sum(dot(w, part, ((1,), (1,))) for part in split3(best[...])) * (1.0 / T)
-    picked = dot(jnp.concatenate(split3(means), axis=0), onehot[...], ((1,), (0,)))
+    picked = dot(jnp.concatenate(split3(means), axis=0), in_group(dest), ((1,), (0,)))
     picked = picked[0:GROUP] + picked[GROUP : 2 * GROUP] + picked[2 * GROUP : 3 * GROUP]
     out = []
     for q in range(Q):
@@ -292,36 +297,40 @@
     hint = pl.CostEstimate(flops=10**11, transcendentals=0, bytes_accessed=2**20)
     got = small_call(by_z_kernel, pltpu.VMEM((Z, 128), jnp.int32), got, hint=hint)
     codes = exchange(got, Z_GROUPS)
+    _, *same = lax.optimization_barrier((got, *same))
     same = jnp.concatenate(same, axis=0)
-    codes, same = lax.optimization_barrier((codes, same))
     other = lax.ppermute(same, "query", [(k, k ^ 1) for k in range(Q)])
+    at = pltpu.with_memory_space_constraint
     hbm = pl.BlockSpec(memory_space=pltpu.HBM)
+    plan, dest, blocks = pl.pallas_call(
+        sort_kernel,
+        out_shape=(
+            pltpu.VMEM((2 * GROUP, 256), jnp.int32),
+            pltpu.VMEM((Q, 128), jnp.int32),
+            pltpu.VMEM(passages.shape, passages.dtype),
+        ),
+        in_specs=[VMEM, hbm],
+        out_specs=(VMEM, VMEM, VMEM),
+        scratch_shapes=[pltpu.SemaphoreType.DMA],
+        cost_estimate=pl.CostEstimate(flops=10**11, transcendentals=0, bytes_accessed=2**22),
+        compiler_params=pltpu.CompilerParams(vmem_limit_bytes=32 << 20),
+    )(at(codes, pltpu.VMEM), at(passages, pltpu.HBM))
     scores = pl.pallas_call(
         score_kernel,
         out_shape=pltpu.VMEM((Z, 128), jnp.float32),
-        in_specs=[hbm, VMEM, VMEM, VMEM, hbm],
+        in_specs=[hbm] + [VMEM] * 5,
         out_specs=VMEM,
         scratch_shapes=[
             pltpu.SMEM((BLK,), jnp.int32),
-            pltpu.VMEM((NQ, T, D), jnp.bfloat16),
-            pltpu.VMEM((BLK, PT, D), jnp.bfloat16),
-            pltpu.VMEM((2 * GROUP, 256), jnp.int32),
             pltpu.SMEM((2 * GROUP, 256), jnp.int32),
-            pltpu.VMEM((GMAX, Q * 128), jnp.bfloat16),
             pltpu.VMEM((GMAX, GROUP * T), jnp.float32),
-            pltpu.SemaphoreType.DMA,
-            pltpu.SemaphoreType.DMA,
-            pltpu.SemaphoreType.DMA,
             pltpu.SemaphoreType.DMA,
             pltpu.SemaphoreType.DMA,
         ],
         compiler_params=pltpu.CompilerParams(vmem_limit_bytes=32 << 20),
     )(
-        pltpu.with_memory_space_constraint(lengths, pltpu.HBM),
-        pltpu.with_memory_space_constraint(codes, pltpu.VMEM),
-        pltpu.with_memory_space_constraint(same, pltpu.VMEM),
-        pltpu.with_memory_space_constraint(other, pltpu.VMEM),
-        pltpu.with_memory_space_constraint(passages, pltpu.HBM),
+        at(lengths, pltpu.HBM),
+        *[at(x, pltpu.VMEM) for x in (plan, dest, same, other, blocks)],
     )
     back = small_call(by_plane_kernel, pltpu.VMEM((YQ, 128), jnp.float32), scores)
     back = exchange(back, YQ_GROUPS)

time: 87.4 us -> 85.4 us (0.977)
  waiting for transfers between devices: 13.3 us -> 7.64 us
  Pallas kernels: 7.77 us -> 10.4 us
  blocking collectives: 25.5 us -> 27.7 us
  starting transfers between devices: 39.5 us -> 38.2 us
    all_to_all x2, waiting for transfers between devices: 11 us -> 7.63 us  [exchange(): lax.all_to_all(x, ('index', 'query'), split_axis=0, concat_axis=0, tiled=...]
    all_to_all x2, blocking collectives: 25.5 us -> 27.7 us  [exchange(): lax.all_to_all(x, ('index', 'query'), split_axis=0, concat_axis=0, tiled=...]
    ppermute x1, waiting for transfers between devices: 2.26 us -> 0.01 us  [shards(): other = lax.ppermute(same, 'query', [(k, k ^ 1) for k in range(Q)])]
    pallas_call x0 -> x1, Pallas kernels: none -> 1.6 us  [shards(): pl.pallas_call(sort_kernel, out_shape=(pltpu.VMEM((2 * GROUP, 256), jnp.i...]
    ppermute x1, starting transfers between devices: 4.66 us -> 3.39 us  [shards(): other = lax.ppermute(same, 'query', [(k, k ^ 1) for k in range(Q)])]
    pallas_call x1, Pallas kernels: 4.62 us -> 5.65 us  [shards(): pl.pallas_call(score_kernel, out_shape=pltpu.VMEM((Z, 128), jnp.float32),...]
  transfers between devices with their start and end apart: 6 -> 6, of which waited for: 2 -> 1; matrix products, arithmetic and copies ran while one was open for 0% -> 0% of each run, Pallas kernels for 1% -> 3%
where the time goes in v8:
time: 85.4 us; the launch traced here: 84.9 us
  starting transfers between devices  38.2 us (45%)
  blocking collectives  27.7 us (32%)
  Pallas kernels  10.4 us (12%)
  waiting for transfers between devices  7.64 us (9%)
    all_to_all x2, blocking collectives, exchange(): lax.all_to_all(x, ('index', 'query'), split_axis=0, concat_axis=0, tiled=...  27.7 us
    all_to_all x2, starting transfers between devices, exchange(): lax.all_to_all(x, ('index', 'query'), split_axis=0, concat_axis=0, tiled=...  23.5 us
    ppermute x3, starting transfers between devices, shards(): lax.ppermute(queries, 'query', [(k, (k + 2 * d) % Q) for k in range(Q)])  11.3 us
    all_to_all x2, waiting for transfers between devices, exchange(): lax.all_to_all(x, ('index', 'query'), split_axis=0, concat_axis=0, tiled=...  7.63 us
    pallas_call x1, Pallas kernels, shards(): pl.pallas_call(score_kernel, out_shape=pltpu.VMEM((Z, 128), jnp.float32),...  5.65 us
    ppermute x1, starting transfers between devices, shards(): other = lax.ppermute(same, 'query', [(k, k ^ 1) for k in range(Q)])  3.39 us
    pallas_call x5, Pallas kernels, small_call(): pl.pallas_call(kernel, cost_estimate=hint, out_shape=out_shape, in_specs=...  3.14 us
  transfers between devices with their start and end apart: 6, of which 1 were waited for; matrix products, arithmetic and copies ran while one was open for 0% of the time, Pallas kernels for 3%

profile of v8, /device:TPU:1, one launch (start us, length us, event | category | flops | bytes accessed | tf_op | source)
XLA Modules:
  0.0 84.9 jit_solution(14793551054656658777)
XLA Ops:
  0.0 0.0 copy-start
  0.0 0.7 copy-done
  0.7 1.2 %shard_map.46 = (s32[32,128]{1,0:T(8,128)}, s32[16,128]{1,0:T(8,128)S(1)}) custom-call(s32[16,32]{1,0:T(8,128)S(1)} %bitcast.21), custom_call_target="tpu_custom_call" | custom-call | tf_op jit(solution)/shard_map/pallas_call | solution.py:276
  1.9 10.3 %all-to-all-start = ((s32[32,1,128]{2,1,0:T(1,128)}), s32[32,1,128]{2,1,0:T(1,128)S(1)}, u32[]{:S(2)}, u32[]{:S(2)}) async-start(s32[32,1,128]{2,1,0:T(1,128)} %bitcast.2), calls=%async_computation | async-start | bytes 32768 | tf_op jit(solution)/shard_map/all_to_all | solution.py:29
  12.2 4.8 %collective-permute-start.1 = (bf16[32,32,128]{2,1,0:T(8,128)(2,1)}, bf16[32,32,128]{2,1,0:T(8,128)(2,1)S(1)}, u32[]{:S(2)}, u32[]{:S(2)}) collective-permute-start(bf16[32,32,128]{2,1,0:T(8,128)(2,1)} %param.4), channel_id=1, source_target_pairs={{0,4},{1,5},{2,6},{3,7},{4,0},{5,1},{6,2},{7,3},{8,12},{9,13},{10,... | collective-permute-start | bytes 786440 | tf_op jit(solution)/shard_map/ppermute | solution.py:287
  17.1 2.2 %collective-permute-start = (bf16[32,32,128]{2,1,0:T(8,128)(2,1)}, bf16[32,32,128]{2,1,0:T(8,128)(2,1)S(1)}, u32[]{:S(2)}, u32[]{:S(2)}) collective-permute-start(bf16[32,32,128]{2,1,0:T(8,128)(2,1)} %param.4), channel_id=1, source_target_pairs={{0,2},{1,3},{2,4},{3,5},{4,6},{5,7},{6,0},{7,1},{8,10},{9,11},{10,... | collective-permute-start | bytes 786440 | tf_op jit(solution)/shard_map/ppermute | solution.py:287
  19.3 4.3 %collective-permute-start.2 = (bf16[32,32,128]{2,1,0:T(8,128)(2,1)}, bf16[32,32,128]{2,1,0:T(8,128)(2,1)S(1)}, u32[]{:S(2)}, u32[]{:S(2)}) collective-permute-start(bf16[32,32,128]{2,1,0:T(8,128)(2,1)} %param.4), channel_id=1, source_target_pairs={{0,6},{1,7},{2,0},{3,1},{4,2},{5,3},{6,4},{7,5},{8,14},{9,15},{10,... | collective-permute-start | bytes 786440 | tf_op jit(solution)/shard_map/ppermute | solution.py:287
  23.6 0.0 all-to-all-done
  23.6 0.0 copy-start.2
  23.6 0.7 shard_map.47
  24.3 13.2 %all-to-all-start.1 = ((s32[16,1,128]{2,1,0:T(1,128)}), s32[16,1,128]{2,1,0:T(1,128)S(1)}, u32[]{:S(2)}, u32[]{:S(2)}) async-start(s32[16,1,128]{2,1,0:T(1,128)} %bitcast.5), calls=%async_computation.1 | async-start | bytes 16384 | tf_op jit(solution)/shard_map/all_to_all | solution.py:29
  37.5 0.0 collective-permute-done.1
  37.5 0.0 collective-permute-done
  37.5 0.0 collective-permute-done.2
  37.5 0.0 copy-done.2
  37.7 3.4 %collective-permute-start.3 = (bf16[128,32,128]{2,1,0:T(8,128)(2,1)S(1)}, bf16[128,32,128]{2,1,0:T(8,128)(2,1)S(1)}, u32[]{:S(2)}, u32[]{:S(2)}) collective-permute-start(bf16[128,32,128]{2,1,0:T(8,128)(2,1)S(1)} %constant_dynamic-update-slice_fusion.same_ref), channel_id=1, source_target_pairs={{0,1},{1,0},{2,3},{3,2},{4,5},{5,4},{6,7},{7,6},{8,9},{9,8},{10,11... | collective-permute-start | bytes 3145736 | tf_op jit(solution)/shard_map/ppermute | solution.py:302
  41.1 7.6 %all-to-all-done.1 = s32[16,1,128]{2,1,0:T(1,128)S(1)} async-done(((s32[16,1,128]{2,1,0:T(1,128)}), s32[16,1,128]{2,1,0:T(1,128)S(1)}, u32[]{:S(2)}, u32[]{:S(2)}) %all-to-all-start.1) | async-done | bytes 8224 | tf_op jit(solution)/shard_map/all_to_all | solution.py:29
  48.7 1.6 %shard_map.48 = (s32[16,256]{1,0:T(8,128)S(1)}, s32[8,128]{1,0:T(8,128)S(1)}, bf16[64,128,128]{2,1,0:T(8,128)(2,1)S(1)}) custom-call(s32[16,128]{1,0:T(8,128)S(1)} %bitcast.25, bf16[64,128,128]{2,1,0:T(8,128)(2,1)} %p_hbm.1), custom_call_target="tpu_custom_call" | custom-call | flops 99999997952 | bytes 4194304 | tf_op jit(solution)/shard_map/pallas_call | solution.py:305
  50.3 0.0 collective-permute-done.3.other_ref
  50.4 0.0 copy-start.1
  50.4 5.6 %shard_map.49.x_ref = f32[16,128]{1,0:T(8,128)S(1)} custom-call(s32[64]{0:T(128)} %len_hbm.1, s32[16,256]{1,0:T(8,128)S(1)} %get-tuple-element.16.plan, s32[8,128]{1,0:T(8,128)S(1)} %get-tuple-element.17.dest_ref, bf16[128,32,128]{2,1,0:T(8,128)(2,1)S(1)} %constant_dynamic-update-slice_fusion.same_ref, ...), custom_call_target="tpu_custom_call" | custom-call | tf_op jit(solution)/shard_map/pallas_call | solution.py:318
  56.0 0.1 shard_map.50
  56.1 13.9 %all_to_all.44 = f32[32,1,128]{2,1,0:T(1,128)S(1)} all-to-all(f32[32,1,128]{2,1,0:T(1,128)S(1)} %bitcast.18), channel_id=1, replica_groups={{0,1,2,3,4,5,6,7,8,9,10,11,12,13,14,15,16,17,18,19,20,21,22,23,24,25,26..., dimensions={0} | all-to-all | bytes 32768 | tf_op jit(solution)/shard_map/all_to_all | solution.py:29
  70.0 0.1 shard_map.51
  70.0 13.9 %all_to_all.45 = f32[16,1,128]{2,1,0:T(1,128)S(1)} all-to-all(f32[16,1,128]{2,1,0:T(1,128)S(1)} %bitcast.20), channel_id=1, replica_groups={{0,32,64,96,128,160,192,224,256,288,320,352,384,416,448,480},{1,33,65,9..., dimensions={0} | all-to-all | bytes 16384 | tf_op jit(solution)/shard_map/all_to_all | solution.py:29
  83.9 0.0 copy-done.1
  83.9 1.0 %shard_map.52 = f32[16,32]{1,0:T(8,128)} custom-call(s32[16,32]{1,0:T(8,128)S(1)} %bitcast.22, s32[16,128]{1,0:T(8,128)S(1)} %get-tuple-element.14.key_ref, f32[16,128]{1,0:T(8,128)S(1)} %bitcast.23), custom_call_target="tpu_custom_call" | custom-call | tf_op jit(solution)/shard_map/pallas_call | solution.py:276
  (4 shorter events, 0.1 us)
Async XLA Ops:
  0.0 0.7 copy-start
  1.9 21.7 %all-to-all-start = ((s32[32,1,128]{2,1,0:T(1,128)}), s32[32,1,128]{2,1,0:T(1,128)S(1)}, u32[]{:S(2)}, u32[]{:S(2)}) async-start(s32[32,1,128]{2,1,0:T(1,128)} %bitcast.2), calls=%async_computation | async-start | bytes 32768 | tf_op jit(solution)/shard_map/all_to_all | solution.py:29
  12.2 25.3 %collective-permute-start.1 = (bf16[32,32,128]{2,1,0:T(8,128)(2,1)}, bf16[32,32,128]{2,1,0:T(8,128)(2,1)S(1)}, u32[]{:S(2)}, u32[]{:S(2)}) collective-permute-start(bf16[32,32,128]{2,1,0:T(8,128)(2,1)} %param.4), channel_id=1, source_target_pairs={{0,4},{1,5},{2,6},{3,7},{4,0},{5,1},{6,2},{7,3},{8,12},{9,13},{10,... | collective-permute-start | bytes 786440 | tf_op jit(solution)/shard_map/ppermute | solution.py:287
  17.1 20.5 %collective-permute-start = (bf16[32,32,128]{2,1,0:T(8,128)(2,1)}, bf16[32,32,128]{2,1,0:T(8,128)(2,1)S(1)}, u32[]{:S(2)}, u32[]{:S(2)}) collective-permute-start(bf16[32,32,128]{2,1,0:T(8,128)(2,1)} %param.4), channel_id=1, source_target_pairs={{0,2},{1,3},{2,4},{3,5},{4,6},{5,7},{6,0},{7,1},{8,10},{9,11},{10,... | collective-permute-start | bytes 786440 | tf_op jit(solution)/shard_map/ppermute | solution.py:287
  19.3 18.3 %collective-permute-start.2 = (bf16[32,32,128]{2,1,0:T(8,128)(2,1)}, bf16[32,32,128]{2,1,0:T(8,128)(2,1)S(1)}, u32[]{:S(2)}, u32[]{:S(2)}) collective-permute-start(bf16[32,32,128]{2,1,0:T(8,128)(2,1)} %param.4), channel_id=1, source_target_pairs={{0,6},{1,7},{2,0},{3,1},{4,2},{5,3},{6,4},{7,5},{8,14},{9,15},{10,... | collective-permute-start | bytes 786440 | tf_op jit(solution)/shard_map/ppermute | solution.py:287
  23.6 14.0 %copy-start.2 = (bf16[32,32,128]{2,1,0:T(8,128)(2,1)S(1)}, bf16[32,32,128]{2,1,0:T(8,128)(2,1)}, u32[]{:S(2)}) copy-start(bf16[32,32,128]{2,1,0:T(8,128)(2,1)} %param.4) | copy-start | bytes 786436
  24.3 24.4 %all-to-all-start.1 = ((s32[16,1,128]{2,1,0:T(1,128)}), s32[16,1,128]{2,1,0:T(1,128)S(1)}, u32[]{:S(2)}, u32[]{:S(2)}) async-start(s32[16,1,128]{2,1,0:T(1,128)} %bitcast.5), calls=%async_computation.1 | async-start | bytes 16384 | tf_op jit(solution)/shard_map/all_to_all | solution.py:29
  37.7 12.6 %collective-permute-start.3 = (bf16[128,32,128]{2,1,0:T(8,128)(2,1)S(1)}, bf16[128,32,128]{2,1,0:T(8,128)(2,1)S(1)}, u32[]{:S(2)}, u32[]{:S(2)}) collective-permute-start(bf16[128,32,128]{2,1,0:T(8,128)(2,1)S(1)} %constant_dynamic-update-slice_fusion.same_ref), channel_id=1, source_target_pairs={{0,1},{1,0},{2,3},{3,2},{4,5},{5,4},{6,7},{7,6},{8,9},{9,8},{10,11... | collective-permute-start | bytes 3145736 | tf_op jit(solution)/shard_map/ppermute | solution.py:302
  50.4 33.6 %copy-start.1 = (s32[32,16]{0,1:T(8,128)S(1)}, s32[32,16]{0,1:T(8,128)}, u32[]{:S(2)}) copy-start(s32[32,16]{0,1:T(8,128)} %param.7) | copy-start | bytes 6148

commit v9 on v8

--- a/solution.py
+++ b/solution.py
@@ -99,7 +99,11 @@
     return lax.dot_general(a, b, (dims, ((), ())), preferred_element_type=jnp.float32)
 
 
-def sort_kernel(code_ref, p_hbm, plan_ref, dest_ref, p_ref, p_sem):
+def sort_kernel(
+    code_ref, p_hbm, same_ref, plan_ref, dest_ref, onehot_ref, p_ref, q_ref, p_sem, q_sem
+):
+    q_copy = pltpu.make_async_copy(same_ref, q_ref.at[pl.ds(0, NQ // 2)], q_sem)
+    q_copy.start()
     p_copy = pltpu.make_async_copy(p_hbm, p_ref, p_sem)
     p_copy.start()
     lane8 = iota((Q, 128), 1)
@@ -146,8 +150,10 @@
     for q in range(Q):
         here = ((dest[q : q + 1, :] & 7) == c_iota) & valid[q : q + 1, :]
         named.append(jnp.where(here, query[q : q + 1, :], 0).astype(jnp.float32))
+    onehot = in_group(dest)
+    onehot_ref[...] = onehot
     lists = dot(
-        jnp.concatenate(named, axis=1).astype(jnp.bfloat16), in_group(dest), ((1,), (1,))
+        jnp.concatenate(named, axis=1).astype(jnp.bfloat16), onehot, ((1,), (1,))
     )
     plan_ref[0:GROUP, 0:GMAX] = lists.astype(jnp.int32)
     plan_ref[0:GROUP, GMAX:256] = jnp.zeros((GROUP, 256 - GMAX), jnp.int32)
@@ -163,6 +169,7 @@
         jnp.broadcast_to(total, (GROUP, 256)),
     )
     p_copy.wait()
+    q_copy.wait()
 
 
 def in_group(dest):
@@ -173,8 +180,12 @@
 
 
 def score_kernel(
-    len_hbm, plan, dest_ref, same_ref, other_ref, p_ref, o_ref, len_ref, plan_s, best, sem, len_sem
+    len_hbm, plan, dest_ref, onehot_ref, other_ref, p_ref, _, o_ref, q_ref,
+    len_ref, plan_s, best, sem, len_sem, q_sem,
 ):
+    half = NQ // 2
+    q_copy = pltpu.make_async_copy(other_ref, q_ref.at[pl.ds(half, half)], q_sem)
+    q_copy.start()
     len_copy = pltpu.make_async_copy(len_hbm, len_ref, len_sem)
     len_copy.start()
     copy = pltpu.make_async_copy(plan, plan_s, sem)
@@ -184,10 +195,7 @@
     best[...] = jnp.zeros((GMAX, GROUP * T), jnp.float32)
     copy.wait()
     len_copy.wait()
-    half = NQ // 2
-
-    def rows_of(i):
-        return jnp.where(i < half, same_ref[i & (half - 1)], other_ref[i & (half - 1)])
+    q_copy.wait()
 
     token = iota((PT, GROUP * T), 0)
 
@@ -196,7 +204,7 @@
         for u in range(UNROLL):
             g = it * UNROLL + u
             b = plan_s[GROUP, g]
-            rows_q = jnp.concatenate([rows_of(plan_s[c, g]) for c in range(GROUP)], axis=0)
+            rows_q = jnp.concatenate([q_ref[plan_s[c, g]] for c in range(GROUP)], axis=0)
             similar = dot(p_ref[b], rows_q, ((1,), (1,)))
             similar = jnp.where(token < len_ref[b], similar, -jnp.inf)
             rows.append(jnp.max(similar, axis=0, keepdims=True))
@@ -208,7 +216,7 @@
     w = (iota((GROUP, GROUP * T), 0) == (iota((GROUP, GROUP * T), 1) >> 5)).astype(jnp.float32)
     w = w.astype(jnp.bfloat16)
     means = sum(dot(w, part, ((1,), (1,))) for part in split3(best[...])) * (1.0 / T)
-    picked = dot(jnp.concatenate(split3(means), axis=0), in_group(dest), ((1,), (0,)))
+    picked = dot(jnp.concatenate(split3(means), axis=0), onehot_ref[...], ((1,), (0,)))
     picked = picked[0:GROUP] + picked[GROUP : 2 * GROUP] + picked[2 * GROUP : 3 * GROUP]
     out = []
     for q in range(Q):
@@ -302,35 +310,40 @@
     other = lax.ppermute(same, "query", [(k, k ^ 1) for k in range(Q)])
     at = pltpu.with_memory_space_constraint
     hbm = pl.BlockSpec(memory_space=pltpu.HBM)
-    plan, dest, blocks = pl.pallas_call(
+    every = pltpu.VMEM((NQ, T, D), queries.dtype)
+    plan, dest, onehot, blocks, gathered = pl.pallas_call(
         sort_kernel,
         out_shape=(
             pltpu.VMEM((2 * GROUP, 256), jnp.int32),
             pltpu.VMEM((Q, 128), jnp.int32),
+            pltpu.VMEM((GMAX, Q * 128), jnp.bfloat16),
             pltpu.VMEM(passages.shape, passages.dtype),
+            every,
         ),
-        in_specs=[VMEM, hbm],
-        out_specs=(VMEM, VMEM, VMEM),
-        scratch_shapes=[pltpu.SemaphoreType.DMA],
+        in_specs=[VMEM, hbm, VMEM],
+        out_specs=(VMEM,) * 5,
+        scratch_shapes=[pltpu.SemaphoreType.DMA, pltpu.SemaphoreType.DMA],
         cost_estimate=pl.CostEstimate(flops=10**11, transcendentals=0, bytes_accessed=2**22),
         compiler_params=pltpu.CompilerParams(vmem_limit_bytes=32 << 20),
-    )(at(codes, pltpu.VMEM), at(passages, pltpu.HBM))
-    scores = pl.pallas_call(
+    )(at(codes, pltpu.VMEM), at(passages, pltpu.HBM), at(same, pltpu.VMEM))
+    scores, _ = pl.pallas_call(
         score_kernel,
-        out_shape=pltpu.VMEM((Z, 128), jnp.float32),
-        in_specs=[hbm] + [VMEM] * 5,
-        out_specs=VMEM,
+        out_shape=(pltpu.VMEM((Z, 128), jnp.float32), every),
+        in_specs=[hbm] + [VMEM] * 6,
+        out_specs=(VMEM, VMEM),
+        input_output_aliases={6: 1},
         scratch_shapes=[
             pltpu.SMEM((BLK,), jnp.int32),
             pltpu.SMEM((2 * GROUP, 256), jnp.int32),
             pltpu.VMEM((GMAX, GROUP * T), jnp.float32),
             pltpu.SemaphoreType.DMA,
             pltpu.SemaphoreType.DMA,
+            pltpu.SemaphoreType.DMA,
         ],
         compiler_params=pltpu.CompilerParams(vmem_limit_bytes=32 << 20),
     )(
         at(lengths, pltpu.HBM),
-        *[at(x, pltpu.VMEM) for x in (plan, dest, same, other, blocks)],
+        *[at(x, pltpu.VMEM) for x in (plan, dest, onehot, other, blocks, gathered)],
     )
     back = small_call(by_plane_kernel, pltpu.VMEM((YQ, 128), jnp.float32), scores)
     back = exchange(back, YQ_GROUPS)

time: 85.4 us -> 83.5 us (0.978)
  Pallas kernels: 10.4 us -> 8.55 us
    pallas_call x1, Pallas kernels: 5.65 us -> 3.72 us  [shards(): pl.pallas_call(score_kernel, out_shape=(pltpu.VMEM((Z, 128), jnp.float32)...]
where the time goes in v9:
time: 83.5 us; the launch traced here: 83.1 us
  starting transfers between devices  38.2 us (46%)
  blocking collectives  27.7 us (33%)
  Pallas kernels  8.55 us (10%)
  waiting for transfers between devices  7.64 us (9%)
  local copies, waits for them, and re-layouts  0.84 us (1%)
    all_to_all x2, blocking collectives, exchange(): lax.all_to_all(x, ('index', 'query'), split_axis=0, concat_axis=0, tiled=...  27.7 us
    all_to_all x2, starting transfers between devices, exchange(): lax.all_to_all(x, ('index', 'query'), split_axis=0, concat_axis=0, tiled=...  23.5 us
    ppermute x3, starting transfers between devices, shards(): lax.ppermute(queries, 'query', [(k, (k + 2 * d) % Q) for k in range(Q)])  11.3 us
    all_to_all x2, waiting for transfers between devices, exchange(): lax.all_to_all(x, ('index', 'query'), split_axis=0, concat_axis=0, tiled=...  7.63 us
    pallas_call x1, Pallas kernels, shards(): pl.pallas_call(score_kernel, out_shape=(pltpu.VMEM((Z, 128), jnp.float32)...  3.72 us
    ppermute x1, starting transfers between devices, shards(): other = lax.ppermute(same, 'query', [(k, k ^ 1) for k in range(Q)])  3.39 us
    pallas_call x5, Pallas kernels, small_call(): pl.pallas_call(kernel, cost_estimate=hint, out_shape=out_shape, in_specs=...  3.15 us
    pallas_call x1, Pallas kernels, shards(): pl.pallas_call(sort_kernel, out_shape=(pltpu.VMEM((2 * GROUP, 256), jnp.i...  1.68 us
  transfers between devices with their start and end apart: 6, of which 1 were waited for; matrix products, arithmetic and copies ran while one was open for 0% of the time, Pallas kernels for 3%

profile of v9, /device:TPU:1, one launch (start us, length us, event | category | flops | bytes accessed | tf_op | source)
XLA Modules:
  0.0 83.1 jit_solution(618696901043696280)
XLA Ops:
  0.0 0.0 copy-start
  0.0 0.7 copy-done
  0.7 1.2 %shard_map.46 = (s32[32,128]{1,0:T(8,128)}, s32[16,128]{1,0:T(8,128)S(1)}) custom-call(s32[16,32]{1,0:T(8,128)S(1)} %bitcast.21), custom_call_target="tpu_custom_call" | custom-call | tf_op jit(solution)/shard_map/pallas_call | solution.py:284
  1.9 10.3 %all-to-all-start = ((s32[32,1,128]{2,1,0:T(1,128)}), s32[32,1,128]{2,1,0:T(1,128)S(1)}, u32[]{:S(2)}, u32[]{:S(2)}) async-start(s32[32,1,128]{2,1,0:T(1,128)} %bitcast.2), calls=%async_computation | async-start | bytes 32768 | tf_op jit(solution)/shard_map/all_to_all | solution.py:29
  12.2 4.8 %collective-permute-start.1 = (bf16[32,32,128]{2,1,0:T(8,128)(2,1)}, bf16[32,32,128]{2,1,0:T(8,128)(2,1)S(1)}, u32[]{:S(2)}, u32[]{:S(2)}) collective-permute-start(bf16[32,32,128]{2,1,0:T(8,128)(2,1)} %param.4), channel_id=1, source_target_pairs={{0,4},{1,5},{2,6},{3,7},{4,0},{5,1},{6,2},{7,3},{8,12},{9,13},{10,... | collective-permute-start | bytes 786440 | tf_op jit(solution)/shard_map/ppermute | solution.py:295
  17.1 2.2 %collective-permute-start = (bf16[32,32,128]{2,1,0:T(8,128)(2,1)}, bf16[32,32,128]{2,1,0:T(8,128)(2,1)S(1)}, u32[]{:S(2)}, u32[]{:S(2)}) collective-permute-start(bf16[32,32,128]{2,1,0:T(8,128)(2,1)} %param.4), channel_id=1, source_target_pairs={{0,2},{1,3},{2,4},{3,5},{4,6},{5,7},{6,0},{7,1},{8,10},{9,11},{10,... | collective-permute-start | bytes 786440 | tf_op jit(solution)/shard_map/ppermute | solution.py:295
  19.3 4.3 %collective-permute-start.2 = (bf16[32,32,128]{2,1,0:T(8,128)(2,1)}, bf16[32,32,128]{2,1,0:T(8,128)(2,1)S(1)}, u32[]{:S(2)}, u32[]{:S(2)}) collective-permute-start(bf16[32,32,128]{2,1,0:T(8,128)(2,1)} %param.4), channel_id=1, source_target_pairs={{0,6},{1,7},{2,0},{3,1},{4,2},{5,3},{6,4},{7,5},{8,14},{9,15},{10,... | collective-permute-start | bytes 786440 | tf_op jit(solution)/shard_map/ppermute | solution.py:295
  23.6 0.0 all-to-all-done
  23.6 0.0 copy-start.2
  23.6 0.7 shard_map.47
  24.3 13.2 %all-to-all-start.1 = ((s32[16,1,128]{2,1,0:T(1,128)}), s32[16,1,128]{2,1,0:T(1,128)S(1)}, u32[]{:S(2)}, u32[]{:S(2)}) async-start(s32[16,1,128]{2,1,0:T(1,128)} %bitcast.5), calls=%async_computation.1 | async-start | bytes 16384 | tf_op jit(solution)/shard_map/all_to_all | solution.py:29
  37.5 0.0 collective-permute-done.1
  37.5 0.0 collective-permute-done
  37.5 0.0 collective-permute-done.2
  37.5 0.0 copy-done.2
  37.7 3.4 %collective-permute-start.3 = (bf16[128,32,128]{2,1,0:T(8,128)(2,1)S(1)}, bf16[128,32,128]{2,1,0:T(8,128)(2,1)S(1)}, u32[]{:S(2)}, u32[]{:S(2)}) collective-permute-start(bf16[128,32,128]{2,1,0:T(8,128)(2,1)S(1)} %constant_dynamic-update-slice_fusion.same_ref), channel_id=1, source_target_pairs={{0,1},{1,0},{2,3},{3,2},{4,5},{5,4},{6,7},{7,6},{8,9},{9,8},{10,11... | collective-permute-start | bytes 3145736 | tf_op jit(solution)/shard_map/ppermute | solution.py:310
  41.1 7.6 %all-to-all-done.1 = s32[16,1,128]{2,1,0:T(1,128)S(1)} async-done(((s32[16,1,128]{2,1,0:T(1,128)}), s32[16,1,128]{2,1,0:T(1,128)S(1)}, u32[]{:S(2)}, u32[]{:S(2)}) %all-to-all-start.1) | async-done | bytes 8224 | tf_op jit(solution)/shard_map/all_to_all | solution.py:29
  48.7 1.7 %shard_map.48 = (s32[16,256]{1,0:T(8,128)S(1)}, s32[8,128]{1,0:T(8,128)S(1)}, bf16[192,1024]{1,0:T(8,128)(2,1)S(1)}, bf16[64,128,128]{2,1,0:T(8,128)(2,1)S(1)}, bf16[256,32,128]{2,1,0:T(8,128)(2,1)S(1)}) custom-call(s32[16,128]{1,0:T(8,128)S(1)} %bitcast.25, bf16[64,128,128]{2,1,0:T(8,128)(2,1)} %p_hbm.1, ...), custom_call_target="tpu_custom_call" | custom-call | flops 99999997952 | bytes 4194304 | tf_op jit(solution)/shard_map/pallas_call | solution.py:314
  50.4 0.0 collective-permute-done.3.other_ref
  50.4 0.0 copy-start.1
  50.5 3.7 %shard_map.49 = (f32[16,128]{1,0:T(8,128)S(1)}, bf16[256,32,128]{2,1,0:T(8,128)(2,1)S(1)}) custom-call(s32[64]{0:T(128)} %len_hbm.1, s32[16,256]{1,0:T(8,128)S(1)} %get-tuple-element.23.plan, s32[8,128]{1,0:T(8,128)S(1)} %get-tuple-element.24.dest_ref, bf16[192,1024]{1,0:T(8,128)(2,1)S(1)} %get-tuple-element.25.onehot_ref, ...), custom_call_target="tpu_custom_call", output_to_operand_aliasing={{1}: (6, {})} | custom-call | tf_op jit(solution)/shard_map/pallas_call | solution.py:329
  54.2 0.1 shard_map.50
  54.3 13.8 %all_to_all.44 = f32[32,1,128]{2,1,0:T(1,128)S(1)} all-to-all(f32[32,1,128]{2,1,0:T(1,128)S(1)} %bitcast.18), channel_id=1, replica_groups={{0,1,2,3,4,5,6,7,8,9,10,11,12,13,14,15,16,17,18,19,20,21,22,23,24,25,26..., dimensions={0} | all-to-all | bytes 32768 | tf_op jit(solution)/shard_map/all_to_all | solution.py:29
  68.1 0.1 shard_map.51
  68.2 13.9 %all_to_all.45 = f32[16,1,128]{2,1,0:T(1,128)S(1)} all-to-all(f32[16,1,128]{2,1,0:T(1,128)S(1)} %bitcast.20), channel_id=1, replica_groups={{0,32,64,96,128,160,192,224,256,288,320,352,384,416,448,480},{1,33,65,9..., dimensions={0} | all-to-all | bytes 16384 | tf_op jit(solution)/shard_map/all_to_all | solution.py:29
  82.1 0.0 copy-done.1
  82.1 1.0 %shard_map.52 = f32[16,32]{1,0:T(8,128)} custom-call(s32[16,32]{1,0:T(8,128)S(1)} %bitcast.22, s32[16,128]{1,0:T(8,128)S(1)} %get-tuple-element.17.key_ref, f32[16,128]{1,0:T(8,128)S(1)} %bitcast.23), custom_call_target="tpu_custom_call" | custom-call | tf_op jit(solution)/shard_map/pallas_call | solution.py:284
  (4 shorter events, 0.1 us)
Async XLA Ops:
  0.0 0.7 copy-start
  1.9 21.7 %all-to-all-start = ((s32[32,1,128]{2,1,0:T(1,128)}), s32[32,1,128]{2,1,0:T(1,128)S(1)}, u32[]{:S(2)}, u32[]{:S(2)}) async-start(s32[32,1,128]{2,1,0:T(1,128)} %bitcast.2), calls=%async_computation | async-start | bytes 32768 | tf_op jit(solution)/shard_map/all_to_all | solution.py:29
  12.2 25.3 %collective-permute-start.1 = (bf16[32,32,128]{2,1,0:T(8,128)(2,1)}, bf16[32,32,128]{2,1,0:T(8,128)(2,1)S(1)}, u32[]{:S(2)}, u32[]{:S(2)}) collective-permute-start(bf16[32,32,128]{2,1,0:T(8,128)(2,1)} %param.4), channel_id=1, source_target_pairs={{0,4},{1,5},{2,6},{3,7},{4,0},{5,1},{6,2},{7,3},{8,12},{9,13},{10,... | collective-permute-start | bytes 786440 | tf_op jit(solution)/shard_map/ppermute | solution.py:295
  17.1 20.5 %collective-permute-start = (bf16[32,32,128]{2,1,0:T(8,128)(2,1)}, bf16[32,32,128]{2,1,0:T(8,128)(2,1)S(1)}, u32[]{:S(2)}, u32[]{:S(2)}) collective-permute-start(bf16[32,32,128]{2,1,0:T(8,128)(2,1)} %param.4), channel_id=1, source_target_pairs={{0,2},{1,3},{2,4},{3,5},{4,6},{5,7},{6,0},{7,1},{8,10},{9,11},{10,... | collective-permute-start | bytes 786440 | tf_op jit(solution)/shard_map/ppermute | solution.py:295
  19.3 18.3 %collective-permute-start.2 = (bf16[32,32,128]{2,1,0:T(8,128)(2,1)}, bf16[32,32,128]{2,1,0:T(8,128)(2,1)S(1)}, u32[]{:S(2)}, u32[]{:S(2)}) collective-permute-start(bf16[32,32,128]{2,1,0:T(8,128)(2,1)} %param.4), channel_id=1, source_target_pairs={{0,6},{1,7},{2,0},{3,1},{4,2},{5,3},{6,4},{7,5},{8,14},{9,15},{10,... | collective-permute-start | bytes 786440 | tf_op jit(solution)/shard_map/ppermute | solution.py:295
  23.6 14.0 %copy-start.2 = (bf16[32,32,128]{2,1,0:T(8,128)(2,1)S(1)}, bf16[32,32,128]{2,1,0:T(8,128)(2,1)}, u32[]{:S(2)}) copy-start(bf16[32,32,128]{2,1,0:T(8,128)(2,1)} %param.4) | copy-start | bytes 786436
  24.3 24.4 %all-to-all-start.1 = ((s32[16,1,128]{2,1,0:T(1,128)}), s32[16,1,128]{2,1,0:T(1,128)S(1)}, u32[]{:S(2)}, u32[]{:S(2)}) async-start(s32[16,1,128]{2,1,0:T(1,128)} %bitcast.5), calls=%async_computation.1 | async-start | bytes 16384 | tf_op jit(solution)/shard_map/all_to_all | solution.py:29
  37.7 12.7 %collective-permute-start.3 = (bf16[128,32,128]{2,1,0:T(8,128)(2,1)S(1)}, bf16[128,32,128]{2,1,0:T(8,128)(2,1)S(1)}, u32[]{:S(2)}, u32[]{:S(2)}) collective-permute-start(bf16[128,32,128]{2,1,0:T(8,128)(2,1)S(1)} %constant_dynamic-update-slice_fusion.same_ref), channel_id=1, source_target_pairs={{0,1},{1,0},{2,3},{3,2},{4,5},{5,4},{6,7},{7,6},{8,9},{9,8},{10,11... | collective-permute-start | bytes 3145736 | tf_op jit(solution)/shard_map/ppermute | solution.py:310
  50.4 31.6 %copy-start.1 = (s32[32,16]{0,1:T(8,128)S(1)}, s32[32,16]{0,1:T(8,128)}, u32[]{:S(2)}) copy-start(s32[32,16]{0,1:T(8,128)} %param.7) | copy-start | bytes 6148

commit v10 on v9

--- a/solution.py
+++ b/solution.py
@@ -17,8 +17,10 @@
 UNROLL = 32
 BIG = 1 << 30
 
-Z_GROUPS = [[r + YQ * z for z in range(Z)] for r in range(YQ)]
-YQ_GROUPS = [[YQ * z + r for r in range(YQ)] for z in range(Z)]
+FIRST_Z, FIRST_YQ = Z // 2, (Y // 2) * Q + Q // 2
+FIRST = FIRST_Z * YQ + FIRST_YQ
+Z_GROUPS = [[r + YQ * (z ^ FIRST_Z) for z in range(Z)] for r in range(YQ)]
+YQ_GROUPS = [[YQ * z + (r ^ FIRST_YQ) for r in range(YQ)] for z in range(Z)]
 
 
 def iota(shape, axis):
@@ -73,7 +75,7 @@
     for q in range(QL):
         col = cand[:, q : q + 1]
         key = (q << 10) + (sub << 6) + (col & 63)
-        match = (col >> 6) == lane_owner
+        match = ((col >> 6) ^ FIRST) == lane_owner
         low = jnp.minimum(low, jnp.where(match, key, BIG))
         high = jnp.maximum(high, jnp.where(match, key, -1))
     last = jnp.max(high, axis=0, keepdims=True)
@@ -111,7 +113,7 @@
     valid = code >= 0
     block = jnp.where(valid, code & 63, BLK)
     me = lax.axis_index("query")
-    source = lane8 & (Q - 1)
+    source = (lane8 ^ FIRST_YQ) & (Q - 1)
     piece = (((source ^ me) & 1) << 2) + (((me >> 1) - (source >> 1)) & 3)
     query = jnp.where(valid, (code >> 6) + QL * piece, 0)
 
@@ -242,7 +244,7 @@
     asked = jnp.concatenate(segs, axis=1)
     place = iota((1, QL * CL), 1)
     own_key = ((place & 31) << 10) + ((place >> 5) << 6) + (asked & 63)
-    owner = asked >> 6
+    owner = (asked >> 6) ^ FIRST
     lane_z = iota((Z, 128), 1)
     x = jnp.where(lane_z < 2 * YQ, x_ref[...], 0.0)
     key = jnp.where(lane_z < YQ, key_ref[...], 0)

time: 83.5 us -> 74.2 us (0.89)
  waiting for transfers between devices: 7.64 us -> 0.57 us
  blocking collectives: 27.7 us -> 22.4 us
  starting transfers between devices: 38.2 us -> 41 us
    all_to_all x2, waiting for transfers between devices: 7.63 us -> 0.01 us  [exchange(): lax.all_to_all(x, ('index', 'query'), split_axis=0, concat_axis=0, tiled=...]
    all_to_all x2, blocking collectives: 27.7 us -> 22.4 us  [exchange(): lax.all_to_all(x, ('index', 'query'), split_axis=0, concat_axis=0, tiled=...]
    all_to_all x2, starting transfers between devices: 23.5 us -> 28.6 us  [exchange(): lax.all_to_all(x, ('index', 'query'), split_axis=0, concat_axis=0, tiled=...]
    ppermute x3, starting transfers between devices: 11.3 us -> 8.68 us  [shards(): lax.ppermute(queries, 'query', [(k, (k + 2 * d) % Q) for k in range(Q)])]
where the time goes in v10:
time: 74.2 us; the launch traced here: 73.5 us
  starting transfers between devices  41 us (55%)
  blocking collectives  22.4 us (30%)
  Pallas kernels  8.55 us (12%)
  local copies, waits for them, and re-layouts  0.83 us (1%)
    all_to_all x2, starting transfers between devices, exchange(): lax.all_to_all(x, ('index', 'query'), split_axis=0, concat_axis=0, tiled=...  28.6 us
    all_to_all x2, blocking collectives, exchange(): lax.all_to_all(x, ('index', 'query'), split_axis=0, concat_axis=0, tiled=...  22.4 us
    ppermute x3, starting transfers between devices, shards(): lax.ppermute(queries, 'query', [(k, (k + 2 * d) % Q) for k in range(Q)])  8.68 us
    pallas_call x1, Pallas kernels, shards(): pl.pallas_call(score_kernel, out_shape=(pltpu.VMEM((Z, 128), jnp.float32)...  3.71 us
    ppermute x1, starting transfers between devices, shards(): other = lax.ppermute(same, 'query', [(k, k ^ 1) for k in range(Q)])  3.67 us
    pallas_call x5, Pallas kernels, small_call(): pl.pallas_call(kernel, cost_estimate=hint, out_shape=out_shape, in_specs=...  3.15 us
    pallas_call x1, Pallas kernels, shards(): pl.pallas_call(sort_kernel, out_shape=(pltpu.VMEM((2 * GROUP, 256), jnp.i...  1.69 us
  transfers between devices with their start and end apart: 6, of which 1 were waited for; matrix products, arithmetic and copies ran while one was open for 0% of the time, Pallas kernels for 3%

profile of v10, /device:TPU:1, one launch (start us, length us, event | category | flops | bytes accessed | tf_op | source)
XLA Modules:
  0.0 73.5 jit_solution(12721073862235134287)
XLA Ops:
  0.0 0.0 copy-start
  0.0 0.7 copy-done
  0.7 1.2 %shard_map.46 = (s32[32,128]{1,0:T(8,128)}, s32[16,128]{1,0:T(8,128)S(1)}) custom-call(s32[16,32]{1,0:T(8,128)S(1)} %bitcast.21), custom_call_target="tpu_custom_call" | custom-call | tf_op jit(solution)/shard_map/pallas_call | solution.py:286
  1.9 13.9 %all-to-all-start = ((s32[32,1,128]{2,1,0:T(1,128)}), s32[32,1,128]{2,1,0:T(1,128)S(1)}, u32[]{:S(2)}, u32[]{:S(2)}) async-start(s32[32,1,128]{2,1,0:T(1,128)} %bitcast.2), calls=%async_computation | async-start | bytes 32768 | tf_op jit(solution)/shard_map/all_to_all | solution.py:31
  15.8 2.2 %collective-permute-start.1 = (bf16[32,32,128]{2,1,0:T(8,128)(2,1)}, bf16[32,32,128]{2,1,0:T(8,128)(2,1)S(1)}, u32[]{:S(2)}, u32[]{:S(2)}) collective-permute-start(bf16[32,32,128]{2,1,0:T(8,128)(2,1)} %param.4), channel_id=1, source_target_pairs={{0,4},{1,5},{2,6},{3,7},{4,0},{5,1},{6,2},{7,3},{8,12},{9,13},{10,... | collective-permute-start | bytes 786440 | tf_op jit(solution)/shard_map/ppermute | solution.py:297
  18.0 2.5 %collective-permute-start = (bf16[32,32,128]{2,1,0:T(8,128)(2,1)}, bf16[32,32,128]{2,1,0:T(8,128)(2,1)S(1)}, u32[]{:S(2)}, u32[]{:S(2)}) collective-permute-start(bf16[32,32,128]{2,1,0:T(8,128)(2,1)} %param.4), channel_id=1, source_target_pairs={{0,2},{1,3},{2,4},{3,5},{4,6},{5,7},{6,0},{7,1},{8,10},{9,11},{10,... | collective-permute-start | bytes 786440 | tf_op jit(solution)/shard_map/ppermute | solution.py:297
  20.5 4.0 %collective-permute-start.2 = (bf16[32,32,128]{2,1,0:T(8,128)(2,1)}, bf16[32,32,128]{2,1,0:T(8,128)(2,1)S(1)}, u32[]{:S(2)}, u32[]{:S(2)}) collective-permute-start(bf16[32,32,128]{2,1,0:T(8,128)(2,1)} %param.4), channel_id=1, source_target_pairs={{0,6},{1,7},{2,0},{3,1},{4,2},{5,3},{6,4},{7,5},{8,14},{9,15},{10,... | collective-permute-start | bytes 786440 | tf_op jit(solution)/shard_map/ppermute | solution.py:297
  24.5 0.0 all-to-all-done
  24.5 0.0 copy-start.2
  24.5 0.7 %shard_map.47 = s32[16,128]{1,0:T(8,128)} custom-call(s32[32,128]{1,0:T(8,128)S(1)} %bitcast.24), custom_call_target="tpu_custom_call" | custom-call | flops 99999997952 | bytes 1048576 | tf_op jit(solution)/shard_map/pallas_call | solution.py:286
  25.3 14.7 %all-to-all-start.1 = ((s32[16,1,128]{2,1,0:T(1,128)}), s32[16,1,128]{2,1,0:T(1,128)S(1)}, u32[]{:S(2)}, u32[]{:S(2)}) async-start(s32[16,1,128]{2,1,0:T(1,128)} %bitcast.5), calls=%async_computation.1 | async-start | bytes 16384 | tf_op jit(solution)/shard_map/all_to_all | solution.py:31
  40.0 0.0 collective-permute-done.1
  40.0 0.0 collective-permute-done
  40.0 0.0 collective-permute-done.2
  40.0 0.0 copy-done.2
  40.2 3.7 %collective-permute-start.3 = (bf16[128,32,128]{2,1,0:T(8,128)(2,1)S(1)}, bf16[128,32,128]{2,1,0:T(8,128)(2,1)S(1)}, u32[]{:S(2)}, u32[]{:S(2)}) collective-permute-start(bf16[128,32,128]{2,1,0:T(8,128)(2,1)S(1)} %constant_dynamic-update-slice_fusion.same_ref), channel_id=1, source_target_pairs={{0,1},{1,0},{2,3},{3,2},{4,5},{5,4},{6,7},{7,6},{8,9},{9,8},{10,11... | collective-permute-start | bytes 3145736 | tf_op jit(solution)/shard_map/ppermute | solution.py:312
  43.9 0.0 all-to-all-done.1
  43.9 1.7 %shard_map.48 = (s32[16,256]{1,0:T(8,128)S(1)}, s32[8,128]{1,0:T(8,128)S(1)}, bf16[192,1024]{1,0:T(8,128)(2,1)S(1)}, bf16[64,128,128]{2,1,0:T(8,128)(2,1)S(1)}, bf16[256,32,128]{2,1,0:T(8,128)(2,1)S(1)}) custom-call(s32[16,128]{1,0:T(8,128)S(1)} %bitcast.25, bf16[64,128,128]{2,1,0:T(8,128)(2,1)} %p_hbm.1, ...), custom_call_target="tpu_custom_call" | custom-call | flops 99999997952 | bytes 4194304 | tf_op jit(solution)/shard_map/pallas_call | solution.py:316
  45.6 0.6 collective-permute-done.3.other_ref
  46.2 0.0 copy-start.1
  46.2 3.7 %shard_map.49 = (f32[16,128]{1,0:T(8,128)S(1)}, bf16[256,32,128]{2,1,0:T(8,128)(2,1)S(1)}) custom-call(s32[64]{0:T(128)} %len_hbm.1, s32[16,256]{1,0:T(8,128)S(1)} %get-tuple-element.23.plan, s32[8,128]{1,0:T(8,128)S(1)} %get-tuple-element.24.dest_ref, bf16[192,1024]{1,0:T(8,128)(2,1)S(1)} %get-tuple-element.25.onehot_ref, ...), custom_call_target="tpu_custom_call", output_to_operand_aliasing={{1}: (6, {})} | custom-call | tf_op jit(solution)/shard_map/pallas_call | solution.py:331
  49.9 0.1 shard_map.50
  50.0 9.2 %all_to_all.44 = f32[32,1,128]{2,1,0:T(1,128)S(1)} all-to-all(f32[32,1,128]{2,1,0:T(1,128)S(1)} %bitcast.18), channel_id=1, replica_groups={{20,21,22,23,16,17,18,19,28,29,30,31,24,25,26,27,4,5,6,7,0,1,2,3,12,13,..., dimensions={0} | all-to-all | bytes 32768 | tf_op jit(solution)/shard_map/all_to_all | solution.py:31
  59.2 0.1 shard_map.51
  59.2 13.2 %all_to_all.45 = f32[16,1,128]{2,1,0:T(1,128)S(1)} all-to-all(f32[16,1,128]{2,1,0:T(1,128)S(1)} %bitcast.20), channel_id=1, replica_groups={{256,288,320,352,384,416,448,480,0,32,64,96,128,160,192,224},{257,289,3..., dimensions={0} | all-to-all | bytes 16384 | tf_op jit(solution)/shard_map/all_to_all | solution.py:31
  72.5 0.0 copy-done.1
  72.5 1.0 %shard_map.52 = f32[16,32]{1,0:T(8,128)} custom-call(s32[16,32]{1,0:T(8,128)S(1)} %bitcast.22, s32[16,128]{1,0:T(8,128)S(1)} %get-tuple-element.17.key_ref, f32[16,128]{1,0:T(8,128)S(1)} %bitcast.23), custom_call_target="tpu_custom_call" | custom-call | tf_op jit(solution)/shard_map/pallas_call | solution.py:286
  (4 shorter events, 0.1 us)
Async XLA Ops:
  0.0 0.7 copy-start
  1.9 22.6 %all-to-all-start = ((s32[32,1,128]{2,1,0:T(1,128)}), s32[32,1,128]{2,1,0:T(1,128)S(1)}, u32[]{:S(2)}, u32[]{:S(2)}) async-start(s32[32,1,128]{2,1,0:T(1,128)} %bitcast.2), calls=%async_computation | async-start | bytes 32768 | tf_op jit(solution)/shard_map/all_to_all | solution.py:31
  15.8 24.2 %collective-permute-start.1 = (bf16[32,32,128]{2,1,0:T(8,128)(2,1)}, bf16[32,32,128]{2,1,0:T(8,128)(2,1)S(1)}, u32[]{:S(2)}, u32[]{:S(2)}) collective-permute-start(bf16[32,32,128]{2,1,0:T(8,128)(2,1)} %param.4), channel_id=1, source_target_pairs={{0,4},{1,5},{2,6},{3,7},{4,0},{5,1},{6,2},{7,3},{8,12},{9,13},{10,... | collective-permute-start | bytes 786440 | tf_op jit(solution)/shard_map/ppermute | solution.py:297
  18.0 22.0 %collective-permute-start = (bf16[32,32,128]{2,1,0:T(8,128)(2,1)}, bf16[32,32,128]{2,1,0:T(8,128)(2,1)S(1)}, u32[]{:S(2)}, u32[]{:S(2)}) collective-permute-start(bf16[32,32,128]{2,1,0:T(8,128)(2,1)} %param.4), channel_id=1, source_target_pairs={{0,2},{1,3},{2,4},{3,5},{4,6},{5,7},{6,0},{7,1},{8,10},{9,11},{10,... | collective-permute-start | bytes 786440 | tf_op jit(solution)/shard_map/ppermute | solution.py:297
  20.5 19.5 %collective-permute-start.2 = (bf16[32,32,128]{2,1,0:T(8,128)(2,1)}, bf16[32,32,128]{2,1,0:T(8,128)(2,1)S(1)}, u32[]{:S(2)}, u32[]{:S(2)}) collective-permute-start(bf16[32,32,128]{2,1,0:T(8,128)(2,1)} %param.4), channel_id=1, source_target_pairs={{0,6},{1,7},{2,0},{3,1},{4,2},{5,3},{6,4},{7,5},{8,14},{9,15},{10,... | collective-permute-start | bytes 786440 | tf_op jit(solution)/shard_map/ppermute | solution.py:297
  24.5 15.5 %copy-start.2 = (bf16[32,32,128]{2,1,0:T(8,128)(2,1)S(1)}, bf16[32,32,128]{2,1,0:T(8,128)(2,1)}, u32[]{:S(2)}) copy-start(bf16[32,32,128]{2,1,0:T(8,128)(2,1)} %param.4) | copy-start | bytes 786436
  25.3 18.6 %all-to-all-start.1 = ((s32[16,1,128]{2,1,0:T(1,128)}), s32[16,1,128]{2,1,0:T(1,128)S(1)}, u32[]{:S(2)}, u32[]{:S(2)}) async-start(s32[16,1,128]{2,1,0:T(1,128)} %bitcast.5), calls=%async_computation.1 | async-start | bytes 16384 | tf_op jit(solution)/shard_map/all_to_all | solution.py:31
  40.2 5.9 %collective-permute-start.3 = (bf16[128,32,128]{2,1,0:T(8,128)(2,1)S(1)}, bf16[128,32,128]{2,1,0:T(8,128)(2,1)S(1)}, u32[]{:S(2)}, u32[]{:S(2)}) collective-permute-start(bf16[128,32,128]{2,1,0:T(8,128)(2,1)S(1)} %constant_dynamic-update-slice_fusion.same_ref), channel_id=1, source_target_pairs={{0,1},{1,0},{2,3},{3,2},{4,5},{5,4},{6,7},{7,6},{8,9},{9,8},{10,11... | collective-permute-start | bytes 3145736 | tf_op jit(solution)/shard_map/ppermute | solution.py:312
  46.2 26.3 %copy-start.1 = (s32[32,16]{0,1:T(8,128)S(1)}, s32[32,16]{0,1:T(8,128)}, u32[]{:S(2)}) copy-start(s32[32,16]{0,1:T(8,128)} %param.7) | copy-start | bytes 6148

commit v11 on v10

--- a/solution.py
+++ b/solution.py
@@ -17,7 +17,7 @@
 UNROLL = 32
 BIG = 1 << 30
 
-FIRST_Z, FIRST_YQ = Z // 2, (Y // 2) * Q + Q // 2
+FIRST_Z, FIRST_YQ = Z // 2, (Y // 2) * Q + Q // 2 + 1
 FIRST = FIRST_Z * YQ + FIRST_YQ
 Z_GROUPS = [[r + YQ * (z ^ FIRST_Z) for z in range(Z)] for r in range(YQ)]
 YQ_GROUPS = [[YQ * z + (r ^ FIRST_YQ) for r in range(YQ)] for z in range(Z)]
@@ -85,8 +85,9 @@
     lane = iota((Z, 128), 1)
     key = spread((first, last), row, lane)
     key_ref[...] = key
-    code = jnp.where((key >= 0) & (lane < 2 * YQ), ((key >> 10) << 6) + (key & 63), -1)
-    code_ref[...] = by_plane(code)
+    code_ref[...] = jnp.where(
+        (key >= 0) & (lane < 2 * YQ), ((key >> 10) << 6) + (key & 63), -1
+    )
 
 
 def split3(x):
@@ -108,12 +109,16 @@
     q_copy.start()
     p_copy = pltpu.make_async_copy(p_hbm, p_ref, p_sem)
     p_copy.start()
+    code = jnp.full((Q, 128), -1, jnp.int32)
     lane8 = iota((Q, 128), 1)
-    code = jnp.where(lane8 < 64, code_ref[0:8, :], pltpu.roll(code_ref[8:16, :], 64, 1))
+    for y in range(Y):
+        part = code_ref[Q * y : Q * (y + 1), :]
+        part = pltpu.roll(part, 32 * y, 1) if y else part
+        code = jnp.where(lane8 >> 5 == y, part, code)
     valid = code >= 0
     block = jnp.where(valid, code & 63, BLK)
     me = lax.axis_index("query")
-    source = (lane8 ^ FIRST_YQ) & (Q - 1)
+    source = iota((Q, 128), 0) ^ (FIRST_YQ & (Q - 1))
     piece = (((source ^ me) & 1) << 2) + (((me >> 1) - (source >> 1)) & 3)
     query = jnp.where(valid, (code >> 6) + QL * piece, 0)
 
@@ -227,8 +232,9 @@
             jnp.sum(jnp.where(here, picked[:, 128 * q : 128 * (q + 1)], 0.0), axis=0, keepdims=True)
         )
     out = jnp.concatenate(out, axis=0)
-    o_ref[0:8, :] = out
-    o_ref[8:16, :] = pltpu.roll(out, 64, 1)
+    for y in range(Y):
+        shift = (128 - 32 * y) % 128
+        o_ref[Q * y : Q * (y + 1), :] = pltpu.roll(out, shift, 1) if shift else out
 
 
 def place_kernel(cand_ref, key_ref, x_ref, o_ref):
@@ -300,13 +306,13 @@
     cand = candidates.T
     table, keys = small_call(
         request_kernel,
-        (pltpu.VMEM((YQ, 128), jnp.int32), pltpu.VMEM((Z, 128), jnp.int32)),
+        (pltpu.VMEM((Z, 128), jnp.int32), pltpu.VMEM((Z, 128), jnp.int32)),
         cand,
     )
-    got = exchange(table, YQ_GROUPS)
+    got = exchange(table, Z_GROUPS)
     hint = pl.CostEstimate(flops=10**11, transcendentals=0, bytes_accessed=2**20)
-    got = small_call(by_z_kernel, pltpu.VMEM((Z, 128), jnp.int32), got, hint=hint)
-    codes = exchange(got, Z_GROUPS)
+    got = small_call(by_plane_kernel, pltpu.VMEM((YQ, 128), jnp.int32), got, hint=hint)
+    codes = exchange(got, YQ_GROUPS)
     _, *same = lax.optimization_barrier((got, *same))
     same = jnp.concatenate(same, axis=0)
     other = lax.ppermute(same, "query", [(k, k ^ 1) for k in range(Q)])
@@ -330,7 +336,7 @@
     )(at(codes, pltpu.VMEM), at(passages, pltpu.HBM), at(same, pltpu.VMEM))
     scores, _ = pl.pallas_call(
         score_kernel,
-        out_shape=(pltpu.VMEM((Z, 128), jnp.float32), every),
+        out_shape=(pltpu.VMEM((YQ, 128), jnp.float32), every),
         in_specs=[hbm] + [VMEM] * 6,
         out_specs=(VMEM, VMEM),
         input_output_aliases={6: 1},
@@ -347,8 +353,7 @@
         at(lengths, pltpu.HBM),
         *[at(x, pltpu.VMEM) for x in (plan, dest, onehot, other, blocks, gathered)],
     )
-    back = small_call(by_plane_kernel, pltpu.VMEM((YQ, 128), jnp.float32), scores)
-    back = exchange(back, YQ_GROUPS)
+    back = exchange(scores, YQ_GROUPS)
     back = small_call(by_z_kernel, pltpu.VMEM((Z, 128), jnp.float32), back)
     back = exchange(back, Z_GROUPS)
     out = small_call(

time: 74.2 us -> 75.3 us (1.015)
  starting transfers between devices: 41 us -> 42.3 us
    ppermute x3, starting transfers between devices: 8.68 us -> 11.1 us  [shards(): lax.ppermute(queries, 'query', [(k, (k + 2 * d) % Q) for k in range(Q)])]
    ppermute x1, starting transfers between devices: 3.67 us -> 2.34 us  [shards(): other = lax.ppermute(same, 'query', [(k, k ^ 1) for k in range(Q)])]
    pallas_call x5 -> x4, Pallas kernels: 3.15 us -> 2.92 us  [small_call(): pl.pallas_call(kernel, cost_estimate=hint, out_shape=out_shape, in_specs=...]
where the time goes in v11:
time: 75.3 us; the launch traced here: 74.3 us
  starting transfers between devices  42.3 us (56%)
  blocking collectives  22.1 us (29%)
  Pallas kernels  8.33 us (11%)
  local copies, waits for them, and re-layouts  0.83 us (1%)
    all_to_all x2, starting transfers between devices, exchange(): lax.all_to_all(x, ('index', 'query'), split_axis=0, concat_axis=0, tiled=...  28.9 us
    all_to_all x2, blocking collectives, exchange(): lax.all_to_all(x, ('index', 'query'), split_axis=0, concat_axis=0, tiled=...  22.1 us
    ppermute x3, starting transfers between devices, shards(): lax.ppermute(queries, 'query', [(k, (k + 2 * d) % Q) for k in range(Q)])  11.1 us
    pallas_call x1, Pallas kernels, shards(): pl.pallas_call(score_kernel, out_shape=(pltpu.VMEM((YQ, 128), jnp.float32...  3.72 us
    pallas_call x4, Pallas kernels, small_call(): pl.pallas_call(kernel, cost_estimate=hint, out_shape=out_shape, in_specs=...  2.92 us
    ppermute x1, starting transfers between devices, shards(): other = lax.ppermute(same, 'query', [(k, k ^ 1) for k in range(Q)])  2.34 us
    pallas_call x1, Pallas kernels, shards(): pl.pallas_call(sort_kernel, out_shape=(pltpu.VMEM((2 * GROUP, 256), jnp.i...  1.69 us
  transfers between devices with their start and end apart: 6, of which 1 were waited for; matrix products, arithmetic and copies ran while one was open for 0% of the time, Pallas kernels for 3%

profile of v11, /device:TPU:1, one launch (start us, length us, event | category | flops | bytes accessed | tf_op | source)
XLA Modules:
  0.0 74.3 jit_solution(7863125766622164004)
XLA Ops:
  0.0 0.0 copy-start
  0.0 0.7 copy-done
  0.7 1.1 %shard_map.46 = (s32[16,128]{1,0:T(8,128)}, s32[16,128]{1,0:T(8,128)S(1)}) custom-call(s32[16,32]{1,0:T(8,128)S(1)} %bitcast.20), custom_call_target="tpu_custom_call" | custom-call | tf_op jit(solution)/shard_map/pallas_call | solution.py:292
  1.8 19.1 %all-to-all-start = ((s32[16,1,128]{2,1,0:T(1,128)}), s32[16,1,128]{2,1,0:T(1,128)S(1)}, u32[]{:S(2)}, u32[]{:S(2)}) async-start(s32[16,1,128]{2,1,0:T(1,128)} %bitcast.2), calls=%async_computation | async-start | bytes 16384 | tf_op jit(solution)/shard_map/all_to_all | solution.py:31
  20.9 4.6 %collective-permute-start.1 = (bf16[32,32,128]{2,1,0:T(8,128)(2,1)}, bf16[32,32,128]{2,1,0:T(8,128)(2,1)S(1)}, u32[]{:S(2)}, u32[]{:S(2)}) collective-permute-start(bf16[32,32,128]{2,1,0:T(8,128)(2,1)} %param.4), channel_id=1, source_target_pairs={{0,4},{1,5},{2,6},{3,7},{4,0},{5,1},{6,2},{7,3},{8,12},{9,13},{10,... | collective-permute-start | bytes 786440 | tf_op jit(solution)/shard_map/ppermute | solution.py:303
  25.5 2.2 %collective-permute-start = (bf16[32,32,128]{2,1,0:T(8,128)(2,1)}, bf16[32,32,128]{2,1,0:T(8,128)(2,1)S(1)}, u32[]{:S(2)}, u32[]{:S(2)}) collective-permute-start(bf16[32,32,128]{2,1,0:T(8,128)(2,1)} %param.4), channel_id=1, source_target_pairs={{0,2},{1,3},{2,4},{3,5},{4,6},{5,7},{6,0},{7,1},{8,10},{9,11},{10,... | collective-permute-start | bytes 786440 | tf_op jit(solution)/shard_map/ppermute | solution.py:303
  27.8 4.3 %collective-permute-start.2 = (bf16[32,32,128]{2,1,0:T(8,128)(2,1)}, bf16[32,32,128]{2,1,0:T(8,128)(2,1)S(1)}, u32[]{:S(2)}, u32[]{:S(2)}) collective-permute-start(bf16[32,32,128]{2,1,0:T(8,128)(2,1)} %param.4), channel_id=1, source_target_pairs={{0,6},{1,7},{2,0},{3,1},{4,2},{5,3},{6,4},{7,5},{8,14},{9,15},{10,... | collective-permute-start | bytes 786440 | tf_op jit(solution)/shard_map/ppermute | solution.py:303
  32.0 0.0 all-to-all-done
  32.0 0.0 copy-start.2
  32.1 0.8 %shard_map.47 = s32[32,128]{1,0:T(8,128)} custom-call(s32[16,128]{1,0:T(8,128)S(1)} %bitcast.25), custom_call_target="tpu_custom_call" | custom-call | flops 99999997952 | bytes 1048576 | tf_op jit(solution)/shard_map/pallas_call | solution.py:292
  32.8 9.7 %all-to-all-start.1 = ((s32[32,1,128]{2,1,0:T(1,128)}), s32[32,1,128]{2,1,0:T(1,128)S(1)}, u32[]{:S(2)}, u32[]{:S(2)}) async-start(s32[32,1,128]{2,1,0:T(1,128)} %bitcast.5), calls=%async_computation.1 | async-start | bytes 32768 | tf_op jit(solution)/shard_map/all_to_all | solution.py:31
  42.6 0.0 collective-permute-done.1
  42.6 0.0 collective-permute-done
  42.6 0.0 collective-permute-done.2
  42.6 0.0 copy-done.2
  42.8 2.3 %collective-permute-start.3 = (bf16[128,32,128]{2,1,0:T(8,128)(2,1)S(1)}, bf16[128,32,128]{2,1,0:T(8,128)(2,1)S(1)}, u32[]{:S(2)}, u32[]{:S(2)}) collective-permute-start(bf16[128,32,128]{2,1,0:T(8,128)(2,1)S(1)} %constant_dynamic-update-slice_fusion.same_ref), channel_id=1, source_target_pairs={{0,1},{1,0},{2,3},{3,2},{4,5},{5,4},{6,7},{7,6},{8,9},{9,8},{10,11... | collective-permute-start | bytes 3145736 | tf_op jit(solution)/shard_map/ppermute | solution.py:318
  45.1 0.0 all-to-all-done.1
  45.1 1.7 %shard_map.48 = (s32[16,256]{1,0:T(8,128)S(1)}, s32[8,128]{1,0:T(8,128)S(1)}, bf16[192,1024]{1,0:T(8,128)(2,1)S(1)}, bf16[64,128,128]{2,1,0:T(8,128)(2,1)S(1)}, bf16[256,32,128]{2,1,0:T(8,128)(2,1)S(1)}) custom-call(s32[32,128]{1,0:T(8,128)S(1)} %bitcast.23, bf16[64,128,128]{2,1,0:T(8,128)(2,1)} %p_hbm.1, ...), custom_call_target="tpu_custom_call" | custom-call | flops 99999997952 | bytes 4194304 | tf_op jit(solution)/shard_map/pallas_call | solution.py:322
  46.8 0.6 collective-permute-done.3.other_ref
  47.4 0.0 copy-start.1
  47.4 3.7 %shard_map.49 = (f32[32,128]{1,0:T(8,128)S(1)}, bf16[256,32,128]{2,1,0:T(8,128)(2,1)S(1)}) custom-call(s32[64]{0:T(128)} %len_hbm.1, s32[16,256]{1,0:T(8,128)S(1)} %get-tuple-element.23.plan, s32[8,128]{1,0:T(8,128)S(1)} %get-tuple-element.24.dest_ref, bf16[192,1024]{1,0:T(8,128)(2,1)S(1)} %get-tuple-element.25.onehot_ref, ...), custom_call_target="tpu_custom_call", output_to_operand_aliasing={{1}: (6, {})} | custom-call | tf_op jit(solution)/shard_map/pallas_call | solution.py:337
  51.1 9.2 %all_to_all.44 = f32[32,1,128]{2,1,0:T(1,128)S(1)} all-to-all(f32[32,1,128]{2,1,0:T(1,128)S(1)} %bitcast.24), channel_id=1, replica_groups={{21,20,23,22,17,16,19,18,29,28,31,30,25,24,27,26,5,4,7,6,1,0,3,2,13,12,..., dimensions={0} | all-to-all | bytes 32768 | tf_op jit(solution)/shard_map/all_to_all | solution.py:31
  60.3 0.1 shard_map.50
  60.4 12.9 %all_to_all.45 = f32[16,1,128]{2,1,0:T(1,128)S(1)} all-to-all(f32[16,1,128]{2,1,0:T(1,128)S(1)} %bitcast.19), channel_id=1, replica_groups={{256,288,320,352,384,416,448,480,0,32,64,96,128,160,192,224},{257,289,3..., dimensions={0} | all-to-all | bytes 16384 | tf_op jit(solution)/shard_map/all_to_all | solution.py:31
  73.3 0.0 copy-done.1
  73.3 1.0 %shard_map.51 = f32[16,32]{1,0:T(8,128)} custom-call(s32[16,32]{1,0:T(8,128)S(1)} %bitcast.21, s32[16,128]{1,0:T(8,128)S(1)} %get-tuple-element.17.key_ref, f32[16,128]{1,0:T(8,128)S(1)} %bitcast.22), custom_call_target="tpu_custom_call" | custom-call | tf_op jit(solution)/shard_map/pallas_call | solution.py:292
  (4 shorter events, 0.1 us)
Async XLA Ops:
  0.0 0.7 copy-start
  1.8 30.3 %all-to-all-start = ((s32[16,1,128]{2,1,0:T(1,128)}), s32[16,1,128]{2,1,0:T(1,128)S(1)}, u32[]{:S(2)}, u32[]{:S(2)}) async-start(s32[16,1,128]{2,1,0:T(1,128)} %bitcast.2), calls=%async_computation | async-start | bytes 16384 | tf_op jit(solution)/shard_map/all_to_all | solution.py:31
  20.9 21.7 %collective-permute-start.1 = (bf16[32,32,128]{2,1,0:T(8,128)(2,1)}, bf16[32,32,128]{2,1,0:T(8,128)(2,1)S(1)}, u32[]{:S(2)}, u32[]{:S(2)}) collective-permute-start(bf16[32,32,128]{2,1,0:T(8,128)(2,1)} %param.4), channel_id=1, source_target_pairs={{0,4},{1,5},{2,6},{3,7},{4,0},{5,1},{6,2},{7,3},{8,12},{9,13},{10,... | collective-permute-start | bytes 786440 | tf_op jit(solution)/shard_map/ppermute | solution.py:303
  25.5 17.0 %collective-permute-start = (bf16[32,32,128]{2,1,0:T(8,128)(2,1)}, bf16[32,32,128]{2,1,0:T(8,128)(2,1)S(1)}, u32[]{:S(2)}, u32[]{:S(2)}) collective-permute-start(bf16[32,32,128]{2,1,0:T(8,128)(2,1)} %param.4), channel_id=1, source_target_pairs={{0,2},{1,3},{2,4},{3,5},{4,6},{5,7},{6,0},{7,1},{8,10},{9,11},{10,... | collective-permute-start | bytes 786440 | tf_op jit(solution)/shard_map/ppermute | solution.py:303
  27.8 14.8 %collective-permute-start.2 = (bf16[32,32,128]{2,1,0:T(8,128)(2,1)}, bf16[32,32,128]{2,1,0:T(8,128)(2,1)S(1)}, u32[]{:S(2)}, u32[]{:S(2)}) collective-permute-start(bf16[32,32,128]{2,1,0:T(8,128)(2,1)} %param.4), channel_id=1, source_target_pairs={{0,6},{1,7},{2,0},{3,1},{4,2},{5,3},{6,4},{7,5},{8,14},{9,15},{10,... | collective-permute-start | bytes 786440 | tf_op jit(solution)/shard_map/ppermute | solution.py:303
  32.0 10.5 %copy-start.2 = (bf16[32,32,128]{2,1,0:T(8,128)(2,1)S(1)}, bf16[32,32,128]{2,1,0:T(8,128)(2,1)}, u32[]{:S(2)}) copy-start(bf16[32,32,128]{2,1,0:T(8,128)(2,1)} %param.4) | copy-start | bytes 786436
  32.8 12.3 %all-to-all-start.1 = ((s32[32,1,128]{2,1,0:T(1,128)}), s32[32,1,128]{2,1,0:T(1,128)S(1)}, u32[]{:S(2)}, u32[]{:S(2)}) async-start(s32[32,1,128]{2,1,0:T(1,128)} %bitcast.5), calls=%async_computation.1 | async-start | bytes 32768 | tf_op jit(solution)/shard_map/all_to_all | solution.py:31
  42.8 4.6 %collective-permute-start.3 = (bf16[128,32,128]{2,1,0:T(8,128)(2,1)S(1)}, bf16[128,32,128]{2,1,0:T(8,128)(2,1)S(1)}, u32[]{:S(2)}, u32[]{:S(2)}) collective-permute-start(bf16[128,32,128]{2,1,0:T(8,128)(2,1)S(1)} %constant_dynamic-update-slice_fusion.same_ref), channel_id=1, source_target_pairs={{0,1},{1,0},{2,3},{3,2},{4,5},{5,4},{6,7},{7,6},{8,9},{9,8},{10,11... | collective-permute-start | bytes 3145736 | tf_op jit(solution)/shard_map/ppermute | solution.py:318
  47.4 25.9 %copy-start.1 = (s32[32,16]{0,1:T(8,128)S(1)}, s32[32,16]{0,1:T(8,128)}, u32[]{:S(2)}) copy-start(s32[32,16]{0,1:T(8,128)} %param.7) | copy-start | bytes 6148

commit v12 on v10

--- a/solution.py
+++ b/solution.py
@@ -17,7 +17,7 @@
 UNROLL = 32
 BIG = 1 << 30
 
-FIRST_Z, FIRST_YQ = Z // 2, (Y // 2) * Q + Q // 2
+FIRST_Z, FIRST_YQ = Z // 2, (Y // 2) * Q + Q // 2 + 1
 FIRST = FIRST_Z * YQ + FIRST_YQ
 Z_GROUPS = [[r + YQ * (z ^ FIRST_Z) for z in range(Z)] for r in range(YQ)]
 YQ_GROUPS = [[YQ * z + (r ^ FIRST_YQ) for r in range(YQ)] for z in range(Z)]
@@ -102,8 +102,11 @@
 
 
 def sort_kernel(
-    code_ref, p_hbm, same_ref, plan_ref, dest_ref, onehot_ref, p_ref, q_ref, p_sem, q_sem
+    code_ref, p_hbm, same_ref, len_hbm, plan_ref, dest_ref, onehot_ref, p_ref, q_ref,
+    len_ref, p_sem, q_sem, len_sem,
 ):
+    len_copy = pltpu.make_async_copy(len_hbm, len_ref, len_sem)
+    len_copy.start()
     q_copy = pltpu.make_async_copy(same_ref, q_ref.at[pl.ds(0, NQ // 2)], q_sem)
     q_copy.start()
     p_copy = pltpu.make_async_copy(p_hbm, p_ref, p_sem)
@@ -165,10 +168,17 @@
         jnp.sum((ends2 <= g_lane).astype(jnp.int32), axis=0, keepdims=True), BLK - 1
     )
     total = jnp.broadcast_to(ends2[BLK - 1 : BLK, :], (1, 256))
+    len_copy.wait()
+    live = jnp.concatenate([len_ref[...], jnp.zeros((1, 256 - BLK), jnp.int32)], axis=1)
+    row = iota((GROUP, 256), 0)
     plan_ref[GROUP : 2 * GROUP, :] = jnp.where(
-        iota((GROUP, 256), 0) == 0,
+        row == 0,
         jnp.broadcast_to(owner_block, (GROUP, 256)),
-        jnp.broadcast_to(total, (GROUP, 256)),
+        jnp.where(
+            row == 1,
+            jnp.broadcast_to(total, (GROUP, 256)),
+            jnp.broadcast_to(live, (GROUP, 256)),
+        ),
     )
     p_copy.wait()
     q_copy.wait()
@@ -182,21 +192,17 @@
 
 
 def score_kernel(
-    len_hbm, plan, dest_ref, onehot_ref, other_ref, p_ref, _, o_ref, q_ref,
-    len_ref, plan_s, best, sem, len_sem, q_sem,
+    plan, dest_ref, onehot_ref, other_ref, p_ref, _, o_ref, q_ref, plan_s, best, sem, q_sem
 ):
     half = NQ // 2
     q_copy = pltpu.make_async_copy(other_ref, q_ref.at[pl.ds(half, half)], q_sem)
     q_copy.start()
-    len_copy = pltpu.make_async_copy(len_hbm, len_ref, len_sem)
-    len_copy.start()
     copy = pltpu.make_async_copy(plan, plan_s, sem)
     copy.start()
     dest = dest_ref[...]
     c_iota = iota((GROUP, 128), 0)
     best[...] = jnp.zeros((GMAX, GROUP * T), jnp.float32)
     copy.wait()
-    len_copy.wait()
     q_copy.wait()
 
     token = iota((PT, GROUP * T), 0)
@@ -208,7 +214,7 @@
             b = plan_s[GROUP, g]
             rows_q = jnp.concatenate([q_ref[plan_s[c, g]] for c in range(GROUP)], axis=0)
             similar = dot(p_ref[b], rows_q, ((1,), (1,)))
-            similar = jnp.where(token < len_ref[b], similar, -jnp.inf)
+            similar = jnp.where(token < plan_s[GROUP + 2, b], similar, -jnp.inf)
             rows.append(jnp.max(similar, axis=0, keepdims=True))
         best[pl.ds(pl.multiple_of(it * UNROLL, UNROLL), UNROLL), :] = jnp.concatenate(rows, axis=0)
         return carry
@@ -322,29 +328,31 @@
             pltpu.VMEM(passages.shape, passages.dtype),
             every,
         ),
-        in_specs=[VMEM, hbm, VMEM],
+        in_specs=[VMEM, hbm, VMEM, hbm],
         out_specs=(VMEM,) * 5,
-        scratch_shapes=[pltpu.SemaphoreType.DMA, pltpu.SemaphoreType.DMA],
+        scratch_shapes=[pltpu.VMEM((1, BLK), jnp.int32)] + [pltpu.SemaphoreType.DMA] * 3,
         cost_estimate=pl.CostEstimate(flops=10**11, transcendentals=0, bytes_accessed=2**22),
         compiler_params=pltpu.CompilerParams(vmem_limit_bytes=32 << 20),
-    )(at(codes, pltpu.VMEM), at(passages, pltpu.HBM), at(same, pltpu.VMEM))
+    )(
+        at(codes, pltpu.VMEM),
+        at(passages, pltpu.HBM),
+        at(same, pltpu.VMEM),
+        at(lengths.reshape(1, BLK), pltpu.HBM),
+    )
     scores, _ = pl.pallas_call(
         score_kernel,
         out_shape=(pltpu.VMEM((Z, 128), jnp.float32), every),
-        in_specs=[hbm] + [VMEM] * 6,
+        in_specs=[VMEM] * 6,
         out_specs=(VMEM, VMEM),
-        input_output_aliases={6: 1},
+        input_output_aliases={5: 1},
         scratch_shapes=[
-            pltpu.SMEM((BLK,), jnp.int32),
             pltpu.SMEM((2 * GROUP, 256), jnp.int32),
             pltpu.VMEM((GMAX, GROUP * T), jnp.float32),
-            pltpu.SemaphoreType.DMA,
             pltpu.SemaphoreType.DMA,
             pltpu.SemaphoreType.DMA,
         ],
         compiler_params=pltpu.CompilerParams(vmem_limit_bytes=32 << 20),
     )(
-        at(lengths, pltpu.HBM),
         *[at(x, pltpu.VMEM) for x in (plan, dest, onehot, other, blocks, gathered)],
     )
     back = small_call(by_plane_kernel, pltpu.VMEM((YQ, 128), jnp.float32), scores)

time: 74.2 us -> 73.9 us (level)
  no operation moved by 1% of the time
where the time goes in v12:
time: 73.9 us; the launch traced here: 73.2 us
  starting transfers between devices  40.6 us (55%)
  blocking collectives  22.6 us (31%)
  Pallas kernels  8.54 us (12%)
  local copies, waits for them, and re-layouts  0.83 us (1%)
    all_to_all x2, starting transfers between devices, exchange(): lax.all_to_all(x, ('index', 'query'), split_axis=0, concat_axis=0, tiled=...  28.1 us
    all_to_all x2, blocking collectives, exchange(): lax.all_to_all(x, ('index', 'query'), split_axis=0, concat_axis=0, tiled=...  22.6 us
    ppermute x3, starting transfers between devices, shards(): lax.ppermute(queries, 'query', [(k, (k + 2 * d) % Q) for k in range(Q)])  8.68 us
    ppermute x1, starting transfers between devices, shards(): other = lax.ppermute(same, 'query', [(k, k ^ 1) for k in range(Q)])  3.74 us
    pallas_call x1, Pallas kernels, shards(): pl.pallas_call(score_kernel, out_shape=(pltpu.VMEM((Z, 128), jnp.float32)...  3.7 us
    pallas_call x5, Pallas kernels, small_call(): pl.pallas_call(kernel, cost_estimate=hint, out_shape=out_shape, in_specs=...  3.15 us
    pallas_call x1, Pallas kernels, shards(): pl.pallas_call(sort_kernel, out_shape=(pltpu.VMEM((2 * GROUP, 256), jnp.i...  1.7 us
  transfers between devices with their start and end apart: 6, of which 1 were waited for; matrix products, arithmetic and copies ran while one was open for 0% of the time, Pallas kernels for 3%

profile of v12, /device:TPU:1, one launch (start us, length us, event | category | flops | bytes accessed | tf_op | source)
XLA Modules:
  0.0 73.2 jit_solution(3138168633145123620)
XLA Ops:
  0.0 0.0 copy-start
  0.0 0.7 copy-done
  0.7 1.2 %shard_map.46 = (s32[32,128]{1,0:T(8,128)}, s32[16,128]{1,0:T(8,128)S(1)}) custom-call(s32[16,32]{1,0:T(8,128)S(1)} %bitcast.22), custom_call_target="tpu_custom_call" | custom-call | tf_op jit(solution)/shard_map/pallas_call | solution.py:292
  1.9 13.6 %all-to-all-start = ((s32[32,1,128]{2,1,0:T(1,128)}), s32[32,1,128]{2,1,0:T(1,128)S(1)}, u32[]{:S(2)}, u32[]{:S(2)}) async-start(s32[32,1,128]{2,1,0:T(1,128)} %bitcast.2), calls=%async_computation | async-start | bytes 32768 | tf_op jit(solution)/shard_map/all_to_all | solution.py:31
  15.5 2.2 %collective-permute-start.1 = (bf16[32,32,128]{2,1,0:T(8,128)(2,1)}, bf16[32,32,128]{2,1,0:T(8,128)(2,1)S(1)}, u32[]{:S(2)}, u32[]{:S(2)}) collective-permute-start(bf16[32,32,128]{2,1,0:T(8,128)(2,1)} %param.4), channel_id=1, source_target_pairs={{0,4},{1,5},{2,6},{3,7},{4,0},{5,1},{6,2},{7,3},{8,12},{9,13},{10,... | collective-permute-start | bytes 786440 | tf_op jit(solution)/shard_map/ppermute | solution.py:303
  17.7 2.5 %collective-permute-start = (bf16[32,32,128]{2,1,0:T(8,128)(2,1)}, bf16[32,32,128]{2,1,0:T(8,128)(2,1)S(1)}, u32[]{:S(2)}, u32[]{:S(2)}) collective-permute-start(bf16[32,32,128]{2,1,0:T(8,128)(2,1)} %param.4), channel_id=1, source_target_pairs={{0,2},{1,3},{2,4},{3,5},{4,6},{5,7},{6,0},{7,1},{8,10},{9,11},{10,... | collective-permute-start | bytes 786440 | tf_op jit(solution)/shard_map/ppermute | solution.py:303
  20.2 4.0 %collective-permute-start.2 = (bf16[32,32,128]{2,1,0:T(8,128)(2,1)}, bf16[32,32,128]{2,1,0:T(8,128)(2,1)S(1)}, u32[]{:S(2)}, u32[]{:S(2)}) collective-permute-start(bf16[32,32,128]{2,1,0:T(8,128)(2,1)} %param.4), channel_id=1, source_target_pairs={{0,6},{1,7},{2,0},{3,1},{4,2},{5,3},{6,4},{7,5},{8,14},{9,15},{10,... | collective-permute-start | bytes 786440 | tf_op jit(solution)/shard_map/ppermute | solution.py:303
  24.2 0.0 all-to-all-done
  24.2 0.0 copy-start.2
  24.2 0.7 %shard_map.47 = s32[16,128]{1,0:T(8,128)} custom-call(s32[32,128]{1,0:T(8,128)S(1)} %bitcast.25), custom_call_target="tpu_custom_call" | custom-call | flops 99999997952 | bytes 1048576 | tf_op jit(solution)/shard_map/pallas_call | solution.py:292
  25.0 14.6 %all-to-all-start.1 = ((s32[16,1,128]{2,1,0:T(1,128)}), s32[16,1,128]{2,1,0:T(1,128)S(1)}, u32[]{:S(2)}, u32[]{:S(2)}) async-start(s32[16,1,128]{2,1,0:T(1,128)} %bitcast.5), calls=%async_computation.1 | async-start | bytes 16384 | tf_op jit(solution)/shard_map/all_to_all | solution.py:31
  39.5 0.0 collective-permute-done.1
  39.5 0.0 collective-permute-done
  39.5 0.0 collective-permute-done.2
  39.6 0.0 copy-done.2
  39.7 3.7 %collective-permute-start.3 = (bf16[128,32,128]{2,1,0:T(8,128)(2,1)S(1)}, bf16[128,32,128]{2,1,0:T(8,128)(2,1)S(1)}, u32[]{:S(2)}, u32[]{:S(2)}) collective-permute-start(bf16[128,32,128]{2,1,0:T(8,128)(2,1)S(1)} %constant_dynamic-update-slice_fusion.same_ref), channel_id=1, source_target_pairs={{0,1},{1,0},{2,3},{3,2},{4,5},{5,4},{6,7},{7,6},{8,9},{9,8},{10,11... | collective-permute-start | bytes 3145736 | tf_op jit(solution)/shard_map/ppermute | solution.py:318
  43.5 0.0 all-to-all-done.1
  43.5 1.7 %shard_map.48 = (s32[16,256]{1,0:T(8,128)S(1)}, s32[8,128]{1,0:T(8,128)S(1)}, bf16[192,1024]{1,0:T(8,128)(2,1)S(1)}, bf16[64,128,128]{2,1,0:T(8,128)(2,1)S(1)}, bf16[256,32,128]{2,1,0:T(8,128)(2,1)S(1)}) custom-call(s32[16,128]{1,0:T(8,128)S(1)} %bitcast.26, bf16[64,128,128]{2,1,0:T(8,128)(2,1)} %p_hbm.1, ...), custom_call_target="tpu_custom_call" | custom-call | flops 99999997952 | bytes 4194304 | tf_op jit(solution)/shard_map/pallas_call | solution.py:322
  45.2 0.5 collective-permute-done.3.other_ref
  45.7 0.0 copy-start.1
  45.7 3.7 %shard_map.49 = (f32[16,128]{1,0:T(8,128)S(1)}, bf16[256,32,128]{2,1,0:T(8,128)(2,1)S(1)}) custom-call(s32[16,256]{1,0:T(8,128)S(1)} %get-tuple-element.23.plan, s32[8,128]{1,0:T(8,128)S(1)} %get-tuple-element.24.dest_ref, bf16[192,1024]{1,0:T(8,128)(2,1)S(1)} %get-tuple-element.25.onehot_ref, ...), custom_call_target="tpu_custom_call", output_to_operand_aliasing={{1}: (5, {})} | custom-call | tf_op jit(solution)/shard_map/pallas_call | solution.py:342
  49.4 0.1 shard_map.50
  49.5 9.7 %all_to_all.44 = f32[32,1,128]{2,1,0:T(1,128)S(1)} all-to-all(f32[32,1,128]{2,1,0:T(1,128)S(1)} %bitcast.19), channel_id=1, replica_groups={{21,20,23,22,17,16,19,18,29,28,31,30,25,24,27,26,5,4,7,6,1,0,3,2,13,12,..., dimensions={0} | all-to-all | bytes 32768 | tf_op jit(solution)/shard_map/all_to_all | solution.py:31
  59.2 0.1 shard_map.51
  59.3 12.9 %all_to_all.45 = f32[16,1,128]{2,1,0:T(1,128)S(1)} all-to-all(f32[16,1,128]{2,1,0:T(1,128)S(1)} %bitcast.21), channel_id=1, replica_groups={{256,288,320,352,384,416,448,480,0,32,64,96,128,160,192,224},{257,289,3..., dimensions={0} | all-to-all | bytes 16384 | tf_op jit(solution)/shard_map/all_to_all | solution.py:31
  72.2 0.0 copy-done.1
  72.2 1.0 %shard_map.52 = f32[16,32]{1,0:T(8,128)} custom-call(s32[16,32]{1,0:T(8,128)S(1)} %bitcast.23, s32[16,128]{1,0:T(8,128)S(1)} %get-tuple-element.17.key_ref, f32[16,128]{1,0:T(8,128)S(1)} %bitcast.24), custom_call_target="tpu_custom_call" | custom-call | tf_op jit(solution)/shard_map/pallas_call | solution.py:292
  (4 shorter events, 0.1 us)
Async XLA Ops:
  0.0 0.7 copy-start
  1.9 22.3 %all-to-all-start = ((s32[32,1,128]{2,1,0:T(1,128)}), s32[32,1,128]{2,1,0:T(1,128)S(1)}, u32[]{:S(2)}, u32[]{:S(2)}) async-start(s32[32,1,128]{2,1,0:T(1,128)} %bitcast.2), calls=%async_computation | async-start | bytes 32768 | tf_op jit(solution)/shard_map/all_to_all | solution.py:31
  15.5 24.0 %collective-permute-start.1 = (bf16[32,32,128]{2,1,0:T(8,128)(2,1)}, bf16[32,32,128]{2,1,0:T(8,128)(2,1)S(1)}, u32[]{:S(2)}, u32[]{:S(2)}) collective-permute-start(bf16[32,32,128]{2,1,0:T(8,128)(2,1)} %param.4), channel_id=1, source_target_pairs={{0,4},{1,5},{2,6},{3,7},{4,0},{5,1},{6,2},{7,3},{8,12},{9,13},{10,... | collective-permute-start | bytes 786440 | tf_op jit(solution)/shard_map/ppermute | solution.py:303
  17.7 21.8 %collective-permute-start = (bf16[32,32,128]{2,1,0:T(8,128)(2,1)}, bf16[32,32,128]{2,1,0:T(8,128)(2,1)S(1)}, u32[]{:S(2)}, u32[]{:S(2)}) collective-permute-start(bf16[32,32,128]{2,1,0:T(8,128)(2,1)} %param.4), channel_id=1, source_target_pairs={{0,2},{1,3},{2,4},{3,5},{4,6},{5,7},{6,0},{7,1},{8,10},{9,11},{10,... | collective-permute-start | bytes 786440 | tf_op jit(solution)/shard_map/ppermute | solution.py:303
  20.2 19.4 %collective-permute-start.2 = (bf16[32,32,128]{2,1,0:T(8,128)(2,1)}, bf16[32,32,128]{2,1,0:T(8,128)(2,1)S(1)}, u32[]{:S(2)}, u32[]{:S(2)}) collective-permute-start(bf16[32,32,128]{2,1,0:T(8,128)(2,1)} %param.4), channel_id=1, source_target_pairs={{0,6},{1,7},{2,0},{3,1},{4,2},{5,3},{6,4},{7,5},{8,14},{9,15},{10,... | collective-permute-start | bytes 786440 | tf_op jit(solution)/shard_map/ppermute | solution.py:303
  24.2 15.3 %copy-start.2 = (bf16[32,32,128]{2,1,0:T(8,128)(2,1)S(1)}, bf16[32,32,128]{2,1,0:T(8,128)(2,1)}, u32[]{:S(2)}) copy-start(bf16[32,32,128]{2,1,0:T(8,128)(2,1)} %param.4) | copy-start | bytes 786436
  25.0 18.5 %all-to-all-start.1 = ((s32[16,1,128]{2,1,0:T(1,128)}), s32[16,1,128]{2,1,0:T(1,128)S(1)}, u32[]{:S(2)}, u32[]{:S(2)}) async-start(s32[16,1,128]{2,1,0:T(1,128)} %bitcast.5), calls=%async_computation.1 | async-start | bytes 16384 | tf_op jit(solution)/shard_map/all_to_all | solution.py:31
  39.7 6.0 %collective-permute-start.3 = (bf16[128,32,128]{2,1,0:T(8,128)(2,1)S(1)}, bf16[128,32,128]{2,1,0:T(8,128)(2,1)S(1)}, u32[]{:S(2)}, u32[]{:S(2)}) collective-permute-start(bf16[128,32,128]{2,1,0:T(8,128)(2,1)S(1)} %constant_dynamic-update-slice_fusion.same_ref), channel_id=1, source_target_pairs={{0,1},{1,0},{2,3},{3,2},{4,5},{5,4},{6,7},{7,6},{8,9},{9,8},{10,11... | collective-permute-start | bytes 3145736 | tf_op jit(solution)/shard_map/ppermute | solution.py:318
  45.7 26.4 %copy-start.1 = (s32[32,16]{0,1:T(8,128)S(1)}, s32[32,16]{0,1:T(8,128)}, u32[]{:S(2)}) copy-start(s32[32,16]{0,1:T(8,128)} %param.7) | copy-start | bytes 6148

commit v13 on v12

--- a/solution.py
+++ b/solution.py
@@ -102,15 +102,12 @@
 
 
 def sort_kernel(
-    code_ref, p_hbm, same_ref, len_hbm, plan_ref, dest_ref, onehot_ref, p_ref, q_ref,
-    len_ref, p_sem, q_sem, len_sem,
+    code_ref, same_ref, len_hbm, plan_ref, dest_ref, onehot_ref, q_ref, len_ref, q_sem, len_sem
 ):
     len_copy = pltpu.make_async_copy(len_hbm, len_ref, len_sem)
     len_copy.start()
     q_copy = pltpu.make_async_copy(same_ref, q_ref.at[pl.ds(0, NQ // 2)], q_sem)
     q_copy.start()
-    p_copy = pltpu.make_async_copy(p_hbm, p_ref, p_sem)
-    p_copy.start()
     lane8 = iota((Q, 128), 1)
     code = jnp.where(lane8 < 64, code_ref[0:8, :], pltpu.roll(code_ref[8:16, :], 64, 1))
     valid = code >= 0
@@ -180,8 +177,13 @@
             jnp.broadcast_to(live, (GROUP, 256)),
         ),
     )
-    p_copy.wait()
     q_copy.wait()
+
+
+def fetch_kernel(_, p_hbm, p_ref, sem):
+    copy = pltpu.make_async_copy(p_hbm, p_ref, sem)
+    copy.start()
+    copy.wait()
 
 
 def in_group(dest):
@@ -313,29 +315,37 @@
     hint = pl.CostEstimate(flops=10**11, transcendentals=0, bytes_accessed=2**20)
     got = small_call(by_z_kernel, pltpu.VMEM((Z, 128), jnp.int32), got, hint=hint)
     codes = exchange(got, Z_GROUPS)
+    blocks = pl.pallas_call(
+        fetch_kernel,
+        out_shape=pltpu.VMEM(passages.shape, passages.dtype),
+        in_specs=[VMEM, pl.BlockSpec(memory_space=pltpu.HBM)],
+        out_specs=VMEM,
+        scratch_shapes=[pltpu.SemaphoreType.DMA],
+    )(
+        pltpu.with_memory_space_constraint(got, pltpu.VMEM),
+        pltpu.with_memory_space_constraint(passages, pltpu.HBM),
+    )
     _, *same = lax.optimization_barrier((got, *same))
     same = jnp.concatenate(same, axis=0)
     other = lax.ppermute(same, "query", [(k, k ^ 1) for k in range(Q)])
     at = pltpu.with_memory_space_constraint
     hbm = pl.BlockSpec(memory_space=pltpu.HBM)
     every = pltpu.VMEM((NQ, T, D), queries.dtype)
-    plan, dest, onehot, blocks, gathered = pl.pallas_call(
+    plan, dest, onehot, gathered = pl.pallas_call(
         sort_kernel,
         out_shape=(
             pltpu.VMEM((2 * GROUP, 256), jnp.int32),
             pltpu.VMEM((Q, 128), jnp.int32),
             pltpu.VMEM((GMAX, Q * 128), jnp.bfloat16),
-            pltpu.VMEM(passages.shape, passages.dtype),
             every,
         ),
-        in_specs=[VMEM, hbm, VMEM, hbm],
-        out_specs=(VMEM,) * 5,
-        scratch_shapes=[pltpu.VMEM((1, BLK), jnp.int32)] + [pltpu.SemaphoreType.DMA] * 3,
+        in_specs=[VMEM, VMEM, hbm],
+        out_specs=(VMEM,) * 4,
+        scratch_shapes=[pltpu.VMEM((1, BLK), jnp.int32)] + [pltpu.SemaphoreType.DMA] * 2,
         cost_estimate=pl.CostEstimate(flops=10**11, transcendentals=0, bytes_accessed=2**22),
         compiler_params=pltpu.CompilerParams(vmem_limit_bytes=32 << 20),
     )(
         at(codes, pltpu.VMEM),
-        at(passages, pltpu.HBM),
         at(same, pltpu.VMEM),
         at(lengths.reshape(1, BLK), pltpu.HBM),
     )

time: 73.9 us -> 78.8 us (1.066)
  Pallas kernels: 8.54 us -> 11.4 us
  local copies, waits for them, and re-layouts: 0.83 us -> 3.58 us
  blocking collectives: 22.6 us -> 21.8 us
    pallas_call x0 -> x1, Pallas kernels: none -> 2.36 us  [shards(): pl.pallas_call(fetch_kernel, out_shape=pltpu.VMEM(passages.shape, passage...]
    unnamed x9, local copies, waits for them, and re-layouts: 0.8 us -> 2.85 us
  transfers between devices with their start and end apart: 6 -> 6, of which waited for: 1 -> 1; matrix products, arithmetic and copies ran while one was open for 0% -> 4% of each run, Pallas kernels for 3% -> 7%
where the time goes in v13:
time: 78.8 us; the launch traced here: 77.8 us
  starting transfers between devices  40.5 us (51%)
  blocking collectives  21.8 us (28%)
  Pallas kernels  11.4 us (14%)
  local copies, waits for them, and re-layouts  3.58 us (5%)
    all_to_all x2, starting transfers between devices, exchange(): lax.all_to_all(x, ('index', 'query'), split_axis=0, concat_axis=0, tiled=...  28.1 us
    all_to_all x2, blocking collectives, exchange(): lax.all_to_all(x, ('index', 'query'), split_axis=0, concat_axis=0, tiled=...  21.8 us
    ppermute x3, starting transfers between devices, shards(): lax.ppermute(queries, 'query', [(k, (k + 2 * d) % Q) for k in range(Q)])  8.68 us
    ppermute x1, starting transfers between devices, shards(): other = lax.ppermute(same, 'query', [(k, k ^ 1) for k in range(Q)])  3.72 us
    pallas_call x1, Pallas kernels, shards(): pl.pallas_call(score_kernel, out_shape=(pltpu.VMEM((Z, 128), jnp.float32)...  3.71 us
    pallas_call x5, Pallas kernels, small_call(): pl.pallas_call(kernel, cost_estimate=hint, out_shape=out_shape, in_specs=...  3.15 us
    unnamed x9, local copies, waits for them, and re-layouts  2.85 us
    pallas_call x1, Pallas kernels, shards(): pl.pallas_call(fetch_kernel, out_shape=pltpu.VMEM(passages.shape, passage...  2.36 us
  transfers between devices with their start and end apart: 6, of which 1 were waited for; matrix products, arithmetic and copies ran while one was open for 4% of the time, Pallas kernels for 7%

profile of v13, /device:TPU:1, one launch (start us, length us, event | category | flops | bytes accessed | tf_op | source)
XLA Modules:
  0.0 77.8 jit_solution(15609681281310432190)
XLA Ops:
  0.0 0.0 copy-start
  0.0 0.7 copy-done
  0.7 1.2 %shard_map.46 = (s32[32,128]{1,0:T(8,128)}, s32[16,128]{1,0:T(8,128)S(1)}) custom-call(s32[16,32]{1,0:T(8,128)S(1)} %bitcast.22), custom_call_target="tpu_custom_call" | custom-call | tf_op jit(solution)/shard_map/pallas_call | solution.py:294
  1.9 13.6 %all-to-all-start = ((s32[32,1,128]{2,1,0:T(1,128)}), s32[32,1,128]{2,1,0:T(1,128)S(1)}, u32[]{:S(2)}, u32[]{:S(2)}) async-start(s32[32,1,128]{2,1,0:T(1,128)} %bitcast.2), calls=%async_computation | async-start | bytes 32768 | tf_op jit(solution)/shard_map/all_to_all | solution.py:31
  15.5 2.2 %collective-permute-start.1 = (bf16[32,32,128]{2,1,0:T(8,128)(2,1)}, bf16[32,32,128]{2,1,0:T(8,128)(2,1)S(1)}, u32[]{:S(2)}, u32[]{:S(2)}) collective-permute-start(bf16[32,32,128]{2,1,0:T(8,128)(2,1)} %param.4), channel_id=1, source_target_pairs={{0,4},{1,5},{2,6},{3,7},{4,0},{5,1},{6,2},{7,3},{8,12},{9,13},{10,... | collective-permute-start | bytes 786440 | tf_op jit(solution)/shard_map/ppermute | solution.py:305
  17.7 2.5 %collective-permute-start = (bf16[32,32,128]{2,1,0:T(8,128)(2,1)}, bf16[32,32,128]{2,1,0:T(8,128)(2,1)S(1)}, u32[]{:S(2)}, u32[]{:S(2)}) collective-permute-start(bf16[32,32,128]{2,1,0:T(8,128)(2,1)} %param.4), channel_id=1, source_target_pairs={{0,2},{1,3},{2,4},{3,5},{4,6},{5,7},{6,0},{7,1},{8,10},{9,11},{10,... | collective-permute-start | bytes 786440 | tf_op jit(solution)/shard_map/ppermute | solution.py:305
  20.2 4.0 %collective-permute-start.2 = (bf16[32,32,128]{2,1,0:T(8,128)(2,1)}, bf16[32,32,128]{2,1,0:T(8,128)(2,1)S(1)}, u32[]{:S(2)}, u32[]{:S(2)}) collective-permute-start(bf16[32,32,128]{2,1,0:T(8,128)(2,1)} %param.4), channel_id=1, source_target_pairs={{0,6},{1,7},{2,0},{3,1},{4,2},{5,3},{6,4},{7,5},{8,14},{9,15},{10,... | collective-permute-start | bytes 786440 | tf_op jit(solution)/shard_map/ppermute | solution.py:305
  24.2 0.0 all-to-all-done
  24.2 0.7 shard_map.47._
  25.0 14.6 %all-to-all-start.1 = ((s32[16,1,128]{2,1,0:T(1,128)}), s32[16,1,128]{2,1,0:T(1,128)S(1)}, u32[]{:S(2)}, u32[]{:S(2)}) async-start(s32[16,1,128]{2,1,0:T(1,128)} %bitcast.5), calls=%async_computation.1 | async-start | bytes 16384 | tf_op jit(solution)/shard_map/all_to_all | solution.py:31
  39.5 0.0 copy-start.2
  39.5 2.4 %shard_map.49.p_ref = bf16[64,128,128]{2,1,0:T(8,128)(2,1)S(1)} custom-call(s32[16,128]{1,0:T(8,128)} %shard_map.47._, bf16[64,128,128]{2,1,0:T(8,128)(2,1)} %p_hbm.1), custom_call_target="tpu_custom_call" | custom-call | tf_op jit(solution)/shard_map/pallas_call | solution.py:318
  41.9 0.0 collective-permute-done.1
  41.9 0.0 collective-permute-done
  41.9 0.0 collective-permute-done.2
  41.9 0.0 copy-done.2
  41.9 0.7 constant_dynamic-update-slice_fusion.3
  42.6 0.7 constant_dynamic-update-slice_fusion.2
  43.4 0.7 constant_dynamic-update-slice_fusion.1
  44.1 0.7 constant_dynamic-update-slice_fusion.same_ref
  44.8 3.7 %collective-permute-start.3 = (bf16[128,32,128]{2,1,0:T(8,128)(2,1)}, bf16[128,32,128]{2,1,0:T(8,128)(2,1)S(1)}, u32[]{:S(2)}, u32[]{:S(2)}) collective-permute-start(bf16[128,32,128]{2,1,0:T(8,128)(2,1)} %constant_dynamic-update-slice_fusion.same_ref), channel_id=1, source_target_pairs={{0,1},{1,0},{2,3},{3,2},{4,5},{5,4},{6,7},{7,6},{8,9},{9,8},{10,11... | collective-permute-start | bytes 3145736 | tf_op jit(solution)/shard_map/ppermute | solution.py:330
  48.5 0.0 all-to-all-done.1
  48.6 2.2 %shard_map.48 = (s32[16,256]{1,0:T(8,128)S(1)}, s32[8,128]{1,0:T(8,128)S(1)}, bf16[192,1024]{1,0:T(8,128)(2,1)S(1)}, bf16[256,32,128]{2,1,0:T(8,128)(2,1)S(1)}) custom-call(s32[16,128]{1,0:T(8,128)S(1)} %bitcast.26, bf16[128,32,128]{2,1,0:T(8,128)(2,1)} %constant_dynamic-update-slice_fusion.same_ref, s32[1,64]{1,0:T(1,128)} %bitcast.27), custom_call_target="tpu_custom_call" | custom-call | flops 99999997952 | bytes 4194304 | tf_op jit(solution)/shard_map/pallas_call | solution.py:334
  50.7 0.3 collective-permute-done.3.other_ref
  51.0 0.0 copy-start.1
  51.0 3.7 %shard_map.50 = (f32[16,128]{1,0:T(8,128)S(1)}, bf16[256,32,128]{2,1,0:T(8,128)(2,1)S(1)}) custom-call(s32[16,256]{1,0:T(8,128)S(1)} %get-tuple-element.22.plan, s32[8,128]{1,0:T(8,128)S(1)} %get-tuple-element.23.dest_ref, bf16[192,1024]{1,0:T(8,128)(2,1)S(1)} %get-tuple-element.24.onehot_ref, ...), custom_call_target="tpu_custom_call", output_to_operand_aliasing={{1}: (5, {})} | custom-call | tf_op jit(solution)/shard_map/pallas_call | solution.py:352
  54.7 0.1 shard_map.51
  54.8 8.9 %all_to_all.44 = f32[32,1,128]{2,1,0:T(1,128)S(1)} all-to-all(f32[32,1,128]{2,1,0:T(1,128)S(1)} %bitcast.19), channel_id=1, replica_groups={{21,20,23,22,17,16,19,18,29,28,31,30,25,24,27,26,5,4,7,6,1,0,3,2,13,12,..., dimensions={0} | all-to-all | bytes 32768 | tf_op jit(solution)/shard_map/all_to_all | solution.py:31
  63.8 0.1 shard_map.52
  63.9 12.9 %all_to_all.45 = f32[16,1,128]{2,1,0:T(1,128)S(1)} all-to-all(f32[16,1,128]{2,1,0:T(1,128)S(1)} %bitcast.21), channel_id=1, replica_groups={{256,288,320,352,384,416,448,480,0,32,64,96,128,160,192,224},{257,289,3..., dimensions={0} | all-to-all | bytes 16384 | tf_op jit(solution)/shard_map/all_to_all | solution.py:31
  76.7 0.0 copy-done.1
  76.7 1.0 %shard_map.53 = f32[16,32]{1,0:T(8,128)} custom-call(s32[16,32]{1,0:T(8,128)S(1)} %bitcast.23, s32[16,128]{1,0:T(8,128)S(1)} %get-tuple-element.16.key_ref, f32[16,128]{1,0:T(8,128)S(1)} %bitcast.24), custom_call_target="tpu_custom_call" | custom-call | tf_op jit(solution)/shard_map/pallas_call | solution.py:294
Async XLA Ops:
  0.0 0.7 copy-start
  1.9 22.3 %all-to-all-start = ((s32[32,1,128]{2,1,0:T(1,128)}), s32[32,1,128]{2,1,0:T(1,128)S(1)}, u32[]{:S(2)}, u32[]{:S(2)}) async-start(s32[32,1,128]{2,1,0:T(1,128)} %bitcast.2), calls=%async_computation | async-start | bytes 32768 | tf_op jit(solution)/shard_map/all_to_all | solution.py:31
  15.5 26.4 %collective-permute-start.1 = (bf16[32,32,128]{2,1,0:T(8,128)(2,1)}, bf16[32,32,128]{2,1,0:T(8,128)(2,1)S(1)}, u32[]{:S(2)}, u32[]{:S(2)}) collective-permute-start(bf16[32,32,128]{2,1,0:T(8,128)(2,1)} %param.4), channel_id=1, source_target_pairs={{0,4},{1,5},{2,6},{3,7},{4,0},{5,1},{6,2},{7,3},{8,12},{9,13},{10,... | collective-permute-start | bytes 786440 | tf_op jit(solution)/shard_map/ppermute | solution.py:305
  17.7 24.2 %collective-permute-start = (bf16[32,32,128]{2,1,0:T(8,128)(2,1)}, bf16[32,32,128]{2,1,0:T(8,128)(2,1)S(1)}, u32[]{:S(2)}, u32[]{:S(2)}) collective-permute-start(bf16[32,32,128]{2,1,0:T(8,128)(2,1)} %param.4), channel_id=1, source_target_pairs={{0,2},{1,3},{2,4},{3,5},{4,6},{5,7},{6,0},{7,1},{8,10},{9,11},{10,... | collective-permute-start | bytes 786440 | tf_op jit(solution)/shard_map/ppermute | solution.py:305
  20.2 21.7 %collective-permute-start.2 = (bf16[32,32,128]{2,1,0:T(8,128)(2,1)}, bf16[32,32,128]{2,1,0:T(8,128)(2,1)S(1)}, u32[]{:S(2)}, u32[]{:S(2)}) collective-permute-start(bf16[32,32,128]{2,1,0:T(8,128)(2,1)} %param.4), channel_id=1, source_target_pairs={{0,6},{1,7},{2,0},{3,1},{4,2},{5,3},{6,4},{7,5},{8,14},{9,15},{10,... | collective-permute-start | bytes 786440 | tf_op jit(solution)/shard_map/ppermute | solution.py:305
  25.0 23.6 %all-to-all-start.1 = ((s32[16,1,128]{2,1,0:T(1,128)}), s32[16,1,128]{2,1,0:T(1,128)S(1)}, u32[]{:S(2)}, u32[]{:S(2)}) async-start(s32[16,1,128]{2,1,0:T(1,128)} %bitcast.5), calls=%async_computation.1 | async-start | bytes 16384 | tf_op jit(solution)/shard_map/all_to_all | solution.py:31
  39.5 2.4 %copy-start.2 = (bf16[32,32,128]{2,1,0:T(8,128)(2,1)S(1)}, bf16[32,32,128]{2,1,0:T(8,128)(2,1)}, u32[]{:S(2)}) copy-start(bf16[32,32,128]{2,1,0:T(8,128)(2,1)} %param.4) | copy-start | bytes 786436
  44.8 6.2 %collective-permute-start.3 = (bf16[128,32,128]{2,1,0:T(8,128)(2,1)}, bf16[128,32,128]{2,1,0:T(8,128)(2,1)S(1)}, u32[]{:S(2)}, u32[]{:S(2)}) collective-permute-start(bf16[128,32,128]{2,1,0:T(8,128)(2,1)} %constant_dynamic-update-slice_fusion.same_ref), channel_id=1, source_target_pairs={{0,1},{1,0},{2,3},{3,2},{4,5},{5,4},{6,7},{7,6},{8,9},{9,8},{10,11... | collective-permute-start | bytes 3145736 | tf_op jit(solution)/shard_map/ppermute | solution.py:330
  51.0 25.7 %copy-start.1 = (s32[32,16]{0,1:T(8,128)S(1)}, s32[32,16]{0,1:T(8,128)}, u32[]{:S(2)}) copy-start(s32[32,16]{0,1:T(8,128)} %param.7) | copy-start | bytes 6148

commit v14 on v7

--- a/solution.py
+++ b/solution.py
@@ -17,8 +17,10 @@
 UNROLL = 32
 BIG = 1 << 30
 
-Z_GROUPS = [[r + YQ * z for z in range(Z)] for r in range(YQ)]
-YQ_GROUPS = [[YQ * z + r for r in range(YQ)] for z in range(Z)]
+FIRST_Z, FIRST_YQ = Z // 2, (Y // 2) * Q + Q // 2 + 1
+FIRST = FIRST_Z * YQ + FIRST_YQ
+Z_GROUPS = [[r + YQ * (z ^ FIRST_Z) for z in range(Z)] for r in range(YQ)]
+YQ_GROUPS = [[YQ * z + (r ^ FIRST_YQ) for r in range(YQ)] for z in range(Z)]
 
 
 def iota(shape, axis):
@@ -73,7 +75,7 @@
     for q in range(QL):
         col = cand[:, q : q + 1]
         key = (q << 10) + (sub << 6) + (col & 63)
-        match = (col >> 6) == lane_owner
+        match = ((col >> 6) ^ FIRST) == lane_owner
         low = jnp.minimum(low, jnp.where(match, key, BIG))
         high = jnp.maximum(high, jnp.where(match, key, -1))
     last = jnp.max(high, axis=0, keepdims=True)
@@ -97,6 +99,10 @@
 
 def dot(a, b, dims):
     return lax.dot_general(a, b, (dims, ((), ())), preferred_element_type=jnp.float32)
+
+
+def pass_kernel(x_ref, o_ref):
+    o_ref[...] = x_ref[...]
 
 
 def score_kernel(
@@ -117,7 +123,7 @@
     valid = code >= 0
     block = jnp.where(valid, code & 63, BLK)
     me = lax.axis_index("query")
-    source = lane8 & (Q - 1)
+    source = (lane8 ^ FIRST_YQ) & (Q - 1)
     piece = (((source ^ me) & 1) << 2) + (((me >> 1) - (source >> 1)) & 3)
     query = jnp.where(valid, (code >> 6) + QL * piece, 0)
 
@@ -229,7 +235,7 @@
     asked = jnp.concatenate(segs, axis=1)
     place = iota((1, QL * CL), 1)
     own_key = ((place & 31) << 10) + ((place >> 5) << 6) + (asked & 63)
-    owner = asked >> 6
+    owner = (asked >> 6) ^ FIRST
     lane_z = iota((Z, 128), 1)
     x = jnp.where(lane_z < 2 * YQ, x_ref[...], 0.0)
     key = jnp.where(lane_z < YQ, key_ref[...], 0)
@@ -292,10 +298,12 @@
     hint = pl.CostEstimate(flops=10**11, transcendentals=0, bytes_accessed=2**20)
     got = small_call(by_z_kernel, pltpu.VMEM((Z, 128), jnp.int32), got, hint=hint)
     codes = exchange(got, Z_GROUPS)
+    _, *same = lax.optimization_barrier((got, *same))
     same = jnp.concatenate(same, axis=0)
-    codes, same = lax.optimization_barrier((codes, same))
     other = lax.ppermute(same, "query", [(k, k ^ 1) for k in range(Q)])
+    at = pltpu.with_memory_space_constraint
     hbm = pl.BlockSpec(memory_space=pltpu.HBM)
+    codes = small_call(pass_kernel, pltpu.VMEM((Z, 128), jnp.int32), codes, hint=hint)
     scores = pl.pallas_call(
         score_kernel,
         out_shape=pltpu.VMEM((Z, 128), jnp.float32),

time: 87.4 us -> 74.3 us (0.85)
  waiting for transfers between devices: 13.3 us -> 2.24 us
  blocking collectives: 25.5 us -> 21.8 us
  starting transfers between devices: 39.5 us -> 40.6 us
    all_to_all x2, waiting for transfers between devices: 11 us -> 0.01 us  [exchange(): lax.all_to_all(x, ('index', 'query'), split_axis=0, concat_axis=0, tiled=...]
    all_to_all x2, starting transfers between devices: 23.5 us -> 28.1 us  [exchange(): lax.all_to_all(x, ('index', 'query'), split_axis=0, concat_axis=0, tiled=...]
    all_to_all x2, blocking collectives: 25.5 us -> 21.8 us  [exchange(): lax.all_to_all(x, ('index', 'query'), split_axis=0, concat_axis=0, tiled=...]
    ppermute x3, starting transfers between devices: 11.3 us -> 8.68 us  [shards(): lax.ppermute(queries, 'query', [(k, (k + 2 * d) % Q) for k in range(Q)])]
    ppermute x1, starting transfers between devices: 4.66 us -> 3.74 us  [shards(): other = lax.ppermute(same, 'query', [(k, k ^ 1) for k in range(Q)])]
    pallas_call x5 -> x6, Pallas kernels: 3.15 us -> 3.15 us  [small_call(): pl.pallas_call(kernel, cost_estimate=hint, out_shape=out_shape, in_specs=...]
  transfers between devices with their start and end apart: 6 -> 6, of which waited for: 2 -> 1; matrix products, arithmetic and copies ran while one was open for 0% -> 0% of each run, Pallas kernels for 1% -> 1%
where the time goes in v14:
time: 74.3 us; the launch traced here: 73.4 us
  starting transfers between devices  40.6 us (55%)
  blocking collectives  21.8 us (29%)
  Pallas kernels  7.77 us (10%)
  waiting for transfers between devices  2.24 us (3%)
  local copies, waits for them, and re-layouts  0.84 us (1%)
    all_to_all x2, starting transfers between devices, exchange(): lax.all_to_all(x, ('index', 'query'), split_axis=0, concat_axis=0, tiled=...  28.1 us
    all_to_all x2, blocking collectives, exchange(): lax.all_to_all(x, ('index', 'query'), split_axis=0, concat_axis=0, tiled=...  21.8 us
    ppermute x3, starting transfers between devices, shards(): lax.ppermute(queries, 'query', [(k, (k + 2 * d) % Q) for k in range(Q)])  8.68 us
    pallas_call x1, Pallas kernels, shards(): pl.pallas_call(score_kernel, out_shape=pltpu.VMEM((Z, 128), jnp.float32),...  4.62 us
    ppermute x1, starting transfers between devices, shards(): other = lax.ppermute(same, 'query', [(k, k ^ 1) for k in range(Q)])  3.74 us
    pallas_call x6, Pallas kernels, small_call(): pl.pallas_call(kernel, cost_estimate=hint, out_shape=out_shape, in_specs=...  3.15 us
    ppermute x1, waiting for transfers between devices, shards(): other = lax.ppermute(same, 'query', [(k, k ^ 1) for k in range(Q)])  2.23 us
  transfers between devices with their start and end apart: 6, of which 1 were waited for; matrix products, arithmetic and copies ran while one was open for 0% of the time, Pallas kernels for 1%

profile of v14, /device:TPU:1, one launch (start us, length us, event | category | flops | bytes accessed | tf_op | source)
XLA Modules:
  0.0 73.4 jit_solution(13995285734830298698)
XLA Ops:
  0.0 0.0 copy-start
  0.0 0.7 copy-done
  0.7 1.2 %shard_map.46 = (s32[32,128]{1,0:T(8,128)}, s32[16,128]{1,0:T(8,128)S(1)}) custom-call(s32[16,32]{1,0:T(8,128)S(1)} %bitcast.21), custom_call_target="tpu_custom_call" | custom-call | tf_op jit(solution)/shard_map/pallas_call | solution.py:277
  1.9 13.6 %all-to-all-start = ((s32[32,1,128]{2,1,0:T(1,128)}), s32[32,1,128]{2,1,0:T(1,128)S(1)}, u32[]{:S(2)}, u32[]{:S(2)}) async-start(s32[32,1,128]{2,1,0:T(1,128)} %bitcast.2), calls=%async_computation | async-start | bytes 32768 | tf_op jit(solution)/shard_map/all_to_all | solution.py:31
  15.5 2.2 %collective-permute-start.1 = (bf16[32,32,128]{2,1,0:T(8,128)(2,1)}, bf16[32,32,128]{2,1,0:T(8,128)(2,1)S(1)}, u32[]{:S(2)}, u32[]{:S(2)}) collective-permute-start(bf16[32,32,128]{2,1,0:T(8,128)(2,1)} %param.4), channel_id=1, source_target_pairs={{0,4},{1,5},{2,6},{3,7},{4,0},{5,1},{6,2},{7,3},{8,12},{9,13},{10,... | collective-permute-start | bytes 786440 | tf_op jit(solution)/shard_map/ppermute | solution.py:288
  17.7 2.5 %collective-permute-start = (bf16[32,32,128]{2,1,0:T(8,128)(2,1)}, bf16[32,32,128]{2,1,0:T(8,128)(2,1)S(1)}, u32[]{:S(2)}, u32[]{:S(2)}) collective-permute-start(bf16[32,32,128]{2,1,0:T(8,128)(2,1)} %param.4), channel_id=1, source_target_pairs={{0,2},{1,3},{2,4},{3,5},{4,6},{5,7},{6,0},{7,1},{8,10},{9,11},{10,... | collective-permute-start | bytes 786440 | tf_op jit(solution)/shard_map/ppermute | solution.py:288
  20.2 4.0 %collective-permute-start.2 = (bf16[32,32,128]{2,1,0:T(8,128)(2,1)}, bf16[32,32,128]{2,1,0:T(8,128)(2,1)S(1)}, u32[]{:S(2)}, u32[]{:S(2)}) collective-permute-start(bf16[32,32,128]{2,1,0:T(8,128)(2,1)} %param.4), channel_id=1, source_target_pairs={{0,6},{1,7},{2,0},{3,1},{4,2},{5,3},{6,4},{7,5},{8,14},{9,15},{10,... | collective-permute-start | bytes 786440 | tf_op jit(solution)/shard_map/ppermute | solution.py:288
  24.2 0.0 all-to-all-done
  24.2 0.0 copy-start.2
  24.2 0.7 %shard_map.47 = s32[16,128]{1,0:T(8,128)} custom-call(s32[32,128]{1,0:T(8,128)S(1)} %bitcast.24), custom_call_target="tpu_custom_call" | custom-call | flops 99999997952 | bytes 1048576 | tf_op jit(solution)/shard_map/pallas_call | solution.py:277
  25.0 14.6 %all-to-all-start.1 = ((s32[16,1,128]{2,1,0:T(1,128)}), s32[16,1,128]{2,1,0:T(1,128)S(1)}, u32[]{:S(2)}, u32[]{:S(2)}) async-start(s32[16,1,128]{2,1,0:T(1,128)} %bitcast.5), calls=%async_computation.1 | async-start | bytes 16384 | tf_op jit(solution)/shard_map/all_to_all | solution.py:31
  39.5 0.0 collective-permute-done.1
  39.5 0.0 collective-permute-done
  39.5 0.0 collective-permute-done.2
  39.6 0.0 copy-done.2
  39.7 3.7 %collective-permute-start.3 = (bf16[128,32,128]{2,1,0:T(8,128)(2,1)S(1)}, bf16[128,32,128]{2,1,0:T(8,128)(2,1)S(1)}, u32[]{:S(2)}, u32[]{:S(2)}) collective-permute-start(bf16[128,32,128]{2,1,0:T(8,128)(2,1)S(1)} %constant_dynamic-update-slice_fusion.same_ref), channel_id=1, source_target_pairs={{0,1},{1,0},{2,3},{3,2},{4,5},{5,4},{6,7},{7,6},{8,9},{9,8},{10,11... | collective-permute-start | bytes 3145736 | tf_op jit(solution)/shard_map/ppermute | solution.py:303
  43.5 0.0 all-to-all-done.1
  43.5 0.0 copy-start.1
  43.5 2.2 %collective-permute-done.3.other_ref = bf16[128,32,128]{2,1,0:T(8,128)(2,1)S(1)} collective-permute-done((bf16[128,32,128]{2,1,0:T(8,128)(2,1)S(1)}, bf16[128,32,128]{2,1,0:T(8,128)(2,1)S(1)}, u32[]{:S(2)}, u32[]{:S(2)}) %collective-permute-start.3) | collective-permute-done | bytes 1048608 | tf_op jit(solution)/shard_map/ppermute | solution.py:303
  45.7 4.6 %shard_map.49.x_ref = f32[16,128]{1,0:T(8,128)S(1)} custom-call(s32[64]{0:T(128)} %len_hbm.1, s32[16,128]{1,0:T(8,128)S(1)} %shard_map.48.code_ref, bf16[128,32,128]{2,1,0:T(8,128)(2,1)S(1)} %constant_dynamic-update-slice_fusion.same_ref, bf16[128,32,128]{2,1,0:T(8,128)(2,1)S(1)} %collective-permute-done.3.other_ref, bf16[64,128,128]{2,1,0:T(8,128)(2,1)} %p_hbm.1), custom_call_target="tpu_custom_call" | custom-call | tf_op jit(solution)/shard_map/pallas_call | solution.py:307
  50.4 0.1 shard_map.50
  50.5 8.9 %all_to_all.44 = f32[32,1,128]{2,1,0:T(1,128)S(1)} all-to-all(f32[32,1,128]{2,1,0:T(1,128)S(1)} %bitcast.18), channel_id=1, replica_groups={{21,20,23,22,17,16,19,18,29,28,31,30,25,24,27,26,5,4,7,6,1,0,3,2,13,12,..., dimensions={0} | all-to-all | bytes 32768 | tf_op jit(solution)/shard_map/all_to_all | solution.py:31
  59.4 0.1 shard_map.51
  59.5 12.9 %all_to_all.45 = f32[16,1,128]{2,1,0:T(1,128)S(1)} all-to-all(f32[16,1,128]{2,1,0:T(1,128)S(1)} %bitcast.20), channel_id=1, replica_groups={{256,288,320,352,384,416,448,480,0,32,64,96,128,160,192,224},{257,289,3..., dimensions={0} | all-to-all | bytes 16384 | tf_op jit(solution)/shard_map/all_to_all | solution.py:31
  72.3 0.0 copy-done.1
  72.3 1.0 %shard_map.52 = f32[16,32]{1,0:T(8,128)} custom-call(s32[16,32]{1,0:T(8,128)S(1)} %bitcast.22, s32[16,128]{1,0:T(8,128)S(1)} %get-tuple-element.11.key_ref, f32[16,128]{1,0:T(8,128)S(1)} %bitcast.23), custom_call_target="tpu_custom_call" | custom-call | tf_op jit(solution)/shard_map/pallas_call | solution.py:277
  (5 shorter events, 0.1 us)
Async XLA Ops:
  0.0 0.7 copy-start
  1.9 22.3 %all-to-all-start = ((s32[32,1,128]{2,1,0:T(1,128)}), s32[32,1,128]{2,1,0:T(1,128)S(1)}, u32[]{:S(2)}, u32[]{:S(2)}) async-start(s32[32,1,128]{2,1,0:T(1,128)} %bitcast.2), calls=%async_computation | async-start | bytes 32768 | tf_op jit(solution)/shard_map/all_to_all | solution.py:31
  15.5 24.0 %collective-permute-start.1 = (bf16[32,32,128]{2,1,0:T(8,128)(2,1)}, bf16[32,32,128]{2,1,0:T(8,128)(2,1)S(1)}, u32[]{:S(2)}, u32[]{:S(2)}) collective-permute-start(bf16[32,32,128]{2,1,0:T(8,128)(2,1)} %param.4), channel_id=1, source_target_pairs={{0,4},{1,5},{2,6},{3,7},{4,0},{5,1},{6,2},{7,3},{8,12},{9,13},{10,... | collective-permute-start | bytes 786440 | tf_op jit(solution)/shard_map/ppermute | solution.py:288
  17.7 21.8 %collective-permute-start = (bf16[32,32,128]{2,1,0:T(8,128)(2,1)}, bf16[32,32,128]{2,1,0:T(8,128)(2,1)S(1)}, u32[]{:S(2)}, u32[]{:S(2)}) collective-permute-start(bf16[32,32,128]{2,1,0:T(8,128)(2,1)} %param.4), channel_id=1, source_target_pairs={{0,2},{1,3},{2,4},{3,5},{4,6},{5,7},{6,0},{7,1},{8,10},{9,11},{10,... | collective-permute-start | bytes 786440 | tf_op jit(solution)/shard_map/ppermute | solution.py:288
  20.2 19.4 %collective-permute-start.2 = (bf16[32,32,128]{2,1,0:T(8,128)(2,1)}, bf16[32,32,128]{2,1,0:T(8,128)(2,1)S(1)}, u32[]{:S(2)}, u32[]{:S(2)}) collective-permute-start(bf16[32,32,128]{2,1,0:T(8,128)(2,1)} %param.4), channel_id=1, source_target_pairs={{0,6},{1,7},{2,0},{3,1},{4,2},{5,3},{6,4},{7,5},{8,14},{9,15},{10,... | collective-permute-start | bytes 786440 | tf_op jit(solution)/shard_map/ppermute | solution.py:288
  24.2 15.3 %copy-start.2 = (bf16[32,32,128]{2,1,0:T(8,128)(2,1)S(1)}, bf16[32,32,128]{2,1,0:T(8,128)(2,1)}, u32[]{:S(2)}) copy-start(bf16[32,32,128]{2,1,0:T(8,128)(2,1)} %param.4) | copy-start | bytes 786436
  25.0 18.5 %all-to-all-start.1 = ((s32[16,1,128]{2,1,0:T(1,128)}), s32[16,1,128]{2,1,0:T(1,128)S(1)}, u32[]{:S(2)}, u32[]{:S(2)}) async-start(s32[16,1,128]{2,1,0:T(1,128)} %bitcast.5), calls=%async_computation.1 | async-start | bytes 16384 | tf_op jit(solution)/shard_map/all_to_all | solution.py:31
  39.7 6.0 %collective-permute-start.3 = (bf16[128,32,128]{2,1,0:T(8,128)(2,1)S(1)}, bf16[128,32,128]{2,1,0:T(8,128)(2,1)S(1)}, u32[]{:S(2)}, u32[]{:S(2)}) collective-permute-start(bf16[128,32,128]{2,1,0:T(8,128)(2,1)S(1)} %constant_dynamic-update-slice_fusion.same_ref), channel_id=1, source_target_pairs={{0,1},{1,0},{2,3},{3,2},{4,5},{5,4},{6,7},{7,6},{8,9},{9,8},{10,11... | collective-permute-start | bytes 3145736 | tf_op jit(solution)/shard_map/ppermute | solution.py:303
  43.5 28.9 %copy-start.1 = (s32[32,16]{0,1:T(8,128)S(1)}, s32[32,16]{0,1:T(8,128)}, u32[]{:S(2)}) copy-start(s32[32,16]{0,1:T(8,128)} %param.7) | copy-start | bytes 6148

commit v15 on v12

--- a/solution.py
+++ b/solution.py
@@ -17,7 +17,7 @@
 UNROLL = 32
 BIG = 1 << 30
 
-FIRST_Z, FIRST_YQ = Z // 2, (Y // 2) * Q + Q // 2 + 1
+FIRST_Z, FIRST_YQ = Z // 2, (Y // 2) * Q + Q // 2
 FIRST = FIRST_Z * YQ + FIRST_YQ
 Z_GROUPS = [[r + YQ * (z ^ FIRST_Z) for z in range(Z)] for r in range(YQ)]
 YQ_GROUPS = [[YQ * z + (r ^ FIRST_YQ) for r in range(YQ)] for z in range(Z)]

time: 73.9 us -> 74.2 us (level)
  no operation moved by 1% of the time
where the time goes in v15:
time: 74.2 us; the launch traced here: 73.5 us
  starting transfers between devices  41 us (55%)
  blocking collectives  22.4 us (30%)
  Pallas kernels  8.56 us (12%)
  local copies, waits for them, and re-layouts  0.83 us (1%)
    all_to_all x2, starting transfers between devices, exchange(): lax.all_to_all(x, ('index', 'query'), split_axis=0, concat_axis=0, tiled=...  28.6 us
    all_to_all x2, blocking collectives, exchange(): lax.all_to_all(x, ('index', 'query'), split_axis=0, concat_axis=0, tiled=...  22.4 us
    ppermute x3, starting transfers between devices, shards(): lax.ppermute(queries, 'query', [(k, (k + 2 * d) % Q) for k in range(Q)])  8.68 us
    pallas_call x1, Pallas kernels, shards(): pl.pallas_call(score_kernel, out_shape=(pltpu.VMEM((Z, 128), jnp.float32)...  3.71 us
    ppermute x1, starting transfers between devices, shards(): other = lax.ppermute(same, 'query', [(k, k ^ 1) for k in range(Q)])  3.67 us
    pallas_call x5, Pallas kernels, small_call(): pl.pallas_call(kernel, cost_estimate=hint, out_shape=out_shape, in_specs=...  3.16 us
    pallas_call x1, Pallas kernels, shards(): pl.pallas_call(sort_kernel, out_shape=(pltpu.VMEM((2 * GROUP, 256), jnp.i...  1.7 us
  transfers between devices with their start and end apart: 6, of which 1 were waited for; matrix products, arithmetic and copies ran while one was open for 0% of the time, Pallas kernels for 3%

profile of v15, /device:TPU:1, one launch (start us, length us, event | category | flops | bytes accessed | tf_op | source)
XLA Modules:
  0.0 73.5 jit_solution(7348403090430004359)
XLA Ops:
  0.0 0.0 copy-start
  0.0 0.7 copy-done
  0.7 1.2 %shard_map.46 = (s32[32,128]{1,0:T(8,128)}, s32[16,128]{1,0:T(8,128)S(1)}) custom-call(s32[16,32]{1,0:T(8,128)S(1)} %bitcast.22), custom_call_target="tpu_custom_call" | custom-call | tf_op jit(solution)/shard_map/pallas_call | solution.py:292
  1.9 13.9 %all-to-all-start = ((s32[32,1,128]{2,1,0:T(1,128)}), s32[32,1,128]{2,1,0:T(1,128)S(1)}, u32[]{:S(2)}, u32[]{:S(2)}) async-start(s32[32,1,128]{2,1,0:T(1,128)} %bitcast.2), calls=%async_computation | async-start | bytes 32768 | tf_op jit(solution)/shard_map/all_to_all | solution.py:31
  15.8 2.2 %collective-permute-start.1 = (bf16[32,32,128]{2,1,0:T(8,128)(2,1)}, bf16[32,32,128]{2,1,0:T(8,128)(2,1)S(1)}, u32[]{:S(2)}, u32[]{:S(2)}) collective-permute-start(bf16[32,32,128]{2,1,0:T(8,128)(2,1)} %param.4), channel_id=1, source_target_pairs={{0,4},{1,5},{2,6},{3,7},{4,0},{5,1},{6,2},{7,3},{8,12},{9,13},{10,... | collective-permute-start | bytes 786440 | tf_op jit(solution)/shard_map/ppermute | solution.py:303
  18.0 2.5 %collective-permute-start = (bf16[32,32,128]{2,1,0:T(8,128)(2,1)}, bf16[32,32,128]{2,1,0:T(8,128)(2,1)S(1)}, u32[]{:S(2)}, u32[]{:S(2)}) collective-permute-start(bf16[32,32,128]{2,1,0:T(8,128)(2,1)} %param.4), channel_id=1, source_target_pairs={{0,2},{1,3},{2,4},{3,5},{4,6},{5,7},{6,0},{7,1},{8,10},{9,11},{10,... | collective-permute-start | bytes 786440 | tf_op jit(solution)/shard_map/ppermute | solution.py:303
  20.5 4.0 %collective-permute-start.2 = (bf16[32,32,128]{2,1,0:T(8,128)(2,1)}, bf16[32,32,128]{2,1,0:T(8,128)(2,1)S(1)}, u32[]{:S(2)}, u32[]{:S(2)}) collective-permute-start(bf16[32,32,128]{2,1,0:T(8,128)(2,1)} %param.4), channel_id=1, source_target_pairs={{0,6},{1,7},{2,0},{3,1},{4,2},{5,3},{6,4},{7,5},{8,14},{9,15},{10,... | collective-permute-start | bytes 786440 | tf_op jit(solution)/shard_map/ppermute | solution.py:303
  24.5 0.0 all-to-all-done
  24.5 0.0 copy-start.2
  24.5 0.7 %shard_map.47 = s32[16,128]{1,0:T(8,128)} custom-call(s32[32,128]{1,0:T(8,128)S(1)} %bitcast.25), custom_call_target="tpu_custom_call" | custom-call | flops 99999997952 | bytes 1048576 | tf_op jit(solution)/shard_map/pallas_call | solution.py:292
  25.3 14.7 %all-to-all-start.1 = ((s32[16,1,128]{2,1,0:T(1,128)}), s32[16,1,128]{2,1,0:T(1,128)S(1)}, u32[]{:S(2)}, u32[]{:S(2)}) async-start(s32[16,1,128]{2,1,0:T(1,128)} %bitcast.5), calls=%async_computation.1 | async-start | bytes 16384 | tf_op jit(solution)/shard_map/all_to_all | solution.py:31
  40.0 0.0 collective-permute-done.1
  40.0 0.0 collective-permute-done
  40.0 0.0 collective-permute-done.2
  40.0 0.0 copy-done.2
  40.2 3.7 %collective-permute-start.3 = (bf16[128,32,128]{2,1,0:T(8,128)(2,1)S(1)}, bf16[128,32,128]{2,1,0:T(8,128)(2,1)S(1)}, u32[]{:S(2)}, u32[]{:S(2)}) collective-permute-start(bf16[128,32,128]{2,1,0:T(8,128)(2,1)S(1)} %constant_dynamic-update-slice_fusion.same_ref), channel_id=1, source_target_pairs={{0,1},{1,0},{2,3},{3,2},{4,5},{5,4},{6,7},{7,6},{8,9},{9,8},{10,11... | collective-permute-start | bytes 3145736 | tf_op jit(solution)/shard_map/ppermute | solution.py:318
  43.9 0.0 all-to-all-done.1
  43.9 1.7 %shard_map.48 = (s32[16,256]{1,0:T(8,128)S(1)}, s32[8,128]{1,0:T(8,128)S(1)}, bf16[192,1024]{1,0:T(8,128)(2,1)S(1)}, bf16[64,128,128]{2,1,0:T(8,128)(2,1)S(1)}, bf16[256,32,128]{2,1,0:T(8,128)(2,1)S(1)}) custom-call(s32[16,128]{1,0:T(8,128)S(1)} %bitcast.26, bf16[64,128,128]{2,1,0:T(8,128)(2,1)} %p_hbm.1, ...), custom_call_target="tpu_custom_call" | custom-call | flops 99999997952 | bytes 4194304 | tf_op jit(solution)/shard_map/pallas_call | solution.py:322
  45.6 0.5 collective-permute-done.3.other_ref
  46.2 0.0 copy-start.1
  46.2 3.7 %shard_map.49 = (f32[16,128]{1,0:T(8,128)S(1)}, bf16[256,32,128]{2,1,0:T(8,128)(2,1)S(1)}) custom-call(s32[16,256]{1,0:T(8,128)S(1)} %get-tuple-element.23.plan, s32[8,128]{1,0:T(8,128)S(1)} %get-tuple-element.24.dest_ref, bf16[192,1024]{1,0:T(8,128)(2,1)S(1)} %get-tuple-element.25.onehot_ref, ...), custom_call_target="tpu_custom_call", output_to_operand_aliasing={{1}: (5, {})} | custom-call | tf_op jit(solution)/shard_map/pallas_call | solution.py:342
  49.9 0.1 shard_map.50
  50.0 9.2 %all_to_all.44 = f32[32,1,128]{2,1,0:T(1,128)S(1)} all-to-all(f32[32,1,128]{2,1,0:T(1,128)S(1)} %bitcast.19), channel_id=1, replica_groups={{20,21,22,23,16,17,18,19,28,29,30,31,24,25,26,27,4,5,6,7,0,1,2,3,12,13,..., dimensions={0} | all-to-all | bytes 32768 | tf_op jit(solution)/shard_map/all_to_all | solution.py:31
  59.1 0.1 shard_map.51
  59.2 13.2 %all_to_all.45 = f32[16,1,128]{2,1,0:T(1,128)S(1)} all-to-all(f32[16,1,128]{2,1,0:T(1,128)S(1)} %bitcast.21), channel_id=1, replica_groups={{256,288,320,352,384,416,448,480,0,32,64,96,128,160,192,224},{257,289,3..., dimensions={0} | all-to-all | bytes 16384 | tf_op jit(solution)/shard_map/all_to_all | solution.py:31
  72.5 0.0 copy-done.1
  72.5 1.0 %shard_map.52 = f32[16,32]{1,0:T(8,128)} custom-call(s32[16,32]{1,0:T(8,128)S(1)} %bitcast.23, s32[16,128]{1,0:T(8,128)S(1)} %get-tuple-element.17.key_ref, f32[16,128]{1,0:T(8,128)S(1)} %bitcast.24), custom_call_target="tpu_custom_call" | custom-call | tf_op jit(solution)/shard_map/pallas_call | solution.py:292
  (4 shorter events, 0.1 us)
Async XLA Ops:
  0.0 0.7 copy-start
  1.9 22.6 %all-to-all-start = ((s32[32,1,128]{2,1,0:T(1,128)}), s32[32,1,128]{2,1,0:T(1,128)S(1)}, u32[]{:S(2)}, u32[]{:S(2)}) async-start(s32[32,1,128]{2,1,0:T(1,128)} %bitcast.2), calls=%async_computation | async-start | bytes 32768 | tf_op jit(solution)/shard_map/all_to_all | solution.py:31
  15.8 24.2 %collective-permute-start.1 = (bf16[32,32,128]{2,1,0:T(8,128)(2,1)}, bf16[32,32,128]{2,1,0:T(8,128)(2,1)S(1)}, u32[]{:S(2)}, u32[]{:S(2)}) collective-permute-start(bf16[32,32,128]{2,1,0:T(8,128)(2,1)} %param.4), channel_id=1, source_target_pairs={{0,4},{1,5},{2,6},{3,7},{4,0},{5,1},{6,2},{7,3},{8,12},{9,13},{10,... | collective-permute-start | bytes 786440 | tf_op jit(solution)/shard_map/ppermute | solution.py:303
  18.0 22.0 %collective-permute-start = (bf16[32,32,128]{2,1,0:T(8,128)(2,1)}, bf16[32,32,128]{2,1,0:T(8,128)(2,1)S(1)}, u32[]{:S(2)}, u32[]{:S(2)}) collective-permute-start(bf16[32,32,128]{2,1,0:T(8,128)(2,1)} %param.4), channel_id=1, source_target_pairs={{0,2},{1,3},{2,4},{3,5},{4,6},{5,7},{6,0},{7,1},{8,10},{9,11},{10,... | collective-permute-start | bytes 786440 | tf_op jit(solution)/shard_map/ppermute | solution.py:303
  20.5 19.5 %collective-permute-start.2 = (bf16[32,32,128]{2,1,0:T(8,128)(2,1)}, bf16[32,32,128]{2,1,0:T(8,128)(2,1)S(1)}, u32[]{:S(2)}, u32[]{:S(2)}) collective-permute-start(bf16[32,32,128]{2,1,0:T(8,128)(2,1)} %param.4), channel_id=1, source_target_pairs={{0,6},{1,7},{2,0},{3,1},{4,2},{5,3},{6,4},{7,5},{8,14},{9,15},{10,... | collective-permute-start | bytes 786440 | tf_op jit(solution)/shard_map/ppermute | solution.py:303
  24.5 15.5 %copy-start.2 = (bf16[32,32,128]{2,1,0:T(8,128)(2,1)S(1)}, bf16[32,32,128]{2,1,0:T(8,128)(2,1)}, u32[]{:S(2)}) copy-start(bf16[32,32,128]{2,1,0:T(8,128)(2,1)} %param.4) | copy-start | bytes 786436
  25.3 18.6 %all-to-all-start.1 = ((s32[16,1,128]{2,1,0:T(1,128)}), s32[16,1,128]{2,1,0:T(1,128)S(1)}, u32[]{:S(2)}, u32[]{:S(2)}) async-start(s32[16,1,128]{2,1,0:T(1,128)} %bitcast.5), calls=%async_computation.1 | async-start | bytes 16384 | tf_op jit(solution)/shard_map/all_to_all | solution.py:31
  40.2 5.9 %collective-permute-start.3 = (bf16[128,32,128]{2,1,0:T(8,128)(2,1)S(1)}, bf16[128,32,128]{2,1,0:T(8,128)(2,1)S(1)}, u32[]{:S(2)}, u32[]{:S(2)}) collective-permute-start(bf16[128,32,128]{2,1,0:T(8,128)(2,1)S(1)} %constant_dynamic-update-slice_fusion.same_ref), channel_id=1, source_target_pairs={{0,1},{1,0},{2,3},{3,2},{4,5},{5,4},{6,7},{7,6},{8,9},{9,8},{10,11... | collective-permute-start | bytes 3145736 | tf_op jit(solution)/shard_map/ppermute | solution.py:318
  46.2 26.3 %copy-start.1 = (s32[32,16]{0,1:T(8,128)S(1)}, s32[32,16]{0,1:T(8,128)}, u32[]{:S(2)}) copy-start(s32[32,16]{0,1:T(8,128)} %param.7) | copy-start | bytes 6148
